TPU v7x, 128 devices: a whole 4x4x4 slice. The times are simulated.
128 devices in a mesh: dp: 16 (over y_lo, z, core), tensor: 8 (over x, y_hi).
Axes of the slice: x: 4, y: 4 (y_hi: 2, y_lo: 2; y = y_hi * 2 + y_lo), z: 4, core: 2. Of those that a mesh axis runs over, the one named last changes fastest.
Arguments:
- hidden_in: float32 [20480, 1024], P(('dp', 'tensor')), may hold values from -6 to 6
- w_qkv: bfloat16 [1024, 2, 3, 1024], P('dp', None, None, 'tensor'), may hold values from -0.1875 to 0.1875
- w_attn_out: bfloat16 [1024, 2, 1024], P('dp', None, 'tensor'), may hold values from -0.75 to 0.75
- w_up: bfloat16 [1024, 2, 4096], P('dp', None, 'tensor'), may hold values from -0.1875 to 0.1875
- w_down: bfloat16 [1024, 2, 4096], P('dp', None, 'tensor'), may hold values from -0.09375 to 0.09375
- qv_bias: bfloat16 [64, 2, 2, 16], P('dp', None, None, 'tensor'), may hold values from -3 to 3
- up_bias: bfloat16 [64, 2, 64], P('dp', None, 'tensor'), may hold values from -3 to 3
- ln_gain: bfloat16 [1024, 2, 2], P('dp'), may hold values from 0.5 to 1.5
- row_bias: bfloat16 [1024, 2, 4], P('dp'), may hold values from -3 to 3
- cotangent: float32 [20480, 1024], P(('dp', 'tensor')), may hold values from -1.5 to 1.5
Outputs:
- hidden_out: float32 [20480, 1024], P(('dp', 'tensor'))
- grad_in: float32 [20480, 1024], P(('dp', 'tensor'))
- grad_w_qkv: float32 [1024, 2, 3, 1024], P('dp', None, None, 'tensor')
- grad_w_attn_out: float32 [1024, 2, 1024], P('dp', None, 'tensor')
- grad_w_up: float32 [1024, 2, 4096], P('dp', None, 'tensor')
- grad_w_down: float32 [1024, 2, 4096], P('dp', None, 'tensor')
- grad_qv_bias: float32 [64, 2, 2, 16], P('dp', None, None, 'tensor')
- grad_up_bias: float32 [64, 2, 64], P('dp', None, 'tensor')
- grad_ln_gain: float32 [1024, 2, 2], P('dp')
- grad_row_bias: float32 [1024, 2, 4], P('dp')
All inputs are finite; a program needn't handle non-finite values.
Results may differ from a plain program's by a relative error of at most 0.03.
Values may be sent and summed in bfloat16 or wider, within the bound.
No kernel may reach another device: no remote copies, remote signals or barrier semaphores. Data moves between devices by JAX's collectives and lax.ppermute only.
A program may use at most 192 MiB of HBM per device.

v0:
```python
from functools import partial

import jax
import jax.numpy as jnp
from jax import lax
from jax.sharding import Mesh
from jax.sharding import PartitionSpec as P

HEADS = 16
HEAD_DIM = 64
LEN = 160
DP = ("dp_0", "dp_1", "dp_2")
DP_TENSOR = ("dp_0", "dp_1", "dp_2", "tensor")


epsilon = 1e-05


def joined_along(tiles, dim):
    tiles = jnp.moveaxis(tiles, 0, dim)
    shape = tiles.shape
    return tiles.reshape(*shape[:dim], shape[dim] * shape[dim + 1], *shape[dim + 2 :])


def sent_to_all(shard, axis):
    length = lax.axis_size(axis)
    return lax.all_to_all(
        jnp.broadcast_to(shard[None], (length, *shard.shape)), axis, 0, 0, tiled=True
    )


def gather_directly(shard, axis, dim):
    return joined_along(sent_to_all(shard, axis), dim)


def in_one_piece(arrays, axis, dim, along):
    columns = [a.reshape(*a.shape[:along], -1) for a in arrays]
    both = jnp.concatenate(columns, axis=along)
    result, at, outs = (lax.all_gather(both, axis, axis=dim, tiled=True), 0, [])
    for a, column in zip(arrays, columns):
        slab = result[..., at : at + column.shape[along]]
        outs.append(slab.reshape(*slab.shape[:along], *a.shape[along:]))
        at += column.shape[along]
    return tuple(outs)


def side_by_side(arrays, axis, dim, along):
    both = jnp.concatenate(arrays, axis=along)
    result, at, outs = (lax.all_gather(both, axis, axis=dim, tiled=True), 0, [])
    for a in arrays:
        outs.append(lax.slice_in_dim(result, at, at + a.shape[along], axis=along))
        at += a.shape[along]
    return tuple(outs)


def split_up(shard, dim, length):
    before, after = (shard.shape[:dim], shard.shape[dim + 1 :])
    return jnp.moveaxis(shard.reshape(*before, length, -1, *after), dim, 0)


def sent_and_summed(shard, axis, dim):
    tiles = split_up(shard, dim, lax.axis_size(axis))
    arrived = lax.all_to_all(tiles, axis, split_axis=0, concat_axis=0, tiled=True)
    return arrived.astype(jnp.float32).sum(axis=0)


def summed_rows(shard, axes, dim):
    far, near = axes
    own = sent_and_summed(split_up(shard, dim, lax.axis_size(far)), near, dim + 1)
    return jnp.sum(
        lax.all_to_all(own.astype(jnp.bfloat16), far, 0, 0, tiled=True).astype(jnp.float32), axis=0
    )


def in_one_piece_2(arrays, axis, dim, along):
    columns = [a.reshape(*a.shape[:along], -1) for a in arrays]
    both = jnp.concatenate(columns, axis=along)
    result, at, outs = (summed_rows(both, axis, dim), 0, [])
    for a, column in zip(arrays, columns):
        slab = result[..., at : at + column.shape[along]]
        outs.append(slab.reshape(*slab.shape[:along], *a.shape[along:]))
        at += column.shape[along]
    return tuple(outs)


def in_one_piece_3(arrays, axis, dim, along):
    both = jnp.concatenate(arrays, axis=along)
    result, at, outs = (summed_rows(both, axis, dim), 0, [])
    for a in arrays:
        outs.append(lax.slice_in_dim(result, at, at + a.shape[along], axis=along))
        at += a.shape[along]
    return tuple(outs)


def taken_together(shard, axis):
    return sent_to_all(shard, axis).sum(axis=0)


def together(arrays, axis):
    ends = [0]
    for a in arrays:
        ends.append(ends[-1] + a.size)
    so_far = taken_together(jnp.concatenate([a.ravel() for a in arrays]), axis)
    return tuple((so_far[b:e].reshape(a.shape) for a, b, e in zip(arrays, ends, ends[1:])))


def norm_parts(hidden, gain, shift):
    center = jnp.mean(hidden, axis=-1, keepdims=True)
    centered = hidden - center
    variance = jnp.mean(centered * centered, axis=-1, keepdims=True)
    inverse = lax.rsqrt(variance + epsilon)
    normed = centered * inverse
    return (normed, inverse, normed * gain + shift)


def norm_back(upstream, normed, inverse, gain, own_sum):
    scaled = upstream * gain
    center = jnp.mean(scaled, axis=-1, keepdims=True)
    spread = jnp.mean(scaled * normed, axis=-1, keepdims=True)
    result = inverse * (scaled - center - normed * spread)
    return (result, own_sum(upstream * normed), own_sum(upstream))


def alibi_scores(query, keys, slopes):
    length = query.shape[1]
    scores = jnp.einsum(
        "sqhd,skhd->shqk", query, keys, preferred_element_type=jnp.float32
    ) * query.shape[3] ** (-0.5)
    row_index = lax.broadcasted_iota(jnp.int32, (length, length), 0)
    col_index = lax.broadcasted_iota(jnp.int32, (length, length), 1)
    offset = (col_index - row_index).astype(jnp.float32)
    scores = scores + slopes[None, :, None, None] * offset[None, None]
    return jnp.where((col_index <= row_index)[None, None], scores, -jnp.inf)


def attend_forward(query, keys, values, slopes):
    scores = alibi_scores(query, keys, slopes)
    highest = jnp.max(scores, axis=-1, keepdims=True)
    log_total = highest + jnp.log(jnp.sum(jnp.exp(scores - highest), axis=-1, keepdims=True))
    chance = jnp.exp(scores - log_total).astype(jnp.bfloat16)
    context = jnp.einsum("shqk,skhd->sqhd", chance, values, preferred_element_type=jnp.float32)
    return (context.astype(jnp.bfloat16), log_total)


def attend_back(query, keys, values, log_total, d_context, slopes):
    chance = jnp.exp(alibi_scores(query, keys, slopes) - log_total)
    d_value = jnp.einsum(
        "shqk,sqhd->skhd",
        chance.astype(jnp.bfloat16),
        d_context,
        preferred_element_type=jnp.float32,
    )
    d_chance = jnp.einsum("sqhd,skhd->shqk", d_context, values, preferred_element_type=jnp.float32)
    inner_sum = jnp.sum(chance * d_chance, axis=-1, keepdims=True)
    d_scores = (chance * (d_chance - inner_sum) * query.shape[3] ** (-0.5)).astype(jnp.bfloat16)
    d_query = jnp.einsum("shqk,skhd->sqhd", d_scores, keys, preferred_element_type=jnp.float32)
    d_key = jnp.einsum("shqk,sqhd->skhd", d_scores, query, preferred_element_type=jnp.float32)
    return (d_query, d_key, d_value)


def unpack(whole):
    w_mix, w_back, w_raise, w_lower, qv_rows, raise_rows, gains, shifts = whole
    qv_wide = jnp.transpose(qv_rows.astype(jnp.float32), (1, 2, 0)).reshape(2, -1)
    qkv_shift = jnp.stack([qv_wide[0], jnp.zeros_like(qv_wide[0]), qv_wide[1]])
    raise_shift = jnp.transpose(raise_rows.astype(jnp.float32)).reshape(-1)
    return (
        w_mix,
        w_back,
        w_raise,
        w_lower,
        qkv_shift,
        raise_shift,
        gains.astype(jnp.float32),
        shifts.astype(jnp.float32),
    )


def shards(
    hidden_in, w_qkv, w_attn_out, w_up, w_down, qv_bias, up_bias, ln_gain, row_bias, cotangent
):
    own_count = hidden_in.shape[0]
    group_count = own_count * lax.axis_size("tensor")
    layer_count = w_qkv.shape[1]
    local_heads = qv_bias.shape[3]
    head_ids = lax.axis_index("tensor") * local_heads + jnp.arange(local_heads)
    slopes = jnp.exp2(-8.0 * (head_ids.astype(jnp.float32) + 1.0) / HEADS)
    hidden, upstream = (hidden_in, cotangent)

    def own_sum(values):
        return jnp.sum(values, axis=0)

    def spread_rows(values):
        return gather_directly(values, "tensor", 0)

    def spread_grads(values):
        return lax.all_gather(values, "tensor", axis=0, tiled=True)

    def sum_rows(term_fn):
        return lax.psum_scatter(
            term_fn(jnp.int32(0), own_count * lax.axis_size("tensor")).astype(jnp.bfloat16),
            "tensor",
            scatter_dimension=0,
            tiled=True,
        ).astype(jnp.float32)

    def sum_grads(term_fn):
        return lax.psum_scatter(
            term_fn(jnp.int32(0), own_count * lax.axis_size("tensor")).astype(jnp.bfloat16),
            "tensor",
            scatter_dimension=0,
            tiled=True,
        ).astype(jnp.float32)

    kept = []
    stored = []
    for layer_index in range(layer_count):
        whole = (
            *in_one_piece(
                (
                    w_qkv[:, layer_index],
                    w_attn_out[:, layer_index],
                    w_up[:, layer_index],
                    w_down[:, layer_index],
                ),
                DP,
                0,
                1,
            ),
            *in_one_piece((qv_bias[:, layer_index], up_bias[:, layer_index]), DP, 0, 1),
            *side_by_side((ln_gain[:, layer_index], row_bias[:, layer_index]), DP, 0, 1),
        )
        kept.append(whole)
        w_mix, w_back, w_raise, w_lower, qkv_shift, raise_shift, gains, shifts = unpack(whole)
        normed_one, inverse_one, first = norm_parts(hidden, gains[:, 0], shifts[:, 0])
        first_all = spread_rows(first.astype(jnp.bfloat16))
        packed = (
            jnp.einsum("nd,dtc->ntc", first_all, w_mix, preferred_element_type=jnp.float32)
            + qkv_shift
        ).astype(jnp.bfloat16)
        heads = packed.reshape(group_count // LEN, LEN, 3, local_heads, HEAD_DIM)
        context, log_total = attend_forward(heads[:, :, 0], heads[:, :, 1], heads[:, :, 2], slopes)
        context_flat = context.reshape(group_count, -1)

        def attn_term(start, count, context_flat=context_flat, w_back=w_back):
            return jnp.einsum("nc,dc->nd", context_flat, w_back, preferred_element_type=jnp.float32)

        mixed = hidden + sum_rows(attn_term) + shifts[:, 2]
        normed_two, inverse_two, second = norm_parts(mixed, gains[:, 1], shifts[:, 1])
        second_all = spread_rows(second.astype(jnp.bfloat16))
        raised = (
            jnp.einsum("nd,df->nf", second_all, w_raise, preferred_element_type=jnp.float32)
            + raise_shift
        )
        activated = jax.nn.gelu(raised, approximate=True).astype(jnp.bfloat16)

        def feed_term(start, count, activated=activated, w_lower=w_lower):
            return jnp.einsum("nf,df->nd", activated, w_lower, preferred_element_type=jnp.float32)

        hidden = mixed + sum_rows(feed_term) + shifts[:, 3]
        stored.append(
            (
                normed_one,
                inverse_one,
                first_all,
                heads,
                log_total,
                context,
                context_flat,
                normed_two,
                inverse_two,
                second_all,
                raised,
                activated,
            )
        )
    results = [None] * layer_count
    for layer_index in reversed(range(layer_count)):
        whole = kept[layer_index]
        w_mix, w_back, w_raise, w_lower, qkv_shift, raise_shift, gains, shifts = unpack(whole)
        (
            normed_one,
            inverse_one,
            first_all,
            heads,
            log_total,
            context,
            context_flat,
            normed_two,
            inverse_two,
            second_all,
            raised,
            activated,
        ) = stored[layer_index]
        d_out_all = spread_grads(upstream.astype(jnp.bfloat16))
        g_lower_shift = own_sum(upstream)
        d_active = jnp.einsum("nd,df->nf", d_out_all, w_lower, preferred_element_type=jnp.float32)
        unused, pull = jax.vjp(partial(jax.nn.gelu, approximate=True), raised)
        d_raised = pull(d_active)[0]
        d_raised_half = d_raised.astype(jnp.bfloat16)
        g_lower = jnp.einsum("nd,nf->df", d_out_all, activated, preferred_element_type=jnp.float32)
        g_raise = jnp.einsum(
            "nd,nf->df", second_all, d_raised_half, preferred_element_type=jnp.float32
        )
        g_raise_shift = jnp.sum(d_raised, axis=0)

        def feed_back(start, count, d_raised_half=d_raised_half, w_raise=w_raise):
            return jnp.einsum(
                "nf,df->nd", d_raised_half, w_raise, preferred_element_type=jnp.float32
            )

        d_second = sum_grads(feed_back)
        d_norm_two, g_gain_two, g_shift_two = norm_back(
            d_second, normed_two, inverse_two, gains[:, 1], own_sum
        )
        d_mixed = upstream + d_norm_two
        d_mixed_all = spread_grads(d_mixed.astype(jnp.bfloat16))
        g_back_shift = own_sum(d_mixed)
        d_context = jnp.einsum(
            "nd,dc->nc", d_mixed_all, w_back, preferred_element_type=jnp.float32
        ).astype(jnp.bfloat16)
        g_back = jnp.einsum(
            "nd,nc->dc", d_mixed_all, context_flat, preferred_element_type=jnp.float32
        )
        d_query, d_key, d_value = attend_back(
            heads[:, :, 0],
            heads[:, :, 1],
            heads[:, :, 2],
            log_total,
            d_context.reshape(context.shape),
            slopes,
        )
        d_query = d_query.reshape(group_count, -1)
        d_key = d_key.reshape(group_count, -1)
        d_value = d_value.reshape(group_count, -1)
        d_packed = jnp.stack([d_query, d_key, d_value], axis=1).astype(jnp.bfloat16)
        g_mix = jnp.einsum("nd,ntc->dtc", first_all, d_packed, preferred_element_type=jnp.float32)
        g_qv = jnp.stack([jnp.sum(d_query, axis=0), jnp.sum(d_value, axis=0)])

        def attn_back(start, count, d_packed=d_packed, w_mix=w_mix):
            return jnp.einsum("ntc,dtc->nd", d_packed, w_mix, preferred_element_type=jnp.float32)

        d_first = sum_grads(attn_back)
        d_norm_one, g_gain_one, g_shift_one = norm_back(
            d_first, normed_one, inverse_one, gains[:, 0], own_sum
        )
        upstream = d_mixed + d_norm_one
        g_qv_rows = jnp.transpose(g_qv.reshape(2, local_heads, HEAD_DIM), (2, 0, 1))
        g_raise_rows = jnp.transpose(g_raise_shift.reshape(-1, HEAD_DIM))
        g_gains = jnp.stack([g_gain_one, g_gain_two], axis=1)
        g_shifts = jnp.stack([g_shift_one, g_shift_two, g_back_shift, g_lower_shift], axis=1)
        summed = (
            *in_one_piece_2(
                (
                    g_mix.astype(jnp.bfloat16),
                    g_back.astype(jnp.bfloat16),
                    g_raise.astype(jnp.bfloat16),
                    g_lower.astype(jnp.bfloat16),
                ),
                (("dp_0", "dp_1"), "dp_2"),
                0,
                1,
            ),
            *in_one_piece_2(
                (g_qv_rows.astype(jnp.bfloat16), g_raise_rows.astype(jnp.bfloat16)),
                (("dp_0", "dp_1"), "dp_2"),
                0,
                1,
            ),
            *in_one_piece_3(
                (g_gains.astype(jnp.bfloat16), g_shifts.astype(jnp.bfloat16)),
                (("dp_0", "dp_1"), "dp_2"),
                0,
                1,
            ),
        )
        vector_gain, vector_shift = together((summed[6], summed[7]), "tensor")
        results[layer_index] = (
            summed[0],
            summed[1],
            summed[2],
            summed[3],
            summed[4],
            summed[5],
            vector_gain,
            vector_shift,
        )
    stacked = tuple(
        (
            jnp.stack([results[position][member] for position in range(layer_count)], axis=1)
            for member in range(8)
        )
    )
    return (
        hidden,
        upstream,
        stacked[0],
        stacked[1],
        stacked[2],
        stacked[3],
        stacked[4],
        stacked[5],
        stacked[6],
        stacked[7],
    )


def solution(mesh):
    torus = Mesh(
        mesh.devices.reshape(2, 4, 2, mesh.shape["tensor"]), ("dp_0", "dp_1", "dp_2", "tensor")
    )
    placed = (
        P(DP_TENSOR, None),
        P(DP, None, None, "tensor"),
        P(DP, None, "tensor"),
        P(DP, None, "tensor"),
        P(DP, None, "tensor"),
        P(DP, None, None, "tensor"),
        P(DP, None, "tensor"),
        P(DP, None, None),
        P(DP, None, None),
        P(DP_TENSOR, None),
    )
    return jax.shard_map(
        shards,
        mesh=torus,
        in_specs=placed,
        out_specs=(
            P(DP_TENSOR, None),
            P(DP_TENSOR, None),
            P(DP, None, None, "tensor"),
            P(DP, None, "tensor"),
            P(DP, None, "tensor"),
            P(DP, None, "tensor"),
            P(DP, None, None, "tensor"),
            P(DP, None, "tensor"),
            P(DP, None, None),
            P(DP, None, None),
        ),
        check_vma=False,
    )
```

profile of v0, /device:TPU:0, one launch (start us, length us, event | category | flops | bytes accessed | tf_op | source)
XLA Modules:
  0.0 1343.1 jit_solution(9168298569211430551)
XLA Ops:
  15.3 21.1 %all-gather = bf16[16,64,6]{1,2,0:T(8,128)(2,1)S(1)} all-gather(bf16[1,64,6]{1,2,0:T(8,128)(2,1)S(1)} %maximum_bitcast_fusion.3), channel_id=1, replica_groups=mesh['dp_0'=2,'dp_1'=4,'dp_2'=2,'tensor'=8] {'dp_0','dp_1','dp_2'}, dimensions={0}, use_global_device_ids=true | all-gather | bytes 13056 | tf_op jit(solution)/shard_map/all_gather | solution.py:49
  40.2 6.7 all-to-all-start
  47.2 38.4 %all-gather.3 = bf16[16,4,12]{2,1,0:T(4,128)(2,1)S(1)} all-gather(bf16[1,4,12]{2,1,0:T(4,128)(2,1)S(1)} %maximum_bitcast_fusion.6), channel_id=1, replica_groups=mesh['dp_0'=2,'dp_1'=4,'dp_2'=2,'tensor'=8] {'dp_0','dp_1','dp_2'}, dimensions={0}, use_global_device_ids=true | all-gather | bytes 1632 | tf_op jit(solution)/shard_map/all_gather | solution.py:39
  86.0 18.7 %all-gather.1 = bf16[16,4,12]{2,1,0:T(4,128)(2,1)S(1)} all-gather(bf16[1,4,12]{2,1,0:T(4,128)(2,1)S(1)} %maximum_bitcast_fusion.5), channel_id=1, replica_groups=mesh['dp_0'=2,'dp_1'=4,'dp_2'=2,'tensor'=8] {'dp_0','dp_1','dp_2'}, dimensions={0}, use_global_device_ids=true | all-gather | bytes 1632 | tf_op jit(solution)/shard_map/all_gather | solution.py:39
  135.7 80.3 %reduce-scatter.9.cloned.1.call-done = bf16[160,1024]{1,0:T(8,128)(2,1)} async-done(((bf16[1280,1024]{1,0:T(8,128)(2,1)}), bf16[160,1024]{1,0:T(8,128)(2,1)}) %reduce-scatter.9.cloned.1.call-update) | async-done | bytes 327696 | tf_op jit(solution)/shard_map/reduce_scatter | solution.py:199
  229.4 32.5 %all-to-all-done.1 = bf16[8,160,1024]{2,1,0:T(8,128)(2,1)} async-done(((bf16[8,160,1024]{2,1,0:T(8,128)(2,1)}), bf16[8,160,1024]{2,1,0:T(8,128)(2,1)}, u32[]{:S(2)}, u32[]{:S(2)}) %all-to-all-start.1) | async-done | bytes 2621472 | tf_op jit(solution)/shard_map/all_to_all | solution.py:27
  274.9 18.8 %all-gather.2 = bf16[16,64,6]{1,2,0:T(8,128)(2,1)S(1)} all-gather(bf16[1,64,6]{1,2,0:T(8,128)(2,1)S(1)} %maximum_bitcast_fusion.4), channel_id=1, replica_groups=mesh['dp_0'=2,'dp_1'=4,'dp_2'=2,'tensor'=8] {'dp_0','dp_1','dp_2'}, dimensions={0}, use_global_device_ids=true | all-gather | bytes 13056 | tf_op jit(solution)/shard_map/all_gather | solution.py:49
  293.8 52.6 %reduce-scatter.11.cloned.1.call-done = bf16[160,1024]{1,0:T(8,128)(2,1)} async-done(((bf16[1280,1024]{1,0:T(8,128)(2,1)}), bf16[160,1024]{1,0:T(8,128)(2,1)}) %reduce-scatter.11.cloned.1.call-update) | async-done | bytes 327696 | tf_op jit(solution)/shard_map/reduce_scatter | solution.py:199
  355.1 50.9 %all-gather.13.cloned.1.call-done = bf16[1024,1536]{1,0:T(8,128)(2,1)} async-done(((bf16[64,1536]{1,0:T(8,128)(2,1)}), bf16[1024,1536]{1,0:T(8,128)(2,1)}) %all-gather.13.cloned.1.call-update) | async-done | bytes 3145744 | tf_op jit(solution)/shard_map/all_gather | solution.py:39
  439.8 77.6 %reduce-scatter.13.cloned.1.call-done = bf16[160,1024]{1,0:T(8,128)(2,1)} async-done(((bf16[1280,1024]{1,0:T(8,128)(2,1)}), bf16[160,1024]{1,0:T(8,128)(2,1)}) %reduce-scatter.13.cloned.1.call-update) | async-done | bytes 327696 | tf_op jit(solution)/shard_map/reduce_scatter | solution.py:199
  529.7 39.1 %all-to-all-done.3 = bf16[8,160,1024]{2,1,0:T(8,128)(2,1)} async-done(((bf16[8,160,1024]{2,1,0:T(8,128)(2,1)}), bf16[8,160,1024]{2,1,0:T(8,128)(2,1)}, u32[]{:S(2)}, u32[]{:S(2)}) %all-to-all-start.3) | async-done | bytes 2621472 | tf_op jit(solution)/shard_map/all_to_all | solution.py:27
  573.9 27.9 %all-gather.15.cloned.1.call-done = bf16[1280,1024]{1,0:T(8,128)(2,1)} async-done(((bf16[160,1024]{1,0:T(8,128)(2,1)}), bf16[1280,1024]{1,0:T(8,128)(2,1)}) %all-gather.15.cloned.1.call-update) | async-done | bytes 2621456 | tf_op jit(solution)/shard_map/all_gather | solution.py:196
  601.8 5.9 fusion.179
  613.3 5.2 convolution_convert_fusion.2
  618.6 71.6 %reduce-scatter.17.cloned.1.call-done = bf16[160,1024]{1,0:T(8,128)(2,1)} async-done(((bf16[1280,1024]{1,0:T(8,128)(2,1)}), bf16[160,1024]{1,0:T(8,128)(2,1)}) %reduce-scatter.17.cloned.1.call-update) | async-done | bytes 327696 | tf_op jit(solution)/shard_map/reduce_scatter | solution.py:207
  691.8 79.0 %reduce-scatter.15.cloned.1.call-done = bf16[160,1024]{1,0:T(8,128)(2,1)} async-done(((bf16[1280,1024]{1,0:T(8,128)(2,1)}), bf16[160,1024]{1,0:T(8,128)(2,1)}) %reduce-scatter.15.cloned.1.call-update) | async-done | bytes 327696 | tf_op jit(solution)/shard_map/reduce_scatter | solution.py:199
  775.2 57.5 %all-gather.17.cloned.1.call-done = bf16[1280,1024]{1,0:T(8,128)(2,1)} async-done(((bf16[160,1024]{1,0:T(8,128)(2,1)}), bf16[1280,1024]{1,0:T(8,128)(2,1)}) %all-gather.17.cloned.1.call-update) | async-done | bytes 2621456 | tf_op jit(solution)/shard_map/all_gather | solution.py:196
  845.6 6.2 fusion.66
  851.8 6.2 fusion.159
  879.1 77.0 %reduce-scatter.19.cloned.1.call-done = bf16[160,1024]{1,0:T(8,128)(2,1)} async-done(((bf16[1280,1024]{1,0:T(8,128)(2,1)}), bf16[160,1024]{1,0:T(8,128)(2,1)}) %reduce-scatter.19.cloned.1.call-update) | async-done | bytes 327696 | tf_op jit(solution)/shard_map/reduce_scatter | solution.py:207
  961.1 57.8 %all-gather.19.cloned.1.call-done = bf16[1280,1024]{1,0:T(8,128)(2,1)} async-done(((bf16[160,1024]{1,0:T(8,128)(2,1)}), bf16[1280,1024]{1,0:T(8,128)(2,1)}) %all-gather.19.cloned.1.call-update) | async-done | bytes 2621456 | tf_op jit(solution)/shard_map/all_gather | solution.py:196
  1018.8 6.0 fusion.180
  1030.6 76.6 %reduce-scatter.21.cloned.1.call-done = bf16[160,1024]{1,0:T(8,128)(2,1)} async-done(((bf16[1280,1024]{1,0:T(8,128)(2,1)}), bf16[160,1024]{1,0:T(8,128)(2,1)}) %reduce-scatter.21.cloned.1.call-update) | async-done | bytes 327696 | tf_op jit(solution)/shard_map/reduce_scatter | solution.py:207
  1112.1 5.2 fusion.36
  1150.2 10.3 all_to_all.93
  1206.9 5.9 all-to-all-start.7
  1212.8 5.2 convolution_convert_fusion.10
  1240.7 6.8 all-to-all-start.17
  1255.2 10.3 all_to_all.95
  1283.0 17.2 %all-to-all-done.5 = bf16[8,64,1536]{2,1,0:T(8,128)(2,1)} async-done(((bf16[8,64,1536]{2,1,0:T(8,128)(2,1)}), bf16[8,64,1536]{2,1,0:T(8,128)(2,1)}, u32[]{:S(2)}, u32[]{:S(2)}) %all-to-all-start.5) | async-done | bytes 1572896 | tf_op jit(solution)/shard_map/all_to_all | solution.py:71
  1316.4 6.2 all-to-all-done.13
  1329.2 5.5 all-to-all-done.14
  (455 shorter events, 341.6 us)
Async XLA Ops:
  7.2 29.3 %copy-start.1 = (f32[160,1024]{1,0:T(8,128)S(1)}, f32[160,1024]{1,0:T(8,128)}, u32[]{:S(2)}) copy-start(f32[160,1024]{1,0:T(8,128)} %param.10) | copy-start | bytes 1966084
  7.2 100.2 %all-gather.11.cloned.1.call-start = ((), (), s32[]{:S(2)}) async-start(), calls=%async_computation.26 | async-start | bytes 3342336 | tf_op jit(solution)/shard_map/all_gather | solution.py:39
  40.2 68.8 %all-to-all-start = ((bf16[8,160,1024]{2,1,0:T(8,128)(2,1)}), bf16[8,160,1024]{2,1,0:T(8,128)(2,1)}, u32[]{:S(2)}, u32[]{:S(2)}) async-start(bf16[8,160,1024]{2,1,0:T(8,128)(2,1)} %broadcast_in_dim.38), calls=%async_computation | async-start | bytes 5242880 | tf_op jit(solution)/shard_map/all_to_all | solution.py:27
  46.8 169.2 %reduce-scatter.9.cloned.1.call-start = ((), (), s32[]{:S(2)}) async-start(), calls=%async_computation.27 | async-start | bytes 2949120 | tf_op jit(solution)/shard_map/reduce_scatter | solution.py:199
  220.8 41.1 %all-to-all-start.1 = ((bf16[8,160,1024]{2,1,0:T(8,128)(2,1)}), bf16[8,160,1024]{2,1,0:T(8,128)(2,1)}, u32[]{:S(2)}, u32[]{:S(2)}) async-start(bf16[8,160,1024]{2,1,0:T(8,128)(2,1)} %broadcast_in_dim.41), calls=%async_computation.2 | async-start | bytes 5242880 | tf_op jit(solution)/shard_map/all_to_all | solution.py:27
  225.2 121.3 %reduce-scatter.11.cloned.1.call-start = ((), (), s32[]{:S(2)}) async-start(), calls=%async_computation.28 | async-start | bytes 2949120 | tf_op jit(solution)/shard_map/reduce_scatter | solution.py:199
  271.6 134.5 %all-gather.13.cloned.1.call-start = ((), (), s32[]{:S(2)}) async-start(), calls=%async_computation.29 | async-start | bytes 3342336 | tf_op jit(solution)/shard_map/all_gather | solution.py:39
  350.7 59.8 %all-to-all-start.2 = ((bf16[8,160,1024]{2,1,0:T(8,128)(2,1)}), bf16[8,160,1024]{2,1,0:T(8,128)(2,1)}, u32[]{:S(2)}, u32[]{:S(2)}) async-start(bf16[8,160,1024]{2,1,0:T(8,128)(2,1)} %broadcast_in_dim.42), calls=%async_computation.4 | async-start | bytes 5242880 | tf_op jit(solution)/shard_map/all_to_all | solution.py:27
  355.1 55.4 %copy-start.42 = (f32[3,128]{1,0:T(4,128)S(1)}, f32[3,128]{1,0:T(4,128)}, u32[]{:S(2)}) copy-start(f32[3,128]{1,0:T(4,128)} %get-tuple-element.177) | copy-start | bytes 4612
  355.1 162.3 %reduce-scatter.13.cloned.1.call-start = ((), (), s32[]{:S(2)}) async-start(), calls=%async_computation.30 | async-start | bytes 2949120 | tf_op jit(solution)/shard_map/reduce_scatter | solution.py:199
  439.7 162.1 %all-gather.15.cloned.1.call-start = ((), (), s32[]{:S(2)}) async-start(), calls=%async_computation.32 | async-start | bytes 2949120 | tf_op jit(solution)/shard_map/all_gather | solution.py:196
  524.5 44.3 %all-to-all-start.3 = ((bf16[8,160,1024]{2,1,0:T(8,128)(2,1)}), bf16[8,160,1024]{2,1,0:T(8,128)(2,1)}, u32[]{:S(2)}, u32[]{:S(2)}) async-start(bf16[8,160,1024]{2,1,0:T(8,128)(2,1)} %broadcast_in_dim.43), calls=%async_computation.6 | async-start | bytes 5242880 | tf_op jit(solution)/shard_map/all_to_all | solution.py:27
  529.0 161.1 %reduce-scatter.17.cloned.1.call-start = ((), (), s32[]{:S(2)}) async-start(), calls=%async_computation.33 | async-start | bytes 2949120 | tf_op jit(solution)/shard_map/reduce_scatter | solution.py:207
  613.2 157.6 %reduce-scatter.15.cloned.1.call-start = ((), (), s32[]{:S(2)}) async-start(), calls=%async_computation.31 | async-start | bytes 2949120 | tf_op jit(solution)/shard_map/reduce_scatter | solution.py:199
  618.5 214.2 %all-gather.17.cloned.1.call-start = ((), (), s32[]{:S(2)}) async-start(), calls=%async_computation.34 | async-start | bytes 2949120 | tf_op jit(solution)/shard_map/all_gather | solution.py:196
  775.0 181.1 %reduce-scatter.19.cloned.1.call-start = ((), (), s32[]{:S(2)}) async-start(), calls=%async_computation.35 | async-start | bytes 2949120 | tf_op jit(solution)/shard_map/reduce_scatter | solution.py:207
  879.1 139.8 %all-gather.19.cloned.1.call-start = ((), (), s32[]{:S(2)}) async-start(), calls=%async_computation.36 | async-start | bytes 2949120 | tf_op jit(solution)/shard_map/all_gather | solution.py:196
  961.0 146.1 %reduce-scatter.21.cloned.1.call-start = ((), (), s32[]{:S(2)}) async-start(), calls=%async_computation.37 | async-start | bytes 2949120 | tf_op jit(solution)/shard_map/reduce_scatter | solution.py:207
  1030.1 77.1 %copy-start.30 = (f32[1024,1]{0,1:T(1,128)S(1)}, f32[1024,1]{0,1:T(1,128)}, u32[]{:S(2)}) copy-start(f32[1024,1]{0,1:T(1,128)} %get-tuple-element.163) | copy-start | bytes 12292
  1030.1 77.1 %copy-start.34 = (f32[160]{0:T(256)S(1)}, f32[160]{0:T(256)}, u32[]{:S(2)}) copy-start(f32[160]{0:T(256)} %copy-done.33) | copy-start | bytes 1924
  1030.1 77.1 %copy-start.38 = (f32[160]{0:T(256)S(1)}, f32[160]{0:T(256)}, u32[]{:S(2)}) copy-start(f32[160]{0:T(256)} %copy-done.37) | copy-start | bytes 1924
  1030.1 145.5 %all-gather.21.cloned.1.call-start = ((), (), s32[]{:S(2)}) async-start(), calls=%async_computation.38 | async-start | bytes 2949120 | tf_op jit(solution)/shard_map/all_gather | solution.py:196
  1145.6 4.6 all-to-all-start.10
  1160.5 10.6 all-to-all-start.16
  1171.2 35.7 %all-to-all-start.11 = ((bf16[8,4,12]{2,1,0:T(4,128)(2,1)}), bf16[8,4,12]{2,1,0:T(4,128)(2,1)S(1)}, u32[]{:S(2)}, u32[]{:S(2)}) async-start(bf16[8,4,12]{2,1,0:T(4,128)(2,1)} %reduce_sum.518), calls=%async_computation.19 | async-start | bytes 16384 | tf_op jit(solution)/shard_map/all_to_all | solution.py:71
  1175.5 130.0 %reduce-scatter.23.cloned.1.call-start = ((), (), s32[]{:S(2)}) async-start(), calls=%async_computation.39 | async-start | bytes 2949120 | tf_op jit(solution)/shard_map/reduce_scatter | solution.py:207
  1206.9 29.5 %all-to-all-start.7 = ((bf16[8,64,1536]{2,1,0:T(8,128)(2,1)}), bf16[8,64,1536]{2,1,0:T(8,128)(2,1)S(1)}, u32[]{:S(2)}, u32[]{:S(2)}) async-start(bf16[8,64,1536]{2,1,0:T(8,128)(2,1)} %reduce_sum.508), calls=%async_computation.15 | async-start | bytes 3145728 | tf_op jit(solution)/shard_map/all_to_all | solution.py:71
  1240.7 14.5 %all-to-all-start.17 = ((f32[8,1,384]{2,1,0:T(1,128)}), f32[8,1,384]{2,1,0:T(1,128)S(1)}, u32[]{:S(2)}, u32[]{:S(2)}) async-start(f32[8,1,384]{2,1,0:T(1,128)} %broadcast_in_dim.45), calls=%async_computation.25 | async-start | bytes 24576 | tf_op jit(solution)/shard_map/all_to_all | solution.py:27
  1265.5 10.5 all-to-all-start.9
  1276.1 24.1 %all-to-all-start.5 = ((bf16[8,64,1536]{2,1,0:T(8,128)(2,1)}), bf16[8,64,1536]{2,1,0:T(8,128)(2,1)}, u32[]{:S(2)}, u32[]{:S(2)}) async-start(bf16[8,64,1536]{2,1,0:T(8,128)(2,1)} %reduce_sum.506), calls=%async_computation.13 | async-start | bytes 3145728 | tf_op jit(solution)/shard_map/all_to_all | solution.py:71
  1312.7 9.8 all-to-all-start.13
  1323.8 11.0 all-to-all-start.14
  (42 other events, 180.7 us)
Sparse Core Ops, SparseCore 0:
  14.3 53.8 all-gather.10
  135.9 80.1 reduce-scatter.8
  271.7 74.7 reduce-scatter.10
  348.6 57.4 all-gather.12
  439.8 77.4 reduce-scatter.12
  520.1 81.6 all-gather.14
  613.3 76.7 reduce-scatter.16
  694.0 76.7 reduce-scatter.14
  775.1 57.5 all-gather.16
  879.2 76.8 reduce-scatter.18
  961.1 57.6 all-gather.18
  1030.2 76.8 reduce-scatter.20
  1112.2 57.6 all-gather.20
  1206.5 81.7 reduce-scatter.22
where the time goes:
time: 1350 us; the launch traced here: 1340 us
  waiting for transfers between devices  822 us (61%)
  matrix products  138 us (10%)
  blocking collectives  129 us (10%)
  local copies, waits for them, and re-layouts  124 us (9%)
  starting transfers between devices  62 us (5%)
  other arithmetic  53.1 us (4%)
  between operations  15.4 us (1%)
    reduce_scatter x4, waiting for transfers between devices, sum_rows(): lax.psum_scatter(term_fn(jnp.int32(0), own_count * lax.axis_size('tensor'...  290 us
    reduce_scatter x4, waiting for transfers between devices, sum_grads(): lax.psum_scatter(term_fn(jnp.int32(0), own_count * lax.axis_size('tensor'...  225 us
    all_gather x4, waiting for transfers between devices, spread_grads(): return lax.all_gather(values, 'tensor', axis=0, tiled=True)  143 us
    all_to_all x6, waiting for transfers between devices, sent_to_all(): lax.all_to_all(jnp.broadcast_to(shard[None], (length, *shard.shape)), axi...  81.1 us
    all_gather x2, blocking collectives, in_one_piece(): result, at, outs = (lax.all_gather(both, axis, axis=dim, tiled=True), 0, [])  57.1 us
    all_gather x2, waiting for transfers between devices, in_one_piece(): result, at, outs = (lax.all_gather(both, axis, axis=dim, tiled=True), 0, [])  50.9 us
    all_gather x2, blocking collectives, side_by_side(): result, at, outs = (lax.all_gather(both, axis, axis=dim, tiled=True), 0, [])  39.9 us
    unnamed x145, local copies, waits for them, and re-layouts  33.6 us
  transfers between devices with their start and end apart: 27, of which 21 were waited for; matrix products, arithmetic and copies ran while one was open for 11% of the time, Pallas kernels for 0%

commit v1 on v0

v1 whole, which is shorter than its diff:
```python
import itertools
from functools import partial

import jax
import jax.numpy as jnp
import numpy as np
from jax import lax
from jax.experimental import pallas as pl
from jax.experimental.pallas import tpu as pltpu
from jax.sharding import Mesh
from jax.sharding import PartitionSpec as P

AXES = ("ylo", "z", "core", "x", "yhi")
SIZES = (2, 4, 2, 4, 2)
DP = ("ylo", "z", "core")
TENSOR = ("x", "yhi")
ORDERS = ("xyz", "yzx", "zxy")
LAYERS = 2
TOK = 160
D = 1024
HEADS = 16
EPS = 1e-05
BF, F32 = jnp.bfloat16, jnp.float32
HIGH = lax.Precision.HIGHEST


def pairs(axis, step):
    out = []
    for ylo, z, core, x, yhi in itertools.product(*map(range, SIZES)):
        c = {"x": x, "y": 2 * yhi + ylo, "z": z, "core": core}
        if axis == "core":
            c["core"] ^= 1
        else:
            c[axis] ^= 1 if (step == 1) == (core == 0) else 3
        src = np.ravel_multi_index((ylo, z, core, x, yhi), SIZES)
        dst = np.ravel_multi_index((c["y"] & 1, c["z"], c["core"], c["x"], c["y"] >> 1), SIZES)
        out.append((int(src), int(dst)))
    return out


def swap(v, axis, step=0):
    return lax.ppermute(v, AXES, pairs(axis, step))


def gather(parts):
    bufs = list(parts)
    res = [None] * len(parts)
    for n in range(6):
        recv = [swap(b, ORDERS[i][n // 2], n % 2 + 1) for i, b in enumerate(bufs)]
        if n < 5:
            bufs = [jnp.stack([b, r]) for b, r in zip(bufs, recv)]
        else:
            for i in range(len(parts)):
                res[i] = (bufs[i], recv[i], swap(bufs[i], "core"), swap(recv[i], "core"))
    return res


def plus(a, b):
    return (a.astype(F32) + b.astype(F32)).astype(BF)


def scatter_one(grad, order):
    own_lo, own_hi, oth_lo, oth_hi = grad
    hi = plus(own_hi, swap(oth_hi, "core"))
    lo = plus(own_lo, swap(oth_lo, "core"))
    for n in reversed(range(6)):
        r = swap(hi, order[n // 2], n % 2 + 1)
        if n == 0:
            return lo.astype(F32) + r.astype(F32)
        s = plus(lo, r)
        lo, hi = s[0], s[1]


def norm(h):
    center = jnp.mean(h, axis=-1, keepdims=True)
    c = h - center
    var = jnp.mean(c * c, axis=-1, keepdims=True)
    inv = lax.rsqrt(var + EPS)
    return c * inv, inv


def dot(a, b):
    return lax.dot_general(a, b, (((1,), (0,)), ((), ())), preferred_element_type=F32)


def dot_nt(a, b):
    return lax.dot_general(a, b, (((1,), (1,)), ((), ())), preferred_element_type=F32)


def dot_tn(a, b):
    return lax.dot_general(a, b, (((0,), (0,)), ((), ())), preferred_element_type=F32)


def turned(x):
    return jnp.transpose(x.astype(F32)).astype(BF)


BITS = tuple(itertools.product((0, 1), repeat=2))


def placed_at(core, half, y2, y1):
    if y1 == y2:
        return y1
    c = core if half == 0 else 1 - core
    return c if y1 else 1 - c


def each_block(part, step, quad):
    a, b = step // 2, step % 2
    for half in (0, 1):
        lo, hi = quad[2 * half], quad[2 * half + 1]
        for (z2, z1), (y2, y1) in itertools.product(BITS, BITS):
            row = half * 8 + (y1 ^ y2) * 4 + z2 * 2 + z1
            if part == 0:
                yield None, half, y2, y1, row, (lo, hi)[z2], (z1 * 4 + y2 * 2 + y1, 0)
            elif part == 2:
                yield None, half, y2, y1, row, (lo, hi)[y2], (y1, 0, z2 * 2 + z1)
            else:
                which = a if half == 0 else b
                for x2 in (0, 1):
                    yield which == x2, half, y2, y1, row, (lo, hi)[x2], (0, z2 * 2 + z1, y2 * 2 + y1)


def by_condition(part, step, quad, fn):
    if part != 1:
        for _, *rest in each_block(part, step, quad):
            fn(*rest)
        return
    groups = {}
    for cond, half, *rest in each_block(part, step, quad):
        groups.setdefault((half, id(rest[3])), (cond, []))[1].append((half, *rest))
    for cond, items in groups.values():

        @pl.when(cond)
        def _(items=items):
            for it in items:
                fn(*it)


def assemble(part, step, core, quad, w_ref):
    def put(half, y2, y1, row, ref, index):
        w_ref[placed_at(core, half, y2, y1), row * 64 : row * 64 + 64, :] = ref[index]

    by_condition(part, step, quad, put)


def disassemble(part, step, core, quad, w_ref):
    def get(half, y2, y1, row, ref, index):
        ref[index] = w_ref[placed_at(core, half, y2, y1), row * 64 : row * 64 + 64, :]

    by_condition(part, step, quad, get)


def merged(part, quad):
    shape = {0: (8, 4, 64, 512), 1: (2, 4, 4, 64, 512), 2: (2, 4, 4, 64, 512)}[part]
    return tuple(q.reshape(shape) for q in quad)


def unmerged(quad):
    return tuple(q.reshape(2, 2, 2, 2, 2, 64, 512) for q in quad)


def quad_shapes(part):
    shape = {0: (8, 4, 64, 512), 1: (2, 4, 4, 64, 512), 2: (2, 4, 4, 64, 512)}[part]
    return [jax.ShapeDtypeStruct(shape, BF)] * 4


def quad_specs(part):
    def own(s):
        return s

    def oth(s):
        return (s % 2) * 2 + s // 2

    if part == 0:
        return [
            pl.BlockSpec((8, 1, 64, 512), lambda s, *_, f=f: (0, f(s), 0, 0))
            for f in (own, own, oth, oth)
        ]
    if part == 2:
        return [
            pl.BlockSpec((2, 1, 4, 64, 512), lambda s, *_, f=f: (0, f(s), 0, 0, 0))
            for f in (own, own, oth, oth)
        ]
    maps = (
        lambda s: jnp.minimum(s, 1),
        lambda s: jnp.maximum(s - 2, 0),
        lambda s: s // 2,
        lambda s: s // 2,
    )
    return [
        pl.BlockSpec((1, 4, 4, 64, 512), lambda s, *_, f=f: (f(s), 0, 0, 0, 0)) for f in maps
    ]


def whole(shape):
    zeros = (0,) * len(shape)
    return pl.BlockSpec(shape, lambda s, *_: zeros)


def per_step(shape):
    zeros = (0,) * (len(shape) - 1)
    return pl.BlockSpec((1, *shape[1:]), lambda s, *_: (s, *zeros))


def call(body, name, core, slopes, ins, in_specs, outs, out_specs, scratch):
    return pl.pallas_call(
        body,
        name=name,
        out_shape=outs,
        grid_spec=pltpu.PrefetchScalarGridSpec(
            num_scalar_prefetch=2,
            grid=(4,),
            in_specs=in_specs,
            out_specs=out_specs,
            scratch_shapes=scratch,
        ),
        compiler_params=pltpu.CompilerParams(
            dimension_semantics=("arbitrary",), vmem_limit_bytes=48 << 20
        ),
    )(core, slopes, *ins)


def sds(shape, dtype=F32):
    return jax.ShapeDtypeStruct(shape, dtype)


def scores_of(q, k, slope):
    s = dot_nt(q, k) * 0.125
    row = lax.broadcasted_iota(jnp.int32, (TOK, TOK), 0)
    col = lax.broadcasted_iota(jnp.int32, (TOK, TOK), 1)
    s = s + slope * (col - row).astype(F32)
    return jnp.where(col <= row, s, -jnp.inf)


def chance_of(q, k, slope):
    s = scores_of(q, k, slope)
    e = jnp.exp(s - jnp.max(s, axis=-1, keepdims=True))
    return e / jnp.sum(e, axis=-1, keepdims=True)


def attn_fwd_body(core_ref, slope_ref, h_ref, vec_ref, bias_ref, *rest):
    quad, (qkv_ref, ctx_ref, hm_ref), (w_ref, a_ref) = rest[:4], rest[4:7], rest[7:]
    s, core = pl.program_id(0), core_ref[0]

    @pl.when(s == 0)
    def _():
        n, _ = norm(h_ref[...])
        a_ref[...] = (n * vec_ref[0:1, :] + vec_ref[1:2, :]).astype(BF)
        hm_ref[...] = h_ref[...] + vec_ref[4:5, :]

    assemble(0, s, core, quad, w_ref)
    total = jnp.zeros((TOK, D), F32)
    for g in (0, 1):
        qkv = (dot(a_ref[...], w_ref[g, :, 0:384]) + bias_ref[0, g : g + 1, :]).astype(BF)
        qkv_ref[0, g] = qkv
        ctx = []
        for hd in (0, 1):
            q, k, v = (qkv[:, j * 128 + hd * 64 : j * 128 + hd * 64 + 64] for j in range(3))
            p = chance_of(q, k, slope_ref[s * 4 + g * 2 + hd]).astype(BF)
            ctx.append(dot(p, v))
        ctx = jnp.concatenate(ctx, axis=1).astype(BF)
        ctx_ref[0, g] = ctx
        total = total + dot_nt(ctx, w_ref[g, :, 384:512])
    hm_ref[...] += total


def attn_fwd(core, slopes, h, vec, bias, quad):
    return call(
        attn_fwd_body,
        "attn_fwd",
        core,
        slopes,
        (h, vec, bias, *merged(0, quad)),
        [whole((TOK, D)), whole((8, D)), per_step((4, 2, 384))] + quad_specs(0),
        [sds((4, 2, TOK, 384), BF), sds((4, 2, TOK, 128), BF), sds((TOK, D))],
        [per_step((4, 2, TOK, 384)), per_step((4, 2, TOK, 128)), whole((TOK, D))],
        [pltpu.VMEM((2, D, 512), BF), pltpu.VMEM((TOK, D), BF)],
    )


C0, C1 = 0.7978845608, 0.044715


def gelu_parts(u):
    t = jnp.tanh(C0 * (u + C1 * (u * u * u)))
    return 0.5 * u * (1.0 + t), t


def feed_fwd_body(core_ref, slope_ref, hm_ref, vec_ref, bias_ref, *rest):
    up, down, (u_ref, out_ref), (wu_ref, wd_ref, m_ref) = rest[:4], rest[4:8], rest[8:10], rest[10:]
    s, core = pl.program_id(0), core_ref[0]

    @pl.when(s == 0)
    def _():
        n, _ = norm(hm_ref[...])
        m_ref[...] = (n * vec_ref[2:3, :] + vec_ref[3:4, :]).astype(BF)
        out_ref[...] = hm_ref[...] + vec_ref[5:6, :]

    assemble(1, s, core, up, wu_ref)
    assemble(2, s, core, down, wd_ref)
    total = jnp.zeros((TOK, D), F32)
    for g in (0, 1):
        u = dot(m_ref[...], wu_ref[g]) + bias_ref[0, g : g + 1, :]
        u_ref[0, g] = u
        act, _ = gelu_parts(u)
        total = total + dot_nt(act.astype(BF), wd_ref[g])
    out_ref[...] += total


def feed_fwd(core, slopes, hm, vec, bias, up, down):
    return call(
        feed_fwd_body,
        "feed_fwd",
        core,
        slopes,
        (hm, vec, bias, *merged(1, up), *merged(2, down)),
        [whole((TOK, D)), whole((8, D)), per_step((4, 2, 512))] + quad_specs(1) + quad_specs(2),
        [sds((4, 2, TOK, 512)), sds((TOK, D))],
        [per_step((4, 2, TOK, 512)), whole((TOK, D))],
        [pltpu.VMEM((2, D, 512), BF), pltpu.VMEM((2, D, 512), BF), pltpu.VMEM((TOK, D), BF)],
    )


def norm_back(up, n, inv, gain):
    scaled = up * gain
    center = jnp.mean(scaled, axis=-1, keepdims=True)
    spread = jnp.mean(scaled * n, axis=-1, keepdims=True)
    return inv * (scaled - center - n * spread)


def col_sum(x):
    return jnp.sum(x, axis=0, keepdims=True)


def feed_bwd_body(core_ref, slope_ref, dh_ref, hm_ref, vec_ref, u_ref, *rest):
    up, down = rest[:4], rest[4:8]
    gup, gdown, (dhm_ref, gbu_ref, gvec_ref) = rest[8:12], rest[12:16], rest[16:19]
    wu_ref, wd_ref, gu_ref, gd_ref, mt_ref, dyt_ref, dm_ref = rest[19:]
    s, core = pl.program_id(0), core_ref[0]

    @pl.when(s == 0)
    def _():
        n, _ = norm(hm_ref[...])
        mt_ref[...] = turned((n * vec_ref[2:3, :] + vec_ref[3:4, :]).astype(BF))
        dyt_ref[...] = turned(dh_ref[...].astype(BF))
        dm_ref[...] = jnp.zeros((TOK, D), F32)

    assemble(1, s, core, up, wu_ref)
    assemble(2, s, core, down, wd_ref)
    dy = dh_ref[...].astype(BF)
    total = jnp.zeros((TOK, D), F32)
    for g in (0, 1):
        u = u_ref[0, g]
        act, t = gelu_parts(u)
        slope = 0.5 * (1.0 + t) + (0.5 * C0) * u * (1.0 - t * t) * (1.0 + (3.0 * C1) * (u * u))
        du = dot(dy, wd_ref[g]) * slope
        gbu_ref[0, g : g + 1, :] = col_sum(du)
        dub = du.astype(BF)
        gd_ref[g] = dot(dyt_ref[...], act.astype(BF)).astype(BF)
        gu_ref[g] = dot(mt_ref[...], dub).astype(BF)
        total = total + dot_nt(dub, wu_ref[g])
    dm_ref[...] += total
    disassemble(1, s, core, gup, gu_ref)
    disassemble(2, s, core, gdown, gd_ref)

    @pl.when(s == 3)
    def _():
        n, inv = norm(hm_ref[...])
        dm, dh = dm_ref[...], dh_ref[...]
        dhm_ref[...] = dh + norm_back(dm, n, inv, vec_ref[2:3, :])
        gvec_ref[...] = jnp.zeros((8, D), F32)
        gvec_ref[0:1, :] = col_sum(dm * n)
        gvec_ref[1:2, :] = col_sum(dm)
        gvec_ref[2:3, :] = col_sum(dh)


def feed_bwd(core, slopes, dh, hm, vec, u, up, down):
    wide = pltpu.VMEM((2, D, 512), BF)
    return call(
        feed_bwd_body,
        "feed_bwd",
        core,
        slopes,
        (dh, hm, vec, u, *merged(1, up), *merged(2, down)),
        [whole((TOK, D)), whole((TOK, D)), whole((8, D)), per_step((4, 2, TOK, 512))]
        + quad_specs(1)
        + quad_specs(2),
        quad_shapes(1) + quad_shapes(2) + [sds((TOK, D)), sds((4, 2, 512)), sds((8, D))],
        quad_specs(1) + quad_specs(2) + [whole((TOK, D)), per_step((4, 2, 512)), whole((8, D))],
        [wide] * 4
        + [pltpu.VMEM((D, TOK), BF), pltpu.VMEM((D, TOK), BF), pltpu.VMEM((TOK, D), F32)],
    )


def attn_bwd_body(core_ref, slope_ref, dhm_ref, h_ref, vec_ref, qkv_ref, ctx_ref, *rest):
    quad, gquad, (dh_ref, gqv_ref, gvec_ref) = rest[:4], rest[4:8], rest[8:11]
    w_ref, gw_ref, at_ref, dzt_ref, da_ref = rest[11:]
    s, core = pl.program_id(0), core_ref[0]

    @pl.when(s == 0)
    def _():
        n, _ = norm(h_ref[...])
        at_ref[...] = turned((n * vec_ref[0:1, :] + vec_ref[1:2, :]).astype(BF))
        dzt_ref[...] = turned(dhm_ref[...].astype(BF))
        da_ref[...] = jnp.zeros((TOK, D), F32)

    assemble(0, s, core, quad, w_ref)
    dz = dhm_ref[...].astype(BF)
    total = jnp.zeros((TOK, D), F32)
    for g in (0, 1):
        qkv = qkv_ref[0, g]
        dctx = dot(dz, w_ref[g, :, 384:512]).astype(BF)
        gw_ref[g, :, 384:512] = dot(dzt_ref[...], ctx_ref[0, g]).astype(BF)
        grads = [[], [], []]
        for hd in (0, 1):
            q, k, v = (qkv[:, j * 128 + hd * 64 : j * 128 + hd * 64 + 64] for j in range(3))
            dc = dctx[:, hd * 64 : hd * 64 + 64]
            p = chance_of(q, k, slope_ref[s * 4 + g * 2 + hd])
            dp = dot_nt(dc, v)
            delta = jnp.sum(p * dp, axis=-1, keepdims=True)
            ds = (p * (dp - delta) * 0.125).astype(BF)
            grads[0].append(dot(ds, k))
            grads[1].append(dot_tn(ds, q))
            grads[2].append(dot_tn(p.astype(BF), dc))
        dqkv = jnp.concatenate([g_ for three in grads for g_ in three], axis=1)
        gqv_ref[0, g : g + 1, :] = col_sum(dqkv)
        dqkv = dqkv.astype(BF)
        gw_ref[g, :, 0:384] = dot(at_ref[...], dqkv).astype(BF)
        total = total + dot_nt(dqkv, w_ref[g, :, 0:384])
    da_ref[...] += total
    disassemble(0, s, core, gquad, gw_ref)

    @pl.when(s == 3)
    def _():
        n, inv = norm(h_ref[...])
        da, dhm = da_ref[...], dhm_ref[...]
        dh_ref[...] = dhm + norm_back(da, n, inv, vec_ref[0:1, :])
        gvec_ref[...] = jnp.zeros((8, D), F32)
        gvec_ref[0:1, :] = col_sum(da * n)
        gvec_ref[1:2, :] = col_sum(da)
        gvec_ref[2:3, :] = col_sum(dhm)


def attn_bwd(core, slopes, dhm, h, vec, qkv, ctx, quad):
    wide = pltpu.VMEM((2, D, 512), BF)
    return call(
        attn_bwd_body,
        "attn_bwd",
        core,
        slopes,
        (dhm, h, vec, qkv, ctx, *merged(0, quad)),
        [
            whole((TOK, D)),
            whole((TOK, D)),
            whole((8, D)),
            per_step((4, 2, TOK, 384)),
            per_step((4, 2, TOK, 128)),
        ]
        + quad_specs(0),
        quad_shapes(0) + [sds((TOK, D)), sds((4, 2, 384)), sds((8, D))],
        quad_specs(0) + [whole((TOK, D)), per_step((4, 2, 384)), whole((8, D))],
        [wide] * 2
        + [pltpu.VMEM((D, TOK), BF), pltpu.VMEM((D, TOK), BF), pltpu.VMEM((TOK, D), F32)],
    )


def orders():
    at = {a: lax.axis_index(a) for a in AXES}
    rows = []
    for half, low, z2, z1 in itertools.product((0, 1), repeat=4):
        core = at["core"] ^ half
        z = at["z"] ^ jnp.where(core == 0, z1 ^ (3 * z2), (3 * z1) ^ z2)
        rows.append(((at["ylo"] ^ low) * 4 + z) * 2 + core)
    cols = []
    for x2, x1, g in itertools.product((0, 1), repeat=3):
        x = at["x"] ^ jnp.where(at["core"] == 0, x1 ^ (3 * x2), (3 * x1) ^ x2)
        cols.append(x * 2 + (at["yhi"] ^ g))
    return at, jnp.stack(rows), jnp.stack(cols)


def one_hot(index, count):
    return (index[:, None] == jnp.arange(count)[None, :]).astype(F32)


def shards(
    hidden_in, w_qkv, w_attn_out, w_up, w_down, qv_bias, up_bias, ln_gain, row_bias, cotangent
):
    at, rows, cols = orders()
    core = at["core"].reshape(1).astype(jnp.int32)
    row_hot, col_hot = one_hot(rows, 16), one_hot(cols, 8)
    lanes = (rows[:, None] * 64 + jnp.arange(64)[None, :]).reshape(-1)
    lane_hot = one_hot(lanes, D)

    def to_own(v):
        return lax.dot_general(v, lane_hot, (((1,), (1,)), ((), ())), precision=HIGH)

    def from_own(v):
        return jnp.dot(v, lane_hot, precision=HIGH)

    heads = cols[:, None] * 2 + jnp.arange(2)[None, :]
    slopes = jnp.exp2(-8.0 * (heads.astype(F32) + 1.0) / HEADS).reshape(-1)

    small = jnp.concatenate([v.reshape(-1) for v in (ln_gain, row_bias, qv_bias, up_bias)])
    small = jnp.pad(small, (0, 1024 - small.size)).reshape(8, 128)
    small = lax.all_gather(small, AXES, axis=0, tiled=False).reshape(16, 8, 1024).astype(F32)
    wide = small[:, 0, :768]
    gains = wide[:, :256].reshape(D, LAYERS, 2)
    shifts = wide[:, 256:].reshape(D, LAYERS, 4)
    qv = small[:, :, 768:800].reshape(16, 8, 4, LAYERS, 2, 2)
    qv = qv.transpose(3, 1, 4, 5, 0, 2).reshape(LAYERS, 8, 2, 128)
    ub = small[:, :, 800:864].reshape(16, 8, 4, LAYERS, 8)
    ub = ub.transpose(3, 1, 4, 0, 2).reshape(LAYERS, 8, 512)

    weights = []
    for l in range(LAYERS):
        part0 = jnp.concatenate([w_qkv[:, l].reshape(64, 384), w_attn_out[:, l]], axis=1)
        weights.append(gather([part0, w_up[:, l], w_down[:, l]]))

    h = to_own(hidden_in)
    dh = to_own(cotangent)
    kept = []
    for l in range(LAYERS):
        vec = jnp.stack([gains[:, l, 0], shifts[:, l, 0], gains[:, l, 1], shifts[:, l, 1]]
                        + [shifts[:, l, 2], shifts[:, l, 3]])
        vec = jnp.pad(to_own(vec), ((0, 2), (0, 0)))
        qv_own = jnp.einsum("st,tjk->sjk", col_hot, qv[l], precision=HIGH)
        bias = jnp.concatenate(
            [qv_own[:, 0], jnp.zeros((8, 128), F32), qv_own[:, 1]], axis=1
        ).reshape(4, 2, 384)
        up_own = jnp.dot(col_hot, ub[l], precision=HIGH).reshape(4, 2, 512)
        mix, up, down = weights[l]
        qkv, ctx, hm = attn_fwd(core, slopes, h, vec, bias, mix)
        u, out = feed_fwd(core, slopes, hm, vec, up_own, up, down)
        kept.append((h, vec, qkv, ctx, hm, u))
        h = out
    hidden_out = from_own(h)

    shares, small_grads = [None] * LAYERS, [None] * LAYERS
    for l in reversed(range(LAYERS)):
        h, vec, qkv, ctx, hm, u = kept[l]
        mix, up, down = weights[l]
        outs = feed_bwd(core, slopes, dh, hm, vec, u, up, down)
        gup, gdown, (dhm, gbu, gvec2) = unmerged(outs[:4]), unmerged(outs[4:8]), outs[8:]
        outs = attn_bwd(core, slopes, dhm, h, vec, qkv, ctx, mix)
        gmix, (dh, gqv, gvec1) = unmerged(outs[:4]), outs[4:]
        shares[l] = [
            scatter_one(g, o) for g, o in zip((gmix, gup, gdown), ORDERS)
        ]
        vectors = jnp.stack([gvec1[0], gvec2[0], gvec1[1], gvec2[1], gvec1[2], gvec2[2]])
        columns = jnp.concatenate([gqv.reshape(8, 384), gbu.reshape(8, 512)], axis=1)
        columns = lax.dot_general(
            col_hot, columns, (((0,), (0,)), ((), ())), precision=HIGH
        )
        small_grads[l] = jnp.concatenate([from_own(vectors).reshape(-1), columns.reshape(-1)])
    grad_in = from_own(dh)

    total = lax.psum(jnp.stack(small_grads), AXES)
    p = (at["ylo"] * 4 + at["z"]) * 2 + at["core"]
    t = at["x"] * 2 + at["yhi"]
    vectors = total[:, : 6 * D].reshape(LAYERS, 6, 16, 64)
    vectors = lax.dynamic_index_in_dim(vectors, p, 2, keepdims=False)
    vectors = vectors.transpose(2, 0, 1)
    columns = total[:, 6 * D :].reshape(LAYERS, 8, 896)
    columns = lax.dynamic_index_in_dim(columns, t, 1, keepdims=False)
    gqv = columns[:, :384].reshape(LAYERS, 3, 2, 16, 4)[:, 0::2]
    gqv = lax.dynamic_index_in_dim(gqv, p, 3, keepdims=False).transpose(3, 0, 1, 2)
    gbu = columns[:, 384:].reshape(LAYERS, 8, 16, 4)
    gbu = lax.dynamic_index_in_dim(gbu, p, 2, keepdims=False).transpose(2, 0, 1)

    mixes = jnp.stack([shares[l][0] for l in range(LAYERS)], axis=1)
    return (
        hidden_out,
        grad_in,
        mixes[:, :, :384].reshape(64, LAYERS, 3, 128),
        mixes[:, :, 384:],
        jnp.stack([shares[l][1] for l in range(LAYERS)], axis=1),
        jnp.stack([shares[l][2] for l in range(LAYERS)], axis=1),
        gqv,
        gbu,
        vectors[:, :, :2],
        vectors[:, :, 2:],
    )


def solution(mesh):
    torus = Mesh(mesh.devices.reshape(SIZES), AXES)
    token = P((*DP, *TENSOR), None)
    placed = (
        token,
        P(DP, None, None, TENSOR),
        P(DP, None, TENSOR),
        P(DP, None, TENSOR),
        P(DP, None, TENSOR),
        P(DP, None, None, TENSOR),
        P(DP, None, TENSOR),
        P(DP, None, None),
        P(DP, None, None),
        token,
    )
    outs = (token, token, *placed[1:9])
    return jax.shard_map(shards, mesh=torus, in_specs=placed, out_specs=outs, check_vma=False)
```

time: 1350 us -> 1010 us (0.75)
  waiting for transfers between devices: 822 us -> 250 us
  blocking collectives: 129 us -> 347 us
  Pallas kernels: 0 us -> 124 us
  matrix products: 138 us -> 21.1 us
  starting transfers between devices: 62 us -> 98.9 us
  local copies, waits for them, and re-layouts: 124 us -> 93.1 us
    reduce_scatter x8 -> x0, waiting for transfers between devices: 515 us -> none  [the longest x4 290 us: sum_rows(): lax.psum_scatter(term_fn(jnp.int32(0), own_count * lax.axis_size('tensor'...]
    all_gather x4 -> x1, blocking collectives: 97 us -> 347 us  [shards(): lax.all_gather(small, AXES, axis=0, tiled=False).reshape(16, 8, 1024)]
    all_gather x6 -> x0, waiting for transfers between devices: 194 us -> none  [the longest x4 143 us: spread_grads(): return lax.all_gather(values, 'tensor', axis=0, tiled=True)]
    psum x0 -> x1, waiting for transfers between devices: none -> 127 us  [shards(): total = lax.psum(jnp.stack(small_grads), AXES)]
    pallas_call x0 -> x8, Pallas kernels: none -> 124 us  [call(): pl.pallas_call(body, name=name, out_shape=outs, grid_spec=pltpu.PrefetchS...]
    ppermute x0 -> x96, waiting for transfers between devices: none -> 123 us  [swap(): return lax.ppermute(v, AXES, pairs(axis, step))]
    dot_general x36 -> x14, matrix products: 138 us -> 21.1 us  [the longest x4 9.11 us: to_own(): lax.dot_general(v, lane_hot, (((1,), (1,)), ((), ())), precision=HIGH)]
    all_to_all x13 -> x0, waiting for transfers between devices: 113 us -> none  [the longest x6 81.1 us: sent_to_all(): lax.all_to_all(jnp.broadcast_to(shard[None], (length, *shard.shape)), axi...]
  transfers between devices with their start and end apart: 27 -> 97, of which waited for: 21 -> 27; matrix products, arithmetic and copies ran while one was open for 11% -> 15% of each run, Pallas kernels for 0% -> 3%
where the time goes in v1:
time: 1010 us; the launch traced here: 1000 us
  blocking collectives  347 us (34%)
  waiting for transfers between devices  250 us (25%)
  Pallas kernels  124 us (12%)
  starting transfers between devices  98.9 us (10%)
  local copies, waits for them, and re-layouts  93.1 us (9%)
  other arithmetic  50.5 us (5%)
  matrix products  21.1 us (2%)
  between operations  16.2 us (2%)
    all_gather x1, blocking collectives, shards(): lax.all_gather(small, AXES, axis=0, tiled=False).reshape(16, 8, 1024)  347 us
    psum x1, waiting for transfers between devices, shards(): total = lax.psum(jnp.stack(small_grads), AXES)  127 us
    pallas_call x8, Pallas kernels, call(): pl.pallas_call(body, name=name, out_shape=outs, grid_spec=pltpu.PrefetchS...  124 us
    ppermute x96, waiting for transfers between devices, swap(): return lax.ppermute(v, AXES, pairs(axis, step))  123 us
    ppermute x96, starting transfers between devices, swap(): return lax.ppermute(v, AXES, pairs(axis, step))  98.9 us
    convert_element_type x36, other arithmetic, plus(): return (a.astype(F32) + b.astype(F32)).astype(BF)  35.2 us
    slice x1, local copies, waits for them, and re-layouts, shards(): shifts[:, l, 3]  32.4 us
    slice x1, local copies, waits for them, and re-layouts, shards(): gains[:, l, 1]  26 us
  transfers between devices with their start and end apart: 97, of which 27 were waited for; matrix products, arithmetic and copies ran while one was open for 15% of the time, Pallas kernels for 3%

profile of v1, /device:TPU:0, one launch (start us, length us, event | category | flops | bytes accessed | tf_op | source)
XLA Modules:
  0.0 1001.2 jit_solution(10793064082314549459)
XLA Ops:
  24.1 3.1 collective-permute-start.9
  30.4 4.2 collective-permute-done.2
  34.6 3.1 collective-permute-start.17
  48.5 3.6 collective-permute-done.18
  61.0 26.6 %collective-permute-done.34 = bf16[2,2,64,512]{3,2,1,0:T(8,128)(2,1)S(1)} collective-permute-done((bf16[2,2,64,512]{3,2,1,0:T(8,128)(2,1)S(1)}, bf16[2,2,64,512]{3,2,1,0:T(8,128)(2,1)S(1)}, u32[]{:S(2)}, u32[]{:S(2)}) %collective-permute-start.34) | collective-permute-done | bytes 262176 | tf_op jit(solution)/shard_map/ppermute | solution.py:42
  95.7 7.9 collective-permute-done.43
  112.1 9.5 collective-permute-done.36
  126.5 4.4 collective-permute-done.5
  135.4 346.8 %all_gather.3 = bf16[128,8,128]{2,1,0:T(8,128)(2,1)S(1)} all-gather(bf16[1,8,128]{2,1,0:T(8,128)(2,1)S(1)} %fusion.86), channel_id=1, replica_groups=mesh['ylo'=2,'z'=4,'core'=2,'x'=4,'yhi'=2] {'ylo','z','core','x','yhi'}, dimensions={0}, use_global_device_ids=true | all-gather | bytes 264192 | tf_op jit(solution)/shard_map/all_gather | solution.py:506
  488.8 32.4 %slice_reduce_fusion = (f32[1024]{0:T(1024)S(1)}, f32[1024]{0:T(1024)S(1)}, f32[1024]{0:T(1024)S(1)}, f32[1024]{0:T(1024)S(1)}, f32[1024]{0:T(1024)S(1)}, /*inde...) fusion(f32[1024,2,4]{2,1,0:T(2,128)} %reshape.611), kind=kLoop, calls=%fused_computation.113 | loop fusion | bytes 65536 | tf_op jit(solution)/shard_map/slice | solution.py:525
  523.9 26.0 %slice_reduce_fusion.3 = (f32[1024]{0:T(1024)S(1)}, f32[1024]{0:T(1024)S(1)}, f32[1024]{0:T(1024)S(1)}, f32[1024]{0:T(1024)S(1)}) fusion(f32[1024,2,2]{2,1,0:T(2,128)S(1)} %copy-done.13), kind=kLoop, calls=%fused_computation.116 | loop fusion | bytes 32768 | tf_op jit(solution)/shard_map/slice | solution.py:524
  568.9 10.3 %attn_fwd.2 = (bf16[4,2,160,384]{3,2,1,0:T(8,128)(2,1)S(1)}, bf16[4,2,160,128]{3,2,1,0:T(8,128)(2,1)S(1)}, f32[160,1024]{1,0:T(8,128)S(1)}) custom-call(s32[1]{0:T(128)} %bitcast.core_ref, f32[16]{0:T(128)S(1)} %reshape.659.slope_ref, f32[160,1024]{1,0:T(8,128)S(1)} %fusion.34.h_ref, f32[8,1024]{1,0:T(8,128)S(1)} %pad.12.vec_ref, ...), custom_call_target="tpu_custom_call" | custom-call | tf_op jit(solution)/shard_map/attn_fwd/pallas_call | solution.py:207
  579.2 10.5 %feed_fwd.2 = (f32[4,2,160,512]{3,2,1,0:T(8,128)}, f32[160,1024]{1,0:T(8,128)S(1)}) custom-call(s32[1]{0:T(128)} %bitcast.core_ref, f32[16]{0:T(128)S(1)} %reshape.659.slope_ref, f32[160,1024]{1,0:T(8,128)S(1)} %get-tuple-element.56.hm_ref, f32[8,1024]{1,0:T(8,128)S(1)} %pad.12.vec_ref, f32[4,2,512]{2,1,0:T(2,128)S(1)} %fusion.71.bias_ref, ...), custom_call_target="tpu_custom_call" | custom-call | tf_op jit(solution)/shard_map/feed_fwd/pallas_call | solution.py:207
  589.7 10.0 attn_fwd.3
  599.7 10.4 %feed_fwd.3 = (f32[4,2,160,512]{3,2,1,0:T(8,128)}, f32[160,1024]{1,0:T(8,128)S(1)}) custom-call(s32[1]{0:T(128)} %bitcast.core_ref, f32[16]{0:T(128)S(1)} %reshape.659.slope_ref, f32[160,1024]{1,0:T(8,128)S(1)} %get-tuple-element.58.hm_ref, f32[8,1024]{1,0:T(8,128)S(1)} %pad.13.vec_ref, f32[4,2,512]{2,1,0:T(2,128)S(1)} %fusion.69.bias_ref, ...), custom_call_target="tpu_custom_call" | custom-call | tf_op jit(solution)/shard_map/feed_fwd/pallas_call | solution.py:207
  610.2 19.5 %feed_bwd.2 = (bf16[2,4,4,64,512]{4,3,2,1,0:T(8,128)(2,1)S(1)}, bf16[2,4,4,64,512]{4,3,2,1,0:T(8,128)(2,1)}, bf16[2,4,4,64,512]{4,3,2,1,0:T(8,128)(2,1)}, bf16[2...) custom-call(s32[1]{0:T(128)} %bitcast.core_ref, ...), custom_call_target="tpu_custom_call" | custom-call | tf_op jit(solution)/shard_map/feed_bwd/pallas_call | solution.py:207
  629.7 22.0 %attn_bwd.2 = (bf16[8,4,64,512]{3,2,1,0:T(8,128)(2,1)S(1)}, bf16[8,4,64,512]{3,2,1,0:T(8,128)(2,1)}, bf16[8,4,64,512]{3,2,1,0:T(8,128)(2,1)}, bf16[8,4,64,512]{3...) custom-call(s32[1]{0:T(128)} %bitcast.core_ref, ...), custom_call_target="tpu_custom_call" | custom-call | tf_op jit(solution)/shard_map/attn_bwd/pallas_call | solution.py:207
  652.9 19.6 %feed_bwd.3 = (bf16[2,4,4,64,512]{4,3,2,1,0:T(8,128)(2,1)S(1)}, bf16[2,4,4,64,512]{4,3,2,1,0:T(8,128)(2,1)}, bf16[2,4,4,64,512]{4,3,2,1,0:T(8,128)(2,1)}, bf16[2...) custom-call(s32[1]{0:T(128)} %bitcast.core_ref, ...), custom_call_target="tpu_custom_call" | custom-call | tf_op jit(solution)/shard_map/feed_bwd/pallas_call | solution.py:207
  673.9 21.9 %attn_bwd.3 = (bf16[8,4,64,512]{3,2,1,0:T(8,128)(2,1)S(1)}, bf16[8,4,64,512]{3,2,1,0:T(8,128)(2,1)}, bf16[8,4,64,512]{3,2,1,0:T(8,128)(2,1)}, bf16[8,4,64,512]{3...) custom-call(s32[1]{0:T(128)} %bitcast.core_ref, ...), custom_call_target="tpu_custom_call" | custom-call | tf_op jit(solution)/shard_map/attn_bwd/pallas_call | solution.py:207
  718.1 127.2 %all-reduce.5.cloned.1.call-done = f32[2,13312]{1,0:T(2,128)} async-done(((f32[2,13312]{1,0:T(2,128)}), f32[2,13312]{1,0:T(2,128)}) %all-reduce.5.cloned.1.call-update) | async-done | bytes 106512 | tf_op jit(solution)/shard_map/psum | solution.py:558
  847.2 4.5 fusion.10
  853.6 3.7 fusion.6
  862.2 3.1 fusion.2
  874.0 5.4 collective-permute-done.50
  881.2 3.3 add_convert_fusion.5
  887.2 3.3 add_convert_fusion.3
  891.6 3.7 collective-permute-done.82
  900.1 6.5 collective-permute-done.58
  910.4 3.9 collective-permute-done.74
  919.5 11.5 %collective-permute-done.90 = bf16[2,2,2,2,2,64,512]{6,5,4,3,2,1,0:T(8,128)(2,1)S(1)} collective-permute-done((bf16[2,2,2,2,2,64,512]{6,5,4,3,2,1,0:T(8,128)(2,1)S(1)}, bf16[2,2,2,2,2,64,512]{6,5,4,3,2,1,0:T(8,128)(2,1)S(1)}, u32[]{:S(2)}, u32[]{:S(2)}) %collective-permute-start.90) | collective-permute-done | bytes 2097184 | tf_op jit(solution)/shard_map/ppermute | solution.py:42
  939.1 12.3 %collective-permute-done.75 = bf16[2,2,2,2,64,512]{5,4,3,2,1,0:T(8,128)(2,1)S(1)} collective-permute-done((bf16[2,2,2,2,64,512]{5,4,3,2,1,0:T(8,128)(2,1)S(1)}, bf16[2,2,2,2,64,512]{5,4,3,2,1,0:T(8,128)(2,1)S(1)}, u32[]{:S(2)}, u32[]{:S(2)}) %collective-permute-start.75) | collective-permute-done | bytes 1048608 | tf_op jit(solution)/shard_map/ppermute | solution.py:42
  960.4 5.8 collective-permute-done.60
  (493 shorter events, 199.0 us)
Async XLA Ops:
  7.2 838.1 %all-reduce.5.cloned.1.call-start = ((), (), s32[]{:S(2)}) async-start(), calls=%async_computation | async-start | bytes 212992 | tf_op jit(solution)/shard_map/psum | solution.py:558
  27.5 29.3 %collective-permute-start.33 = (bf16[2,64,512]{2,1,0:T(8,128)(2,1)S(1)}, bf16[2,64,512]{2,1,0:T(8,128)(2,1)S(1)}, u32[]{:S(2)}, u32[]{:S(2)}) collective-permute-start(bf16[2,64,512]{2,1,0:T(8,128)(2,1)S(1)} %get-tuple-element.199), channel_id=1, source_target_pairs={{0,65},{1,64},{2,67},{3,66},{4,69},{5,68},{6,71},{7,70},{8,72},{9,... | collective-permute-start | bytes 393224 | tf_op jit(solution)/shard_map/ppermute | solution.py:42
  52.0 41.0 %collective-permute-start.4 = (bf16[2,2,2,2,64,512]{5,4,3,2,1,0:T(8,128)(2,1)S(1)}, bf16[2,2,2,2,64,512]{5,4,3,2,1,0:T(8,128)(2,1)S(1)}, u32[]{:S(2)}, u32[]{:S(2)}) collective-permute-start(bf16[2,2,2,2,64,512]{5,4,3,2,1,0:T(8,128)(2,1)S(1)} %get-tuple-element.167), channel_id=1, source_target_pairs={{0,16},{1,17},{2,18},{3,19},{4,20},{5,21},{6,22},{7,23},{8,56},{9,... | collective-permute-start | bytes 3145736 | tf_op jit(solution)/shard_map/ppermute | solution.py:42
  54.0 36.4 %collective-permute-start.19 = (bf16[2,2,2,64,512]{4,3,2,1,0:T(8,128)(2,1)S(1)}, bf16[2,2,2,64,512]{4,3,2,1,0:T(8,128)(2,1)S(1)}, u32[]{:S(2)}, u32[]{:S(2)}) collective-permute-start(bf16[2,2,2,64,512]{4,3,2,1,0:T(8,128)(2,1)S(1)} %get-tuple-element.175), channel_id=1, source_target_pairs={{0,6},{1,7},{2,4},{3,5},{4,2},{5,3},{6,0},{7,1},{8,10},{9,11},{10,... | collective-permute-start | bytes 1572872 | tf_op jit(solution)/shard_map/ppermute | solution.py:42
  56.9 37.1 %collective-permute-start.28 = (bf16[2,2,2,2,64,512]{5,4,3,2,1,0:T(8,128)(2,1)S(1)}, bf16[2,2,2,2,64,512]{5,4,3,2,1,0:T(8,128)(2,1)S(1)}, u32[]{:S(2)}, u32[]{:S(2)}) collective-permute-start(bf16[2,2,2,2,64,512]{5,4,3,2,1,0:T(8,128)(2,1)S(1)} %get-tuple-element.161), channel_id=1, source_target_pairs={{0,16},{1,17},{2,18},{3,19},{4,20},{5,21},{6,22},{7,23},{8,56},{9,... | collective-permute-start | bytes 3145736 | tf_op jit(solution)/shard_map/ppermute | solution.py:42
  57.3 30.2 %collective-permute-start.34 = (bf16[2,2,64,512]{3,2,1,0:T(8,128)(2,1)S(1)}, bf16[2,2,64,512]{3,2,1,0:T(8,128)(2,1)S(1)}, u32[]{:S(2)}, u32[]{:S(2)}) collective-permute-start(bf16[2,2,64,512]{3,2,1,0:T(8,128)(2,1)S(1)} %get-tuple-element.183), channel_id=1, source_target_pairs={{0,16},{1,17},{2,18},{3,19},{4,20},{5,21},{6,22},{7,23},{8,56},{9,... | collective-permute-start | bytes 786440 | tf_op jit(solution)/shard_map/ppermute | solution.py:42
  59.2 32.7 %collective-permute-start.11 = (bf16[2,2,2,64,512]{4,3,2,1,0:T(8,128)(2,1)S(1)}, bf16[2,2,2,64,512]{4,3,2,1,0:T(8,128)(2,1)S(1)}, u32[]{:S(2)}, u32[]{:S(2)}) collective-permute-start(bf16[2,2,2,64,512]{4,3,2,1,0:T(8,128)(2,1)S(1)} %get-tuple-element.177), channel_id=1, source_target_pairs={{0,48},{1,49},{2,50},{3,51},{4,52},{5,53},{6,54},{7,55},{8,24},{9,... | collective-permute-start | bytes 1572872 | tf_op jit(solution)/shard_map/ppermute | solution.py:42
  94.0 32.5 %collective-permute-start.6 = (bf16[2,2,2,2,2,64,512]{6,5,4,3,2,1,0:T(8,128)(2,1)S(1)}, bf16[2,2,2,2,2,64,512]{6,5,4,3,2,1,0:T(8,128)(2,1)S(1)}, u32[]{:S(2)}, u32[]{:S(2)}) collective-permute-start(bf16[2,2,2,2,2,64,512]{6,5,4,3,2,1,0:T(8,128)(2,1)S(1)} %pad_maximum_fusion), channel_id=1, source_target_pairs={{0,8},{1,9},{2,10},{3,11},{4,12},{5,13},{6,14},{7,15},{8,0},{9,1},... | collective-permute-start | bytes 6291464 | tf_op jit(solution)/shard_map/ppermute | solution.py:42
  105.0 28.7 %collective-permute-start.30 = (bf16[2,2,2,2,2,64,512]{6,5,4,3,2,1,0:T(8,128)(2,1)}, bf16[2,2,2,2,2,64,512]{6,5,4,3,2,1,0:T(8,128)(2,1)}, u32[]{:S(2)}, u32[]{:S(2)}) collective-permute-start(bf16[2,2,2,2,2,64,512]{6,5,4,3,2,1,0:T(8,128)(2,1)} %pad_maximum_fusion.5), channel_id=1, source_target_pairs={{0,8},{1,9},{2,10},{3,11},{4,12},{5,13},{6,14},{7,15},{8,0},{9,1},... | collective-permute-start | bytes 6291464 | tf_op jit(solution)/shard_map/ppermute | solution.py:42
  121.6 401.1 %collective-permute-start.29 = (bf16[2,2,2,2,2,64,512]{6,5,4,3,2,1,0:T(8,128)(2,1)}, bf16[2,2,2,2,2,64,512]{6,5,4,3,2,1,0:T(8,128)(2,1)}, u32[]{:S(2)}, u32[]{:S(2)}) collective-permute-start(bf16[2,2,2,2,2,64,512]{6,5,4,3,2,1,0:T(8,128)(2,1)} %pad_maximum_fusion.5), channel_id=1, source_target_pairs={{0,48},{1,49},{2,50},{3,51},{4,52},{5,53},{6,54},{7,55},{8,24},{9,... | collective-permute-start | bytes 6291464 | tf_op jit(solution)/shard_map/ppermute | solution.py:42
  125.1 397.7 %collective-permute-start.37 = (bf16[2,2,2,2,2,64,512]{6,5,4,3,2,1,0:T(8,128)(2,1)}, bf16[2,2,2,2,2,64,512]{6,5,4,3,2,1,0:T(8,128)(2,1)}, u32[]{:S(2)}, u32[]{:S(2)}) collective-permute-start(bf16[2,2,2,2,2,64,512]{6,5,4,3,2,1,0:T(8,128)(2,1)} %pad_maximum_fusion.7), channel_id=1, source_target_pairs={{0,6},{1,7},{2,4},{3,5},{4,2},{5,3},{6,0},{7,1},{8,10},{9,11},{10,... | collective-permute-start | bytes 6291464 | tf_op jit(solution)/shard_map/ppermute | solution.py:42
  126.5 396.3 %collective-permute-start.14 = (bf16[2,2,2,2,2,64,512]{6,5,4,3,2,1,0:T(8,128)(2,1)}, bf16[2,2,2,2,2,64,512]{6,5,4,3,2,1,0:T(8,128)(2,1)}, u32[]{:S(2)}, u32[]{:S(2)}) collective-permute-start(bf16[2,2,2,2,2,64,512]{6,5,4,3,2,1,0:T(8,128)(2,1)} %pad_maximum_fusion.2), channel_id=1, source_target_pairs={{0,8},{1,9},{2,10},{3,11},{4,12},{5,13},{6,14},{7,15},{8,0},{9,1},... | collective-permute-start | bytes 6291464 | tf_op jit(solution)/shard_map/ppermute | solution.py:42
  130.9 392.4 %collective-permute-start.13 = (bf16[2,2,2,2,2,64,512]{6,5,4,3,2,1,0:T(8,128)(2,1)}, bf16[2,2,2,2,2,64,512]{6,5,4,3,2,1,0:T(8,128)(2,1)}, u32[]{:S(2)}, u32[]{:S(2)}) collective-permute-start(bf16[2,2,2,2,2,64,512]{6,5,4,3,2,1,0:T(8,128)(2,1)} %pad_maximum_fusion.2), channel_id=1, source_target_pairs={{0,6},{1,7},{2,4},{3,5},{4,2},{5,3},{6,0},{7,1},{8,10},{9,11},{10,... | collective-permute-start | bytes 6291464 | tf_op jit(solution)/shard_map/ppermute | solution.py:42
  133.7 389.7 %collective-permute-start.21 = (bf16[2,2,2,2,2,64,512]{6,5,4,3,2,1,0:T(8,128)(2,1)}, bf16[2,2,2,2,2,64,512]{6,5,4,3,2,1,0:T(8,128)(2,1)}, u32[]{:S(2)}, u32[]{:S(2)}) collective-permute-start(bf16[2,2,2,2,2,64,512]{6,5,4,3,2,1,0:T(8,128)(2,1)} %pad_maximum_fusion.4), channel_id=1, source_target_pairs={{0,65},{1,64},{2,67},{3,66},{4,69},{5,68},{6,71},{7,70},{8,72},{9,... | collective-permute-start | bytes 6291464 | tf_op jit(solution)/shard_map/ppermute | solution.py:42
  522.7 32.0 %collective-permute-start.22 = (bf16[2,2,2,2,2,64,512]{6,5,4,3,2,1,0:T(8,128)(2,1)}, bf16[2,2,2,2,2,64,512]{6,5,4,3,2,1,0:T(8,128)(2,1)}, u32[]{:S(2)}, u32[]{:S(2)}) collective-permute-start(bf16[2,2,2,2,2,64,512]{6,5,4,3,2,1,0:T(8,128)(2,1)} %pad_maximum_fusion.4), channel_id=1, source_target_pairs={{0,8},{1,9},{2,10},{3,11},{4,12},{5,13},{6,14},{7,15},{8,0},{9,1},... | collective-permute-start | bytes 6291464 | tf_op jit(solution)/shard_map/ppermute | solution.py:42
  522.7 31.8 %collective-permute-start.45 = (bf16[2,2,2,2,2,64,512]{6,5,4,3,2,1,0:T(8,128)(2,1)}, bf16[2,2,2,2,2,64,512]{6,5,4,3,2,1,0:T(8,128)(2,1)}, u32[]{:S(2)}, u32[]{:S(2)}) collective-permute-start(bf16[2,2,2,2,2,64,512]{6,5,4,3,2,1,0:T(8,128)(2,1)} %pad_maximum_fusion.9), channel_id=1, source_target_pairs={{0,65},{1,64},{2,67},{3,66},{4,69},{5,68},{6,71},{7,70},{8,72},{9,... | collective-permute-start | bytes 6291464 | tf_op jit(solution)/shard_map/ppermute | solution.py:42
  522.8 32.3 %collective-permute-start.7 = (bf16[2,2,2,2,2,64,512]{6,5,4,3,2,1,0:T(8,128)(2,1)}, bf16[2,2,2,2,2,64,512]{6,5,4,3,2,1,0:T(8,128)(2,1)}, u32[]{:S(2)}, u32[]{:S(2)}) collective-permute-start(bf16[2,2,2,2,2,64,512]{6,5,4,3,2,1,0:T(8,128)(2,1)} %collective-permute-done.5), channel_id=1, source_target_pairs={{0,8},{1,9},{2,10},{3,11},{4,12},{5,13},{6,14},{7,15},{8,0},{9,1},... | collective-permute-start | bytes 6291464 | tf_op jit(solution)/shard_map/ppermute | solution.py:42
  523.3 31.9 %collective-permute-start.15 = (bf16[2,2,2,2,2,64,512]{6,5,4,3,2,1,0:T(8,128)(2,1)}, bf16[2,2,2,2,2,64,512]{6,5,4,3,2,1,0:T(8,128)(2,1)}, u32[]{:S(2)}, u32[]{:S(2)}) collective-permute-start(bf16[2,2,2,2,2,64,512]{6,5,4,3,2,1,0:T(8,128)(2,1)} %collective-permute-done.13), channel_id=1, source_target_pairs={{0,8},{1,9},{2,10},{3,11},{4,12},{5,13},{6,14},{7,15},{8,0},{9,1},... | collective-permute-start | bytes 6291464 | tf_op jit(solution)/shard_map/ppermute | solution.py:42
  523.4 32.2 %collective-permute-start.23 = (bf16[2,2,2,2,2,64,512]{6,5,4,3,2,1,0:T(8,128)(2,1)}, bf16[2,2,2,2,2,64,512]{6,5,4,3,2,1,0:T(8,128)(2,1)}, u32[]{:S(2)}, u32[]{:S(2)}) collective-permute-start(bf16[2,2,2,2,2,64,512]{6,5,4,3,2,1,0:T(8,128)(2,1)} %collective-permute-done.21), channel_id=1, source_target_pairs={{0,8},{1,9},{2,10},{3,11},{4,12},{5,13},{6,14},{7,15},{8,0},{9,1},... | collective-permute-start | bytes 6291464 | tf_op jit(solution)/shard_map/ppermute | solution.py:42
  554.5 45.2 %collective-permute-start.38 = (bf16[2,2,2,2,2,64,512]{6,5,4,3,2,1,0:T(8,128)(2,1)}, bf16[2,2,2,2,2,64,512]{6,5,4,3,2,1,0:T(8,128)(2,1)}, u32[]{:S(2)}, u32[]{:S(2)}) collective-permute-start(bf16[2,2,2,2,2,64,512]{6,5,4,3,2,1,0:T(8,128)(2,1)} %pad_maximum_fusion.7), channel_id=1, source_target_pairs={{0,8},{1,9},{2,10},{3,11},{4,12},{5,13},{6,14},{7,15},{8,0},{9,1},... | collective-permute-start | bytes 6291464 | tf_op jit(solution)/shard_map/ppermute | solution.py:42
  554.7 45.0 %collective-permute-start.46 = (bf16[2,2,2,2,2,64,512]{6,5,4,3,2,1,0:T(8,128)(2,1)}, bf16[2,2,2,2,2,64,512]{6,5,4,3,2,1,0:T(8,128)(2,1)}, u32[]{:S(2)}, u32[]{:S(2)}) collective-permute-start(bf16[2,2,2,2,2,64,512]{6,5,4,3,2,1,0:T(8,128)(2,1)} %pad_maximum_fusion.9), channel_id=1, source_target_pairs={{0,8},{1,9},{2,10},{3,11},{4,12},{5,13},{6,14},{7,15},{8,0},{9,1},... | collective-permute-start | bytes 6291464 | tf_op jit(solution)/shard_map/ppermute | solution.py:42
  555.1 34.6 %collective-permute-start.31 = (bf16[2,2,2,2,2,64,512]{6,5,4,3,2,1,0:T(8,128)(2,1)}, bf16[2,2,2,2,2,64,512]{6,5,4,3,2,1,0:T(8,128)(2,1)}, u32[]{:S(2)}, u32[]{:S(2)}) collective-permute-start(bf16[2,2,2,2,2,64,512]{6,5,4,3,2,1,0:T(8,128)(2,1)} %collective-permute-done.29), channel_id=1, source_target_pairs={{0,8},{1,9},{2,10},{3,11},{4,12},{5,13},{6,14},{7,15},{8,0},{9,1},... | collective-permute-start | bytes 6291464 | tf_op jit(solution)/shard_map/ppermute | solution.py:42
  555.2 44.5 %collective-permute-start.39 = (bf16[2,2,2,2,2,64,512]{6,5,4,3,2,1,0:T(8,128)(2,1)}, bf16[2,2,2,2,2,64,512]{6,5,4,3,2,1,0:T(8,128)(2,1)}, u32[]{:S(2)}, u32[]{:S(2)}) collective-permute-start(bf16[2,2,2,2,2,64,512]{6,5,4,3,2,1,0:T(8,128)(2,1)} %collective-permute-done.37), channel_id=1, source_target_pairs={{0,8},{1,9},{2,10},{3,11},{4,12},{5,13},{6,14},{7,15},{8,0},{9,1},... | collective-permute-start | bytes 6291464 | tf_op jit(solution)/shard_map/ppermute | solution.py:42
  555.6 44.1 %collective-permute-start.47 = (bf16[2,2,2,2,2,64,512]{6,5,4,3,2,1,0:T(8,128)(2,1)}, bf16[2,2,2,2,2,64,512]{6,5,4,3,2,1,0:T(8,128)(2,1)}, u32[]{:S(2)}, u32[]{:S(2)}) collective-permute-start(bf16[2,2,2,2,2,64,512]{6,5,4,3,2,1,0:T(8,128)(2,1)} %collective-permute-done.45), channel_id=1, source_target_pairs={{0,8},{1,9},{2,10},{3,11},{4,12},{5,13},{6,14},{7,15},{8,0},{9,1},... | collective-permute-start | bytes 6291464 | tf_op jit(solution)/shard_map/ppermute | solution.py:42
  707.9 143.9 %collective-permute-start.65 = (bf16[2,2,2,2,2,64,512]{6,5,4,3,2,1,0:T(8,128)(2,1)}, bf16[2,2,2,2,2,64,512]{6,5,4,3,2,1,0:T(8,128)(2,1)}, u32[]{:S(2)}, u32[]{:S(2)}) collective-permute-start(bf16[2,2,2,2,2,64,512]{6,5,4,3,2,1,0:T(8,128)(2,1)} %bitcast.607), channel_id=1, source_target_pairs={{0,8},{1,9},{2,10},{3,11},{4,12},{5,13},{6,14},{7,15},{8,0},{9,1},... | collective-permute-start | bytes 6291464 | tf_op jit(solution)/shard_map/ppermute | solution.py:42
  708.0 149.3 %collective-permute-start.81 = (bf16[2,2,2,2,2,64,512]{6,5,4,3,2,1,0:T(8,128)(2,1)}, bf16[2,2,2,2,2,64,512]{6,5,4,3,2,1,0:T(8,128)(2,1)}, u32[]{:S(2)}, u32[]{:S(2)}) collective-permute-start(bf16[2,2,2,2,2,64,512]{6,5,4,3,2,1,0:T(8,128)(2,1)} %bitcast.606), channel_id=1, source_target_pairs={{0,8},{1,9},{2,10},{3,11},{4,12},{5,13},{6,14},{7,15},{8,0},{9,1},... | collective-permute-start | bytes 6291464 | tf_op jit(solution)/shard_map/ppermute | solution.py:42
  708.4 149.4 %collective-permute-start.57 = (bf16[2,2,2,2,2,64,512]{6,5,4,3,2,1,0:T(8,128)(2,1)}, bf16[2,2,2,2,2,64,512]{6,5,4,3,2,1,0:T(8,128)(2,1)}, u32[]{:S(2)}, u32[]{:S(2)}) collective-permute-start(bf16[2,2,2,2,2,64,512]{6,5,4,3,2,1,0:T(8,128)(2,1)} %bitcast.605), channel_id=1, source_target_pairs={{0,8},{1,9},{2,10},{3,11},{4,12},{5,13},{6,14},{7,15},{8,0},{9,1},... | collective-permute-start | bytes 6291464 | tf_op jit(solution)/shard_map/ppermute | solution.py:42
  712.0 155.8 %collective-permute-start.73 = (bf16[2,2,2,2,2,64,512]{6,5,4,3,2,1,0:T(8,128)(2,1)}, bf16[2,2,2,2,2,64,512]{6,5,4,3,2,1,0:T(8,128)(2,1)}, u32[]{:S(2)}, u32[]{:S(2)}) collective-permute-start(bf16[2,2,2,2,2,64,512]{6,5,4,3,2,1,0:T(8,128)(2,1)} %bitcast.188), channel_id=1, source_target_pairs={{0,8},{1,9},{2,10},{3,11},{4,12},{5,13},{6,14},{7,15},{8,0},{9,1},... | collective-permute-start | bytes 6291464 | tf_op jit(solution)/shard_map/ppermute | solution.py:42
  714.9 153.1 %collective-permute-start.89 = (bf16[2,2,2,2,2,64,512]{6,5,4,3,2,1,0:T(8,128)(2,1)}, bf16[2,2,2,2,2,64,512]{6,5,4,3,2,1,0:T(8,128)(2,1)}, u32[]{:S(2)}, u32[]{:S(2)}) collective-permute-start(bf16[2,2,2,2,2,64,512]{6,5,4,3,2,1,0:T(8,128)(2,1)} %bitcast.218), channel_id=1, source_target_pairs={{0,8},{1,9},{2,10},{3,11},{4,12},{5,13},{6,14},{7,15},{8,0},{9,1},... | collective-permute-start | bytes 6291464 | tf_op jit(solution)/shard_map/ppermute | solution.py:42
  857.9 27.6 %collective-permute-start.66 = (bf16[2,2,2,2,2,64,512]{6,5,4,3,2,1,0:T(8,128)(2,1)}, bf16[2,2,2,2,2,64,512]{6,5,4,3,2,1,0:T(8,128)(2,1)}, u32[]{:S(2)}, u32[]{:S(2)}) collective-permute-start(bf16[2,2,2,2,2,64,512]{6,5,4,3,2,1,0:T(8,128)(2,1)} %fusion.6), channel_id=1, source_target_pairs={{0,6},{1,7},{2,4},{3,5},{4,2},{5,3},{6,0},{7,1},{8,10},{9,11},{10,... | collective-permute-start | bytes 6291464 | tf_op jit(solution)/shard_map/ppermute | solution.py:42
  885.4 28.8 %collective-permute-start.74 = (bf16[2,2,2,2,2,64,512]{6,5,4,3,2,1,0:T(8,128)(2,1)S(1)}, bf16[2,2,2,2,2,64,512]{6,5,4,3,2,1,0:T(8,128)(2,1)S(1)}, u32[]{:S(2)}, u32[]{:S(2)}) collective-permute-start(bf16[2,2,2,2,2,64,512]{6,5,4,3,2,1,0:T(8,128)(2,1)S(1)} %fusion.4), channel_id=1, source_target_pairs={{0,6},{1,7},{2,4},{3,5},{4,2},{5,3},{6,0},{7,1},{8,10},{9,11},{10,... | collective-permute-start | bytes 6291464 | tf_op jit(solution)/shard_map/ppermute | solution.py:42
  895.3 35.7 %collective-permute-start.90 = (bf16[2,2,2,2,2,64,512]{6,5,4,3,2,1,0:T(8,128)(2,1)S(1)}, bf16[2,2,2,2,2,64,512]{6,5,4,3,2,1,0:T(8,128)(2,1)S(1)}, u32[]{:S(2)}, u32[]{:S(2)}) collective-permute-start(bf16[2,2,2,2,2,64,512]{6,5,4,3,2,1,0:T(8,128)(2,1)S(1)} %fusion), channel_id=1, source_target_pairs={{0,65},{1,64},{2,67},{3,66},{4,69},{5,68},{6,71},{7,70},{8,72},{9,... | collective-permute-start | bytes 6291464 | tf_op jit(solution)/shard_map/ppermute | solution.py:42
  (112 other events, 2215.4 us)
Sparse Core Ops, SparseCore 0:
  709.5 135.7 all-reduce.4

commit v2 on v1

--- a/solution.py
+++ b/solution.py
@@ -42,33 +42,104 @@
     return lax.ppermute(v, AXES, pairs(axis, step))
 
 
-def gather(parts):
-    bufs = list(parts)
-    res = [None] * len(parts)
-    for n in range(6):
-        recv = [swap(b, ORDERS[i][n // 2], n % 2 + 1) for i, b in enumerate(bufs)]
-        if n < 5:
-            bufs = [jnp.stack([b, r]) for b, r in zip(bufs, recv)]
-        else:
-            for i in range(len(parts)):
-                res[i] = (bufs[i], recv[i], swap(bufs[i], "core"), swap(recv[i], "core"))
-    return res
+def plain_pairs(axis, flip):
+    out = []
+    for ylo, z, core, x, yhi in itertools.product(*map(range, SIZES)):
+        c = {"x": x, "y": 2 * yhi + ylo, "z": z, "core": core}
+        c[axis] ^= flip
+        src = np.ravel_multi_index((ylo, z, core, x, yhi), SIZES)
+        dst = np.ravel_multi_index((c["y"] & 1, c["z"], c["core"], c["x"], c["y"] >> 1), SIZES)
+        out.append((int(src), int(dst)))
+    return out
+
+
+def plain_swap(v, axis, flip):
+    return lax.ppermute(v, AXES, plain_pairs(axis, flip))
+
+
+COMMON = 3
+
+
+def joined(*values):
+    return lax.optimization_barrier(values)
+
+
+def exchange(bufs, n):
+    return [swap(b, ORDERS[i][n // 2], n % 2 + 1) for i, b in enumerate(bufs)]
+
+
+def doubled(bufs, recv):
+    return [jnp.stack([b, r]) for b, r in zip(bufs, recv)]
+
+
+def over_cores(values):
+    return [swap(v, "core") for v in values]
+
+
+def small_step(n, rows, cols):
+    def both(r, c, fn):
+        flat = jnp.concatenate([r.reshape(96, 128), c.reshape(-1, 128)])
+        got = fn(flat)
+        return got[:96].reshape(12, 1024), got[96:].reshape(c.shape)
+
+    if n < 3:
+        axis, flip = (("z", 1), ("z", 2), ("y", 1))[n]
+        r, c = both(rows, cols, lambda v: plain_swap(v, axis, flip))
+        return rows + r, cols + c
+    if n == 3:
+        return rows, jnp.stack([cols, plain_swap(cols, "y", 2)])
+    if n < 6:
+        return rows, jnp.stack([cols, swap(cols, "x", n - 3)])
+    r, c = both(rows, cols, lambda v: swap(v, "core"))
+    return rows + r, cols + c.swapaxes(0, 1)
+
+
+def sum_small(rows, cols):
+    def both(r, c, fn):
+        rr, cc = r.reshape(-1, 128), c.reshape(-1, 128)
+        got = fn(jnp.concatenate([rr, cc]))
+        return got[: rr.shape[0]].reshape(r.shape), got[rr.shape[0] :].reshape(c.shape)
+
+    n = cols.shape[-1]
+    rows = rows.reshape(12, 2, 512)
+    r, c = both(rows[:, 1], cols, lambda v: swap(v, "core"))
+    rows, cols = rows[:, 0] + r, cols + c.swapaxes(0, 1)
+    for step in (2, 1):
+        r, c = both(rows, cols[1], lambda v: swap(v, "x", step))
+        rows, cols = rows + r, cols[0] + c
+    r, c = both(rows, cols[1], lambda v: plain_swap(v, "y", 2))
+    rows, cols = rows + r, cols[0] + c
+    rows = rows.reshape(12, 2, 256)
+    r, c = both(rows[:, 1], cols, lambda v: plain_swap(v, "y", 1))
+    rows, cols = rows[:, 0] + r, cols + c
+    for step in (2, 1):
+        rows = rows.reshape(12, 2, -1)
+        away = rows[:, 1]
+        width = away.shape[-1]
+        away = jnp.pad(away, ((0, 0), (0, 128 - width)))
+        r, c = both(away, cols, lambda v: swap(v, "z", step))
+        rows, cols = rows[:, 0] + r[:, :width], cols + c
+    return rows, cols
 
 
 def plus(a, b):
     return (a.astype(F32) + b.astype(F32)).astype(BF)
 
 
-def scatter_one(grad, order):
-    own_lo, own_hi, oth_lo, oth_hi = grad
-    hi = plus(own_hi, swap(oth_hi, "core"))
-    lo = plus(own_lo, swap(oth_lo, "core"))
-    for n in reversed(range(6)):
+def halved(lo, hi, order, n):
+    s = plus(lo, swap(hi, order[n // 2], n % 2 + 1))
+    return s[0], s[1]
+
+
+def scatter_both(sums, order):
+    s = jnp.stack(sums, axis=3)
+    for n in reversed(range(COMMON)):
+        lo, hi = s[0], s[1]
         r = swap(hi, order[n // 2], n % 2 + 1)
-        if n == 0:
-            return lo.astype(F32) + r.astype(F32)
-        s = plus(lo, r)
-        lo, hi = s[0], s[1]
+        if n:
+            s = plus(lo, r)
+        else:
+            return jnp.swapaxes(lo.astype(F32) + r.astype(F32), 0, 1)
 
 
 def norm(h):
@@ -488,7 +559,6 @@
 ):
     at, rows, cols = orders()
     core = at["core"].reshape(1).astype(jnp.int32)
-    row_hot, col_hot = one_hot(rows, 16), one_hot(cols, 8)
     lanes = (rows[:, None] * 64 + jnp.arange(64)[None, :]).reshape(-1)
     lane_hot = one_hot(lanes, D)
 
@@ -501,85 +571,148 @@
     heads = cols[:, None] * 2 + jnp.arange(2)[None, :]
     slopes = jnp.exp2(-8.0 * (heads.astype(F32) + 1.0) / HEADS).reshape(-1)
 
-    small = jnp.concatenate([v.reshape(-1) for v in (ln_gain, row_bias, qv_bias, up_bias)])
-    small = jnp.pad(small, (0, 1024 - small.size)).reshape(8, 128)
-    small = lax.all_gather(small, AXES, axis=0, tiled=False).reshape(16, 8, 1024).astype(F32)
-    wide = small[:, 0, :768]
-    gains = wide[:, :256].reshape(D, LAYERS, 2)
-    shifts = wide[:, 256:].reshape(D, LAYERS, 4)
-    qv = small[:, :, 768:800].reshape(16, 8, 4, LAYERS, 2, 2)
-    qv = qv.transpose(3, 1, 4, 5, 0, 2).reshape(LAYERS, 8, 2, 128)
-    ub = small[:, :, 800:864].reshape(16, 8, 4, LAYERS, 8)
-    ub = ub.transpose(3, 1, 4, 0, 2).reshape(LAYERS, 8, 512)
-
-    weights = []
+    p = (at["ylo"] * 4 + at["z"]) * 2 + at["core"]
+    put_row = (jnp.arange(D)[None, :] == p * 64 + jnp.arange(64)[:, None]).astype(BF)
+    put_col = (jnp.arange(64)[None, :] == p * 4 + jnp.arange(4)[:, None]).astype(BF)
+    own_rows = jnp.concatenate([ln_gain.reshape(64, 4), row_bias.reshape(64, 8)], axis=1)
+    own_cols = jnp.concatenate([qv_bias.reshape(4, 2, 4), up_bias], axis=2).reshape(4, 24)
+    small = (dot_tn(own_rows, put_row).astype(BF), dot_tn(own_cols, put_col).astype(BF))
+    h, dh = to_own(hidden_in), to_own(cotangent)
+    bufs = joined(
+        jnp.concatenate([w_qkv.reshape(64, LAYERS, 384), w_attn_out], axis=2).swapaxes(0, 1),
+        w_up.swapaxes(0, 1),
+        w_down.swapaxes(0, 1),
+    )
+    for n in range(COMMON):
+        recv, small = joined(exchange(bufs, n), small_step(n, *small))
+        bufs = doubled(bufs, recv)
+    first, second = ([b[..., l, :, :] for b in bufs] for l in range(LAYERS))
+
+    for n in (3, 4):
+        recv, small = joined(exchange(first, n), small_step(n, *small))
+        first = doubled(first, recv)
+    first_hi, first_oth, small = joined(
+        exchange(first, 5), over_cores(first), small_step(6, *small_step(5, *small))
+    )
+    whole_rows = to_own(small[0].astype(F32))
+    gains, shifts = whole_rows[:4].reshape(2, 2, D), whole_rows[4:].reshape(2, 4, D)
+    whole_cols = small[1].astype(F32).reshape(4, 2, LAYERS, 12, 64)
+    vecs, qkv_shifts, up_shifts = [], [], []
     for l in range(LAYERS):
-        part0 = jnp.concatenate([w_qkv[:, l].reshape(64, 384), w_attn_out[:, l]], axis=1)
-        weights.append(gather([part0, w_up[:, l], w_down[:, l]]))
-
-    h = to_own(hidden_in)
-    dh = to_own(cotangent)
-    kept = []
-    for l in range(LAYERS):
-        vec = jnp.stack([gains[:, l, 0], shifts[:, l, 0], gains[:, l, 1], shifts[:, l, 1]]
-                        + [shifts[:, l, 2], shifts[:, l, 3]])
-        vec = jnp.pad(to_own(vec), ((0, 2), (0, 0)))
-        qv_own = jnp.einsum("st,tjk->sjk", col_hot, qv[l], precision=HIGH)
-        bias = jnp.concatenate(
-            [qv_own[:, 0], jnp.zeros((8, 128), F32), qv_own[:, 1]], axis=1
-        ).reshape(4, 2, 384)
-        up_own = jnp.dot(col_hot, ub[l], precision=HIGH).reshape(4, 2, 512)
-        mix, up, down = weights[l]
-        qkv, ctx, hm = attn_fwd(core, slopes, h, vec, bias, mix)
-        u, out = feed_fwd(core, slopes, hm, vec, up_own, up, down)
-        kept.append((h, vec, qkv, ctx, hm, u))
-        h = out
-    hidden_out = from_own(h)
-
-    shares, small_grads = [None] * LAYERS, [None] * LAYERS
-    for l in reversed(range(LAYERS)):
-        h, vec, qkv, ctx, hm, u = kept[l]
-        mix, up, down = weights[l]
-        outs = feed_bwd(core, slopes, dh, hm, vec, u, up, down)
-        gup, gdown, (dhm, gbu, gvec2) = unmerged(outs[:4]), unmerged(outs[4:8]), outs[8:]
-        outs = attn_bwd(core, slopes, dhm, h, vec, qkv, ctx, mix)
-        gmix, (dh, gqv, gvec1) = unmerged(outs[:4]), outs[4:]
-        shares[l] = [
-            scatter_one(g, o) for g, o in zip((gmix, gup, gdown), ORDERS)
-        ]
-        vectors = jnp.stack([gvec1[0], gvec2[0], gvec1[1], gvec2[1], gvec1[2], gvec2[2]])
-        columns = jnp.concatenate([gqv.reshape(8, 384), gbu.reshape(8, 512)], axis=1)
-        columns = lax.dot_general(
-            col_hot, columns, (((0,), (0,)), ((), ())), precision=HIGH
+        vecs.append(
+            jnp.concatenate(
+                [gains[l, 0:1], shifts[l, 0:1], gains[l, 1:2], shifts[l, 1:4], jnp.zeros((2, D), F32)]
+            )
         )
-        small_grads[l] = jnp.concatenate([from_own(vectors).reshape(-1), columns.reshape(-1)])
+        qv = whole_cols[:, :, l, :4].reshape(4, 2, 2, 128)
+        qkv_shifts.append(
+            jnp.concatenate([qv[:, :, 0], jnp.zeros((4, 2, 128), F32), qv[:, :, 1]], axis=2)
+        )
+        up_shifts.append(whole_cols[:, :, l, 4:].reshape(4, 2, 512))
+
+
+    mix_oth, recv = joined(swap(first_hi[0], "core"), exchange(second, 3))
+    second = doubled(second, recv)
+    mix0 = (first[0], first_hi[0], first_oth[0], mix_oth)
+    (qkv0, ctx0, hm0), rest_oth, recv = joined(
+        attn_fwd(core, slopes, h, vecs[0], qkv_shifts[0], mix0),
+        over_cores(first_hi[1:]),
+        exchange(second, 4),
+    )
+    second = doubled(second, recv)
+    up0, down0 = ((first[i], first_hi[i], first_oth[i], rest_oth[i - 1]) for i in (1, 2))
+    (u0, h1), second_hi, second_oth = joined(
+        feed_fwd(core, slopes, hm0, vecs[0], up_shifts[0], up0, down0),
+        exchange(second, 5),
+        over_cores(second),
+    )
+    h1, mix_oth, second_hi = joined(h1, swap(second_hi[0], "core"), second_hi)
+    mix1 = (second[0], second_hi[0], second_oth[0], mix_oth)
+    (qkv1, ctx1, hm1), rest_oth = joined(
+        attn_fwd(core, slopes, h1, vecs[1], qkv_shifts[1], mix1), over_cores(second_hi[1:])
+    )
+    up1, down1 = ((second[i], second_hi[i], second_oth[i], rest_oth[i - 1]) for i in (1, 2))
+    u1, out = feed_fwd(core, slopes, hm1, vecs[1], up_shifts[1], up1, down1)
+    hidden_out = from_own(out)
+
+    def feed_back(dh, hm, l, u, up, down):
+        outs = feed_bwd(core, slopes, dh, hm, vecs[l], u, up, down)
+        return unmerged(outs[:4]), unmerged(outs[4:8]), outs[8:]
+
+    def attn_back(dhm, h, l, qkv, ctx, mix):
+        outs = attn_bwd(core, slopes, dhm, h, vecs[l], qkv, ctx, mix)
+        return unmerged(outs[:4]), outs[4:]
+
+    def core_sum(grad, got):
+        return plus(grad[0], got[0]), plus(grad[1], got[1])
+
+    mix_order, up_order, down_order = ORDERS
+    gup1, gdown1, (dhm1, gbu1, gvec21) = feed_back(dh, hm1, 1, u1, up1, down1)
+    (gmix1, (dh, gqv1, gvec11)), up_got, down_got = joined(
+        attn_back(dhm1, h1, 1, qkv1, ctx1, mix1), over_cores(gup1[2:]), over_cores(gdown1[2:])
+    )
+    up_lo, up_hi = core_sum(gup1, up_got)
+    down_lo, down_hi = core_sum(gdown1, down_got)
+    (gup0, gdown0, (dhm0, gbu0, gvec20)), up1_s, down1_s, mix_got = joined(
+        feed_back(dh, hm0, 0, u0, up0, down0),
+        halved(up_lo, up_hi, up_order, 5),
+        halved(down_lo, down_hi, down_order, 5),
+        over_cores(gmix1[2:]),
+    )
+    mix_lo, mix_hi = core_sum(gmix1, mix_got)
+    (gmix0, (dh, gqv0, gvec10)), up1_s, down1_s, mix1_s, up_got, down_got = joined(
+        attn_back(dhm0, h, 0, qkv0, ctx0, mix0),
+        halved(*up1_s, up_order, 4),
+        halved(*down1_s, down_order, 4),
+        halved(mix_lo, mix_hi, mix_order, 5),
+        over_cores(gup0[2:]),
+        over_cores(gdown0[2:]),
+    )
+    lay1 = [halved(*mix1_s, mix_order, 4), up1_s, down1_s]
+    lay1 = [halved(*v, o, 3) for v, o in zip(lay1, ORDERS)]
+    lay0 = [
+        core_sum(gmix0, over_cores(gmix0[2:])),
+        core_sum(gup0, up_got),
+        core_sum(gdown0, down_got),
+    ]
+    lay0 = [halved(*v, o, 5) for v, o in zip(lay0, ORDERS)]
+    rows_back = [
+        jnp.concatenate([v1[0:1], v2[0:1], v1[1:2], v2[1:2], v1[2:3], v2[2:3]])
+        for v1, v2 in ((gvec10, gvec20), (gvec11, gvec21))
+    ]
+    cols_back = [
+        jnp.concatenate([gqv[:, :, :128], gqv[:, :, 256:], gbu], axis=2)
+        for gqv, gbu in ((gqv0, gbu0), (gqv1, gbu1))
+    ]
     grad_in = from_own(dh)
 
-    total = lax.psum(jnp.stack(small_grads), AXES)
-    p = (at["ylo"] * 4 + at["z"]) * 2 + at["core"]
-    t = at["x"] * 2 + at["yhi"]
-    vectors = total[:, : 6 * D].reshape(LAYERS, 6, 16, 64)
-    vectors = lax.dynamic_index_in_dim(vectors, p, 2, keepdims=False)
-    vectors = vectors.transpose(2, 0, 1)
-    columns = total[:, 6 * D :].reshape(LAYERS, 8, 896)
-    columns = lax.dynamic_index_in_dim(columns, t, 1, keepdims=False)
-    gqv = columns[:, :384].reshape(LAYERS, 3, 2, 16, 4)[:, 0::2]
-    gqv = lax.dynamic_index_in_dim(gqv, p, 3, keepdims=False).transpose(3, 0, 1, 2)
-    gbu = columns[:, 384:].reshape(LAYERS, 8, 16, 4)
-    gbu = lax.dynamic_index_in_dim(gbu, p, 2, keepdims=False).transpose(2, 0, 1)
-
-    mixes = jnp.stack([shares[l][0] for l in range(LAYERS)], axis=1)
+    rows_back, cols_back, up_s = joined(
+        jnp.concatenate(rows_back),
+        jnp.concatenate(cols_back, axis=2).reshape(2, 2, 2, LAYERS * 768),
+        lay0[1],
+    )
+    rows, cols = sum_small(rows_back, cols_back)
+    lay0 = [lay0[0], up_s, lay0[2]]
+    for n in (4, 3):
+        lay0 = [halved(*v, o, n) for v, o in zip(lay0, ORDERS)]
+    rows = rows.T.reshape(64, LAYERS, 6)
+    cols = lax.dot_general(
+        put_col.astype(F32), cols.reshape(24, 64), (((1,), (1,)), ((), ())), precision=HIGH
+    ).reshape(4, LAYERS, 12)
+    mixes, ups, downs = (
+        scatter_both([jnp.stack(lay0[i]), jnp.stack(lay1[i])], ORDERS[i]) for i in range(3)
+    )
     return (
         hidden_out,
         grad_in,
         mixes[:, :, :384].reshape(64, LAYERS, 3, 128),
         mixes[:, :, 384:],
-        jnp.stack([shares[l][1] for l in range(LAYERS)], axis=1),
-        jnp.stack([shares[l][2] for l in range(LAYERS)], axis=1),
-        gqv,
-        gbu,
-        vectors[:, :, :2],
-        vectors[:, :, 2:],
+        ups,
+        downs,
+        cols[:, :, :4].reshape(4, LAYERS, 2, 2),
+        cols[:, :, 4:],
+        rows[:, :, :2],
+        rows[:, :, 2:],
     )
 
 

time: 1010 us -> 564 us (0.56)
  blocking collectives: 347 us -> 0 us
  waiting for transfers between devices: 250 us -> 185 us
  local copies, waits for them, and re-layouts: 93.1 us -> 37.3 us
  other arithmetic: 50.5 us -> 105 us
  between operations: 16.2 us -> 2.75 us
  starting transfers between devices: 98.9 us -> 87.2 us
    all_gather x1 -> x0, blocking collectives: 347 us -> none  [shards(): lax.all_gather(small, AXES, axis=0, tiled=False).reshape(16, 8, 1024)]
    psum x1 -> x0, waiting for transfers between devices: 127 us -> none  [shards(): total = lax.psum(jnp.stack(small_grads), AXES)]
    slice x31 -> x38, local copies, waits for them, and re-layouts: 64.9 us -> 2.32 us  [the longest x1 0.75 us: shards(): cols[:, :, :4].reshape(4, LAYERS, 2, 2)]
    ppermute x96 -> x86, waiting for transfers between devices: 123 us -> 171 us  [swap(): return lax.ppermute(v, AXES, pairs(axis, step))]
    another operation x48 -> x34, other arithmetic: 15.1 us -> 44 us  [the longest x25 37.9 us: doubled(): return [jnp.stack([b, r]) for b, r in zip(bufs, recv)]]
    convert_element_type x36 -> x24, other arithmetic: 35.2 us -> 57.4 us  [plus(): return (a.astype(F32) + b.astype(F32)).astype(BF)]
    ppermute x96 -> x86, starting transfers between devices: 98.9 us -> 78.4 us  [swap(): return lax.ppermute(v, AXES, pairs(axis, step))]
    ppermute x0 -> x6, waiting for transfers between devices: none -> 13.7 us  [plain_swap(): return lax.ppermute(v, AXES, plain_pairs(axis, flip))]
  transfers between devices with their start and end apart: 97 -> 92, of which waited for: 27 -> 37; matrix products, arithmetic and copies ran while one was open for 15% -> 22% of each run, Pallas kernels for 3% -> 17%
where the time goes in v2:
time: 564 us; the launch traced here: 554 us
  waiting for transfers between devices  185 us (33%)
  Pallas kernels  124 us (22%)
  other arithmetic  105 us (19%)
  starting transfers between devices  87.2 us (15%)
  local copies, waits for them, and re-layouts  37.3 us (7%)
  matrix products  13.4 us (2%)
    ppermute x86, waiting for transfers between devices, swap(): return lax.ppermute(v, AXES, pairs(axis, step))  171 us
    pallas_call x8, Pallas kernels, call(): pl.pallas_call(body, name=name, out_shape=outs, grid_spec=pltpu.PrefetchS...  124 us
    ppermute x86, starting transfers between devices, swap(): return lax.ppermute(v, AXES, pairs(axis, step))  78.4 us
    convert_element_type x24, other arithmetic, plus(): return (a.astype(F32) + b.astype(F32)).astype(BF)  57.4 us
    another operation x25, other arithmetic, doubled(): return [jnp.stack([b, r]) for b, r in zip(bufs, recv)]  37.9 us
    unnamed x134, local copies, waits for them, and re-layouts  16.3 us
    ppermute x6, waiting for transfers between devices, plain_swap(): return lax.ppermute(v, AXES, plain_pairs(axis, flip))  13.7 us
    squeeze x12, local copies, waits for them, and re-layouts, halved(): return (s[0], s[1])  12.2 us
  transfers between devices with their start and end apart: 92, of which 37 were waited for; matrix products, arithmetic and copies ran while one was open for 22% of the time, Pallas kernels for 17%

profile of v2, /device:TPU:0, one launch (start us, length us, event | category | flops | bytes accessed | tf_op | source)
XLA Modules:
  0.0 554.1 jit_solution(11217273469488667181)
XLA Ops:
  12.6 3.8 collective-permute-done.3
  25.0 4.3 collective-permute-done.7
  69.5 11.7 %collective-permute-done.19 = bf16[2,24,64]{2,1,0:T(8,128)(2,1)S(1)} collective-permute-done((bf16[2,24,64]{2,1,0:T(8,128)(2,1)S(1)}, bf16[2,24,64]{2,1,0:T(8,128)(2,1)S(1)}, u32[]{:S(2)}, u32[]{:S(2)}) %collective-permute-start.19) | collective-permute-done | bytes 6176 | tf_op jit(solution)/shard_map/ppermute | solution.py:42
  90.8 20.2 %collective-permute-done.26 = bf16[2,2,24,64]{3,2,1,0:T(8,128)(2,1)S(1)} collective-permute-done((bf16[2,2,24,64]{3,2,1,0:T(8,128)(2,1)S(1)}, bf16[2,2,24,64]{3,2,1,0:T(8,128)(2,1)S(1)}, u32[]{:S(2)}, u32[]{:S(2)}) %collective-permute-start.26) | collective-permute-done | bytes 12320 | tf_op jit(solution)/shard_map/ppermute | solution.py:42
  117.5 23.4 %collective-permute-done.20 = bf16[2,2,2,2,2,64,512]{6,5,4,3,2,1,0:T(8,128)(2,1)} collective-permute-done((bf16[2,2,2,2,2,64,512]{6,5,4,3,2,1,0:T(8,128)(2,1)S(1)}, bf16[2,2,2,2,2,64,512]{6,5,4,3,2,1,0:T(8,128)(2,1)}, u32[]{:S(2)}, u32[]{:S(2)}) %collective-permute-start.20) | collective-permute-done | bytes 2097184 | tf_op jit(solution)/shard_map/ppermute | solution.py:42
  168.0 9.9 %attn_fwd.2 = (bf16[4,2,160,384]{3,2,1,0:T(8,128)(2,1)S(1)}, bf16[4,2,160,128]{3,2,1,0:T(8,128)(2,1)S(1)}, f32[160,1024]{1,0:T(8,128)S(1)}) custom-call(s32[1]{0:T(128)} %bitcast.core_ref, f32[16]{0:T(128)S(1)} %reshape.709.slope_ref, f32[160,1024]{1,0:T(8,128)S(1)} %fusion.16.h_ref, f32[8,1024]{1,0:T(8,128)S(1)} %concatenate.79.vec_ref, ...), custom_call_target="tpu_custom_call" | custom-call | tf_op jit(solution)/shard_map/attn_fwd/pallas_call | solution.py:278
  201.0 10.4 %feed_fwd.2 = (f32[4,2,160,512]{3,2,1,0:T(8,128)}, f32[160,1024]{1,0:T(8,128)S(1)}) custom-call(s32[1]{0:T(128)} %bitcast.core_ref, f32[16]{0:T(128)S(1)} %reshape.709.slope_ref, f32[160,1024]{1,0:T(8,128)S(1)} %copy-done.7, f32[8,1024]{1,0:T(8,128)S(1)} %concatenate.79.vec_ref, f32[4,2,512]{2,1,0:T(2,128)S(1)} %reshape_squeeze.28.bias_ref, ...), custom_call_target="tpu_custom_call" | custom-call | tf_op jit(solution)/shard_map/feed_fwd/pallas_call | solution.py:278
  212.9 5.0 collective-permute-done.39
  220.2 4.5 collective-permute-done.43
  234.3 10.0 %attn_fwd.3 = (bf16[4,2,160,384]{3,2,1,0:T(8,128)(2,1)S(1)}, bf16[4,2,160,128]{3,2,1,0:T(8,128)(2,1)S(1)}, f32[160,1024]{1,0:T(8,128)S(1)}) custom-call(s32[1]{0:T(128)} %bitcast.core_ref, f32[16]{0:T(128)S(1)} %reshape.709.slope_ref, f32[160,1024]{1,0:T(8,128)S(1)} %get-tuple-element.226.h_ref, f32[8,1024]{1,0:T(8,128)S(1)} %concatenate.81.vec_ref, ...), custom_call_target="tpu_custom_call" | custom-call | tf_op jit(solution)/shard_map/attn_fwd/pallas_call | solution.py:278
  244.3 10.5 %feed_fwd.3 = (f32[4,2,160,512]{3,2,1,0:T(8,128)}, f32[160,1024]{1,0:T(8,128)S(1)}) custom-call(s32[1]{0:T(128)} %bitcast.core_ref, f32[16]{0:T(128)S(1)} %reshape.709.slope_ref, f32[160,1024]{1,0:T(8,128)S(1)} %get-tuple-element.235.hm_ref, f32[8,1024]{1,0:T(8,128)S(1)} %concatenate.81.vec_ref, f32[4,2,512]{2,1,0:T(2,128)S(1)} %reshape_squeeze.30.bias_ref, ...), custom_call_target="tpu_custom_call" | custom-call | tf_op jit(solution)/shard_map/feed_fwd/pallas_call | solution.py:278
  254.8 19.6 %feed_bwd.2 = (bf16[2,4,4,64,512]{4,3,2,1,0:T(8,128)(2,1)S(1)}, bf16[2,4,4,64,512]{4,3,2,1,0:T(8,128)(2,1)}, bf16[2,4,4,64,512]{4,3,2,1,0:T(8,128)(2,1)}, bf16[2...) custom-call(s32[1]{0:T(128)} %bitcast.core_ref, ...), custom_call_target="tpu_custom_call" | custom-call | tf_op jit(solution)/shard_map/feed_bwd/pallas_call | solution.py:278
  275.7 21.7 %attn_bwd.2 = (bf16[8,4,64,512]{3,2,1,0:T(8,128)(2,1)S(1)}, bf16[8,4,64,512]{3,2,1,0:T(8,128)(2,1)}, bf16[8,4,64,512]{3,2,1,0:T(8,128)(2,1)}, bf16[8,4,64,512]{3...) custom-call(s32[1]{0:T(128)} %bitcast.core_ref, ...), custom_call_target="tpu_custom_call" | custom-call | tf_op jit(solution)/shard_map/attn_bwd/pallas_call | solution.py:278
  298.8 3.9 fusion.2
  303.9 3.9 fusion
  311.2 19.6 %feed_bwd.3 = (bf16[2,4,4,64,512]{4,3,2,1,0:T(8,128)(2,1)S(1)}, bf16[2,4,4,64,512]{4,3,2,1,0:T(8,128)(2,1)}, bf16[2,4,4,64,512]{4,3,2,1,0:T(8,128)(2,1)}, bf16[2...) custom-call(s32[1]{0:T(128)} %bitcast.core_ref, ...), custom_call_target="tpu_custom_call" | custom-call | tf_op jit(solution)/shard_map/feed_bwd/pallas_call | solution.py:278
  330.9 4.0 add_convert_fusion.13
  342.2 3.8 add_convert_fusion.10
  351.3 21.7 %attn_bwd.3 = (bf16[8,4,64,512]{3,2,1,0:T(8,128)(2,1)S(1)}, bf16[8,4,64,512]{3,2,1,0:T(8,128)(2,1)}, bf16[8,4,64,512]{3,2,1,0:T(8,128)(2,1)}, bf16[8,4,64,512]{3...) custom-call(s32[1]{0:T(128)} %bitcast.core_ref, ...), custom_call_target="tpu_custom_call" | custom-call | tf_op jit(solution)/shard_map/attn_bwd/pallas_call | solution.py:278
  383.7 4.3 add_convert_fusion.4
  396.4 4.6 add_convert_fusion.1
  405.4 10.1 %collective-permute-done.71 = bf16[2,2,2,2,2,64,512]{6,5,4,3,2,1,0:T(8,128)(2,1)} collective-permute-done((bf16[2,2,2,2,2,64,512]{6,5,4,3,2,1,0:T(8,128)(2,1)}, bf16[2,2,2,2,2,64,512]{6,5,4,3,2,1,0:T(8,128)(2,1)}, u32[]{:S(2)}, u32[]{:S(2)}) %collective-permute-start.71) | collective-permute-done | bytes 2097184 | tf_op jit(solution)/shard_map/ppermute | solution.py:42
  435.9 4.4 add_convert_fusion.7
  445.0 3.9 add_convert_fusion
  451.6 16.3 %collective-permute-done.90 = f32[24,128]{1,0:T(8,128)S(1)} collective-permute-done((f32[24,128]{1,0:T(8,128)S(1)}, f32[24,128]{1,0:T(8,128)S(1)}, u32[]{:S(2)}, u32[]{:S(2)}) %collective-permute-start.90) | collective-permute-done | bytes 12320 | tf_op jit(solution)/shard_map/ppermute | solution.py:42
  477.5 5.4 collective-permute-done.79
  497.7 14.3 %collective-permute-done.75 = bf16[2,2,2,64,512]{4,3,1,0,2:T(8,128)(2,1)} collective-permute-done((bf16[2,2,2,64,512]{4,3,1,0,2:T(8,128)(2,1)S(1)}, bf16[2,2,2,64,512]{4,3,1,0,2:T(8,128)(2,1)}, u32[]{:S(2)}, u32[]{:S(2)}) %collective-permute-start.75) | collective-permute-done | bytes 524320 | tf_op jit(solution)/shard_map/ppermute | solution.py:42
  519.9 8.2 %collective-permute-done.65 = bf16[2,2,2,64,512]{4,3,2,1,0:T(8,128)(2,1)S(1)} collective-permute-done((bf16[2,2,2,64,512]{4,3,2,1,0:T(8,128)(2,1)S(1)}, bf16[2,2,2,64,512]{4,3,2,1,0:T(8,128)(2,1)S(1)}, u32[]{:S(2)}, u32[]{:S(2)}) %collective-permute-start.65) | collective-permute-done | bytes 524320 | tf_op jit(solution)/shard_map/ppermute | solution.py:42
  528.4 5.3 collective-permute-done.76
  534.0 3.6 collective-permute-done.68
  541.1 5.7 %collective-permute-done.69 = bf16[2,2,64,512]{3,2,0,1:T(8,128)(2,1)S(1)} collective-permute-done((bf16[2,2,64,512]{3,2,0,1:T(8,128)(2,1)S(1)}, bf16[2,2,64,512]{3,2,0,1:T(8,128)(2,1)S(1)}, u32[]{:S(2)}, u32[]{:S(2)}) %collective-permute-start.69) | collective-permute-done | bytes 262176 | tf_op jit(solution)/shard_map/ppermute | solution.py:42
  548.0 4.0 collective-permute-done.70
  (523 shorter events, 249.2 us)
Async XLA Ops:
  83.3 30.3 %collective-permute-start.24 = (bf16[2,2,2,2,2,64,512]{6,5,4,3,2,1,0:T(8,128)(2,1)}, bf16[2,2,2,2,2,64,512]{6,5,4,3,2,1,0:T(8,128)(2,1)}, u32[]{:S(2)}, u32[]{:S(2)}) collective-permute-start(bf16[2,2,2,2,2,64,512]{6,5,4,3,2,1,0:T(8,128)(2,1)} %pad_maximum_fusion.1), channel_id=1, source_target_pairs={{0,8},{1,9},{2,10},{3,11},{4,12},{5,13},{6,14},{7,15},{8,0},{9,1},... | collective-permute-start | bytes 6291464 | tf_op jit(solution)/shard_map/ppermute | solution.py:42
  83.3 32.0 %collective-permute-start.21 = (bf16[2,2,2,2,2,64,512]{6,5,4,3,2,1,0:T(8,128)(2,1)}, bf16[2,2,2,2,2,64,512]{6,5,4,3,2,1,0:T(8,128)(2,1)}, u32[]{:S(2)}, u32[]{:S(2)}) collective-permute-start(bf16[2,2,2,2,2,64,512]{6,5,4,3,2,1,0:T(8,128)(2,1)} %pad_maximum_fusion.1), channel_id=1, source_target_pairs={{0,6},{1,7},{2,4},{3,5},{4,2},{5,3},{6,0},{7,1},{8,10},{9,11},{10,... | collective-permute-start | bytes 6291464 | tf_op jit(solution)/shard_map/ppermute | solution.py:42
  84.3 26.7 %collective-permute-start.26 = (bf16[2,2,24,64]{3,2,1,0:T(8,128)(2,1)S(1)}, bf16[2,2,24,64]{3,2,1,0:T(8,128)(2,1)S(1)}, u32[]{:S(2)}, u32[]{:S(2)}) collective-permute-start(bf16[2,2,24,64]{3,2,1,0:T(8,128)(2,1)S(1)} %pad_maximum_fusion.37), channel_id=1, source_target_pairs={{0,6},{1,7},{2,4},{3,5},{4,2},{5,3},{6,0},{7,1},{8,10},{9,11},{10,... | collective-permute-start | bytes 36872 | tf_op jit(solution)/shard_map/ppermute | solution.py:42
  88.0 27.3 %collective-permute-start.25 = (bf16[2,2,2,2,2,64,512]{6,5,4,3,2,1,0:T(8,128)(2,1)}, bf16[2,2,2,2,2,64,512]{6,5,4,3,2,1,0:T(8,128)(2,1)}, u32[]{:S(2)}, u32[]{:S(2)}) collective-permute-start(bf16[2,2,2,2,2,64,512]{6,5,4,3,2,1,0:T(8,128)(2,1)} %pad_maximum_fusion.2), channel_id=1, source_target_pairs={{0,8},{1,9},{2,10},{3,11},{4,12},{5,13},{6,14},{7,15},{8,0},{9,1},... | collective-permute-start | bytes 6291464 | tf_op jit(solution)/shard_map/ppermute | solution.py:42
  88.0 27.6 %collective-permute-start.22 = (bf16[2,2,2,2,2,64,512]{6,5,4,3,2,1,0:T(8,128)(2,1)}, bf16[2,2,2,2,2,64,512]{6,5,4,3,2,1,0:T(8,128)(2,1)}, u32[]{:S(2)}, u32[]{:S(2)}) collective-permute-start(bf16[2,2,2,2,2,64,512]{6,5,4,3,2,1,0:T(8,128)(2,1)} %pad_maximum_fusion.2), channel_id=1, source_target_pairs={{0,65},{1,64},{2,67},{3,66},{4,69},{5,68},{6,71},{7,70},{8,72},{9,... | collective-permute-start | bytes 6291464 | tf_op jit(solution)/shard_map/ppermute | solution.py:42
  113.5 27.4 %collective-permute-start.20 = (bf16[2,2,2,2,2,64,512]{6,5,4,3,2,1,0:T(8,128)(2,1)S(1)}, bf16[2,2,2,2,2,64,512]{6,5,4,3,2,1,0:T(8,128)(2,1)}, u32[]{:S(2)}, u32[]{:S(2)}) collective-permute-start(bf16[2,2,2,2,2,64,512]{6,5,4,3,2,1,0:T(8,128)(2,1)S(1)} %pad_maximum_fusion), channel_id=1, source_target_pairs={{0,48},{1,49},{2,50},{3,51},{4,52},{5,53},{6,54},{7,55},{8,24},{9,... | collective-permute-start | bytes 6291464 | tf_op jit(solution)/shard_map/ppermute | solution.py:42
  149.8 28.2 %collective-permute-start.32 = (bf16[2,2,2,2,2,64,512]{6,5,4,3,2,1,0:T(8,128)(2,1)}, bf16[2,2,2,2,2,64,512]{6,5,4,3,2,1,0:T(8,128)(2,1)}, u32[]{:S(2)}, u32[]{:S(2)}) collective-permute-start(bf16[2,2,2,2,2,64,512]{6,5,4,3,2,1,0:T(8,128)(2,1)} %collective-permute-done.21), channel_id=1, source_target_pairs={{0,8},{1,9},{2,10},{3,11},{4,12},{5,13},{6,14},{7,15},{8,0},{9,1},... | collective-permute-start | bytes 6291464 | tf_op jit(solution)/shard_map/ppermute | solution.py:42
  152.4 25.6 %collective-permute-start.33 = (bf16[2,2,2,2,2,64,512]{6,5,4,3,2,1,0:T(8,128)(2,1)}, bf16[2,2,2,2,2,64,512]{6,5,4,3,2,1,0:T(8,128)(2,1)}, u32[]{:S(2)}, u32[]{:S(2)}) collective-permute-start(bf16[2,2,2,2,2,64,512]{6,5,4,3,2,1,0:T(8,128)(2,1)} %collective-permute-done.22), channel_id=1, source_target_pairs={{0,8},{1,9},{2,10},{3,11},{4,12},{5,13},{6,14},{7,15},{8,0},{9,1},... | collective-permute-start | bytes 6291464 | tf_op jit(solution)/shard_map/ppermute | solution.py:42
  185.3 27.6 %collective-permute-start.38 = (bf16[2,2,2,2,2,64,512]{6,5,4,3,2,1,0:T(8,128)(2,1)}, bf16[2,2,2,2,2,64,512]{6,5,4,3,2,1,0:T(8,128)(2,1)}, u32[]{:S(2)}, u32[]{:S(2)}) collective-permute-start(bf16[2,2,2,2,2,64,512]{6,5,4,3,2,1,0:T(8,128)(2,1)} %pad_maximum_fusion.6), channel_id=1, source_target_pairs={{0,6},{1,7},{2,4},{3,5},{4,2},{5,3},{6,0},{7,1},{8,10},{9,11},{10,... | collective-permute-start | bytes 6291464 | tf_op jit(solution)/shard_map/ppermute | solution.py:42
  189.3 23.6 %collective-permute-start.42 = (bf16[2,2,2,2,2,64,512]{6,5,4,3,2,1,0:T(8,128)(2,1)}, bf16[2,2,2,2,2,64,512]{6,5,4,3,2,1,0:T(8,128)(2,1)}, u32[]{:S(2)}, u32[]{:S(2)}) collective-permute-start(bf16[2,2,2,2,2,64,512]{6,5,4,3,2,1,0:T(8,128)(2,1)} %pad_maximum_fusion.7), channel_id=1, source_target_pairs={{0,8},{1,9},{2,10},{3,11},{4,12},{5,13},{6,14},{7,15},{8,0},{9,1},... | collective-permute-start | bytes 6291464 | tf_op jit(solution)/shard_map/ppermute | solution.py:42
  190.3 27.6 %collective-permute-start.39 = (bf16[2,2,2,2,2,64,512]{6,5,4,3,2,1,0:T(8,128)(2,1)}, bf16[2,2,2,2,2,64,512]{6,5,4,3,2,1,0:T(8,128)(2,1)}, u32[]{:S(2)}, u32[]{:S(2)}) collective-permute-start(bf16[2,2,2,2,2,64,512]{6,5,4,3,2,1,0:T(8,128)(2,1)} %pad_maximum_fusion.7), channel_id=1, source_target_pairs={{0,65},{1,64},{2,67},{3,66},{4,69},{5,68},{6,71},{7,70},{8,72},{9,... | collective-permute-start | bytes 6291464 | tf_op jit(solution)/shard_map/ppermute | solution.py:42
  192.5 25.4 %collective-permute-start.40 = (bf16[2,2,2,2,2,64,512]{6,5,4,3,2,1,0:T(8,128)(2,1)S(1)}, bf16[2,2,2,2,2,64,512]{6,5,4,3,2,1,0:T(8,128)(2,1)}, u32[]{:S(2)}, u32[]{:S(2)}) collective-permute-start(bf16[2,2,2,2,2,64,512]{6,5,4,3,2,1,0:T(8,128)(2,1)S(1)} %pad_maximum_fusion.5), channel_id=1, source_target_pairs={{0,8},{1,9},{2,10},{3,11},{4,12},{5,13},{6,14},{7,15},{8,0},{9,1},... | collective-permute-start | bytes 6291464 | tf_op jit(solution)/shard_map/ppermute | solution.py:42
  192.6 27.4 %collective-permute-start.37 = (bf16[2,2,2,2,2,64,512]{6,5,4,3,2,1,0:T(8,128)(2,1)S(1)}, bf16[2,2,2,2,2,64,512]{6,5,4,3,2,1,0:T(8,128)(2,1)}, u32[]{:S(2)}, u32[]{:S(2)}) collective-permute-start(bf16[2,2,2,2,2,64,512]{6,5,4,3,2,1,0:T(8,128)(2,1)S(1)} %pad_maximum_fusion.5), channel_id=1, source_target_pairs={{0,48},{1,49},{2,50},{3,51},{4,52},{5,53},{6,54},{7,55},{8,24},{9,... | collective-permute-start | bytes 6291464 | tf_op jit(solution)/shard_map/ppermute | solution.py:42
  274.4 23.0 %collective-permute-start.46 = (bf16[2,2,2,2,2,64,512]{6,5,4,3,2,1,0:T(8,128)(2,1)}, bf16[2,2,2,2,2,64,512]{6,5,4,3,2,1,0:T(8,128)(2,1)}, u32[]{:S(2)}, u32[]{:S(2)}) collective-permute-start(bf16[2,2,2,2,2,64,512]{6,5,4,3,2,1,0:T(8,128)(2,1)} %bitcast.529), channel_id=1, source_target_pairs={{0,8},{1,9},{2,10},{3,11},{4,12},{5,13},{6,14},{7,15},{8,0},{9,1},... | collective-permute-start | bytes 6291464 | tf_op jit(solution)/shard_map/ppermute | solution.py:42
  302.7 28.2 %collective-permute-start.50 = (bf16[2,2,2,2,2,64,512]{6,5,4,3,2,1,0:T(8,128)(2,1)}, bf16[2,2,2,2,2,64,512]{6,5,4,3,2,1,0:T(8,128)(2,1)}, u32[]{:S(2)}, u32[]{:S(2)}) collective-permute-start(bf16[2,2,2,2,2,64,512]{6,5,4,3,2,1,0:T(8,128)(2,1)} %fusion.2), channel_id=1, source_target_pairs={{0,6},{1,7},{2,4},{3,5},{4,2},{5,3},{6,0},{7,1},{8,10},{9,11},{10,... | collective-permute-start | bytes 6291464 | tf_op jit(solution)/shard_map/ppermute | solution.py:42
  307.8 28.3 %collective-permute-start.51 = (bf16[2,2,2,2,2,64,512]{6,5,4,3,2,1,0:T(8,128)(2,1)}, bf16[2,2,2,2,2,64,512]{6,5,4,3,2,1,0:T(8,128)(2,1)}, u32[]{:S(2)}, u32[]{:S(2)}) collective-permute-start(bf16[2,2,2,2,2,64,512]{6,5,4,3,2,1,0:T(8,128)(2,1)} %fusion), channel_id=1, source_target_pairs={{0,65},{1,64},{2,67},{3,66},{4,69},{5,68},{6,71},{7,70},{8,72},{9,... | collective-permute-start | bytes 6291464 | tf_op jit(solution)/shard_map/ppermute | solution.py:42
  310.3 31.1 %collective-permute-start.52 = (bf16[2,2,2,2,2,64,512]{6,5,4,3,2,1,0:T(8,128)(2,1)}, bf16[2,2,2,2,2,64,512]{6,5,4,3,2,1,0:T(8,128)(2,1)}, u32[]{:S(2)}, u32[]{:S(2)}) collective-permute-start(bf16[2,2,2,2,2,64,512]{6,5,4,3,2,1,0:T(8,128)(2,1)} %bitcast.137), channel_id=1, source_target_pairs={{0,8},{1,9},{2,10},{3,11},{4,12},{5,13},{6,14},{7,15},{8,0},{9,1},... | collective-permute-start | bytes 6291464 | tf_op jit(solution)/shard_map/ppermute | solution.py:42
  310.3 31.1 %collective-permute-start.53 = (bf16[2,2,2,2,2,64,512]{6,5,4,3,2,1,0:T(8,128)(2,1)}, bf16[2,2,2,2,2,64,512]{6,5,4,3,2,1,0:T(8,128)(2,1)}, u32[]{:S(2)}, u32[]{:S(2)}) collective-permute-start(bf16[2,2,2,2,2,64,512]{6,5,4,3,2,1,0:T(8,128)(2,1)} %bitcast.138), channel_id=1, source_target_pairs={{0,8},{1,9},{2,10},{3,11},{4,12},{5,13},{6,14},{7,15},{8,0},{9,1},... | collective-permute-start | bytes 6291464 | tf_op jit(solution)/shard_map/ppermute | solution.py:42
  341.4 31.6 %collective-permute-start.54 = (bf16[2,2,2,2,64,512]{5,4,3,2,1,0:T(8,128)(2,1)}, bf16[2,2,2,2,64,512]{5,4,3,2,1,0:T(8,128)(2,1)S(1)}, u32[]{:S(2)}, u32[]{:S(2)}) collective-permute-start(bf16[2,2,2,2,64,512]{5,4,3,2,1,0:T(8,128)(2,1)} %get-tuple-element.290), channel_id=1, source_target_pairs={{0,2},{1,3},{2,0},{3,1},{4,6},{5,7},{6,4},{7,5},{8,14},{9,15},{10,... | collective-permute-start | bytes 3145736 | tf_op jit(solution)/shard_map/ppermute | solution.py:42
  342.2 31.8 %collective-permute-start.55 = (bf16[2,2,2,2,64,512]{5,4,3,2,1,0:T(8,128)(2,1)}, bf16[2,2,2,2,64,512]{5,4,3,2,1,0:T(8,128)(2,1)S(1)}, u32[]{:S(2)}, u32[]{:S(2)}) collective-permute-start(bf16[2,2,2,2,64,512]{5,4,3,2,1,0:T(8,128)(2,1)} %get-tuple-element.292), channel_id=1, source_target_pairs={{0,64},{1,65},{2,66},{3,67},{4,68},{5,69},{6,70},{7,71},{8,73},{9,... | collective-permute-start | bytes 3145736 | tf_op jit(solution)/shard_map/ppermute | solution.py:42
  346.0 32.0 %collective-permute-start.56 = (bf16[2,2,2,2,2,64,512]{6,5,4,3,2,1,0:T(8,128)(2,1)}, bf16[2,2,2,2,2,64,512]{6,5,4,3,2,1,0:T(8,128)(2,1)}, u32[]{:S(2)}, u32[]{:S(2)}) collective-permute-start(bf16[2,2,2,2,2,64,512]{6,5,4,3,2,1,0:T(8,128)(2,1)} %add_convert_fusion.10), channel_id=1, source_target_pairs={{0,48},{1,49},{2,50},{3,51},{4,52},{5,53},{6,54},{7,55},{8,24},{9,... | collective-permute-start | bytes 6291464 | tf_op jit(solution)/shard_map/ppermute | solution.py:42
  350.5 32.3 %collective-permute-start.57 = (bf16[2,2,2,2,2,64,512]{6,5,4,3,2,1,0:T(8,128)(2,1)}, bf16[2,2,2,2,2,64,512]{6,5,4,3,2,1,0:T(8,128)(2,1)}, u32[]{:S(2)}, u32[]{:S(2)}) collective-permute-start(bf16[2,2,2,2,2,64,512]{6,5,4,3,2,1,0:T(8,128)(2,1)} %bitcast.145), channel_id=1, source_target_pairs={{0,8},{1,9},{2,10},{3,11},{4,12},{5,13},{6,14},{7,15},{8,0},{9,1},... | collective-permute-start | bytes 6291464 | tf_op jit(solution)/shard_map/ppermute | solution.py:42
  350.7 32.1 %collective-permute-start.58 = (bf16[2,2,2,2,2,64,512]{6,5,4,3,2,1,0:T(8,128)(2,1)}, bf16[2,2,2,2,2,64,512]{6,5,4,3,2,1,0:T(8,128)(2,1)}, u32[]{:S(2)}, u32[]{:S(2)}) collective-permute-start(bf16[2,2,2,2,2,64,512]{6,5,4,3,2,1,0:T(8,128)(2,1)} %bitcast.146), channel_id=1, source_target_pairs={{0,8},{1,9},{2,10},{3,11},{4,12},{5,13},{6,14},{7,15},{8,0},{9,1},... | collective-permute-start | bytes 6291464 | tf_op jit(solution)/shard_map/ppermute | solution.py:42
  388.0 27.6 %collective-permute-start.71 = (bf16[2,2,2,2,2,64,512]{6,5,4,3,2,1,0:T(8,128)(2,1)}, bf16[2,2,2,2,2,64,512]{6,5,4,3,2,1,0:T(8,128)(2,1)}, u32[]{:S(2)}, u32[]{:S(2)}) collective-permute-start(bf16[2,2,2,2,2,64,512]{6,5,4,3,2,1,0:T(8,128)(2,1)} %add_convert_fusion.4), channel_id=1, source_target_pairs={{0,6},{1,7},{2,4},{3,5},{4,2},{5,3},{6,0},{7,1},{8,10},{9,11},{10,... | collective-permute-start | bytes 6291464 | tf_op jit(solution)/shard_map/ppermute | solution.py:42
  394.1 29.0 %collective-permute-start.81 = (bf16[2,2,2,64,512]{4,3,2,1,0:T(8,128)(2,1)}, bf16[2,2,2,64,512]{4,3,2,1,0:T(8,128)(2,1)}, u32[]{:S(2)}, u32[]{:S(2)}) collective-permute-start(bf16[2,2,2,64,512]{4,3,2,1,0:T(8,128)(2,1)} %get-tuple-element.329), channel_id=1, source_target_pairs={{0,6},{1,7},{2,4},{3,5},{4,2},{5,3},{6,0},{7,1},{8,10},{9,11},{10,... | collective-permute-start | bytes 1572872 | tf_op jit(solution)/shard_map/ppermute | solution.py:42
  395.6 30.3 %collective-permute-start.66 = (bf16[2,2,2,2,64,512]{5,4,3,2,1,0:T(8,128)(2,1)}, bf16[2,2,2,2,64,512]{5,4,3,2,1,0:T(8,128)(2,1)}, u32[]{:S(2)}, u32[]{:S(2)}) collective-permute-start(bf16[2,2,2,2,64,512]{5,4,3,2,1,0:T(8,128)(2,1)} %get-tuple-element.307), channel_id=1, source_target_pairs={{0,16},{1,17},{2,18},{3,19},{4,20},{5,21},{6,22},{7,23},{8,56},{9,... | collective-permute-start | bytes 3145736 | tf_op jit(solution)/shard_map/ppermute | solution.py:42
  396.3 90.6 %collective-permute-start.61 = (bf16[2,2,2,2,2,64,512]{6,5,4,3,2,1,0:T(8,128)(2,1)}, bf16[2,2,2,2,2,64,512]{6,5,4,3,2,1,0:T(8,128)(2,1)}, u32[]{:S(2)}, u32[]{:S(2)}) collective-permute-start(bf16[2,2,2,2,2,64,512]{6,5,4,3,2,1,0:T(8,128)(2,1)} %bitcast.161), channel_id=1, source_target_pairs={{0,8},{1,9},{2,10},{3,11},{4,12},{5,13},{6,14},{7,15},{8,0},{9,1},... | collective-permute-start | bytes 6291464 | tf_op jit(solution)/shard_map/ppermute | solution.py:42
  404.0 31.9 %collective-permute-start.62 = (bf16[2,2,2,2,2,64,512]{6,5,4,3,2,1,0:T(8,128)(2,1)}, bf16[2,2,2,2,2,64,512]{6,5,4,3,2,1,0:T(8,128)(2,1)}, u32[]{:S(2)}, u32[]{:S(2)}) collective-permute-start(bf16[2,2,2,2,2,64,512]{6,5,4,3,2,1,0:T(8,128)(2,1)} %bitcast.162), channel_id=1, source_target_pairs={{0,8},{1,9},{2,10},{3,11},{4,12},{5,13},{6,14},{7,15},{8,0},{9,1},... | collective-permute-start | bytes 6291464 | tf_op jit(solution)/shard_map/ppermute | solution.py:42
  415.5 27.9 %collective-permute-start.78 = (bf16[2,2,2,2,2,64,512]{6,5,4,3,2,1,0:T(8,128)(2,1)}, bf16[2,2,2,2,2,64,512]{6,5,4,3,2,1,0:T(8,128)(2,1)}, u32[]{:S(2)}, u32[]{:S(2)}) collective-permute-start(bf16[2,2,2,2,2,64,512]{6,5,4,3,2,1,0:T(8,128)(2,1)} %add_convert_fusion.1), channel_id=1, source_target_pairs={{0,65},{1,64},{2,67},{3,66},{4,69},{5,68},{6,71},{7,70},{8,72},{9,... | collective-permute-start | bytes 6291464 | tf_op jit(solution)/shard_map/ppermute | solution.py:42
  432.1 36.4 %collective-permute-start.67 = (bf16[2,2,2,64,512]{4,3,2,1,0:T(8,128)(2,1)}, bf16[2,2,2,64,512]{4,3,2,1,0:T(8,128)(2,1)}, u32[]{:S(2)}, u32[]{:S(2)}) collective-permute-start(bf16[2,2,2,64,512]{4,3,2,1,0:T(8,128)(2,1)} %slice_bitcast_fusion.16), channel_id=1, source_target_pairs={{0,65},{1,64},{2,67},{3,66},{4,69},{5,68},{6,71},{7,70},{8,72},{9,... | collective-permute-start | bytes 1572872 | tf_op jit(solution)/shard_map/ppermute | solution.py:42
  440.3 46.6 %collective-permute-start.63 = (bf16[2,2,2,2,2,64,512]{6,5,4,3,2,1,0:T(8,128)(2,1)}, bf16[2,2,2,2,2,64,512]{6,5,4,3,2,1,0:T(8,128)(2,1)}, u32[]{:S(2)}, u32[]{:S(2)}) collective-permute-start(bf16[2,2,2,2,2,64,512]{6,5,4,3,2,1,0:T(8,128)(2,1)} %add_convert_fusion.7), channel_id=1, source_target_pairs={{0,48},{1,49},{2,50},{3,51},{4,52},{5,53},{6,54},{7,55},{8,24},{9,... | collective-permute-start | bytes 6291464 | tf_op jit(solution)/shard_map/ppermute | solution.py:42
  441.8 31.8 %collective-permute-start.72 = (bf16[2,2,2,2,64,512]{5,4,3,2,1,0:T(8,128)(2,1)}, bf16[2,2,2,2,64,512]{5,4,3,2,1,0:T(8,128)(2,1)}, u32[]{:S(2)}, u32[]{:S(2)}) collective-permute-start(bf16[2,2,2,2,64,512]{5,4,3,2,1,0:T(8,128)(2,1)} %get-tuple-element.321), channel_id=1, source_target_pairs={{0,2},{1,3},{2,0},{3,1},{4,6},{5,7},{6,4},{7,5},{8,14},{9,15},{10,... | collective-permute-start | bytes 3145736 | tf_op jit(solution)/shard_map/ppermute | solution.py:42
  (120 other events, 1356.1 us)

commit v3 on v2

--- a/solution.py
+++ b/solution.py
@@ -69,11 +69,17 @@
 
 
 def doubled(bufs, recv):
-    return [jnp.stack([b, r]) for b, r in zip(bufs, recv)]
+    return [lax.optimization_barrier(jnp.stack([b, r])) for b, r in zip(bufs, recv)]
 
 
 def over_cores(values):
     return [swap(v, "core") for v in values]
+
+
+def over_cores_in_turn(values):
+    one, two = over_cores(values[:2])
+    one, last = joined(one, values[2])
+    return [one, two, swap(last, "core")]
 
 
 def small_step(n, rows, cols):
@@ -94,52 +100,41 @@
     return rows + r, cols + c.swapaxes(0, 1)
 
 
-def sum_small(rows, cols):
+def sum_small_step(n, rows, cols):
     def both(r, c, fn):
         rr, cc = r.reshape(-1, 128), c.reshape(-1, 128)
         got = fn(jnp.concatenate([rr, cc]))
         return got[: rr.shape[0]].reshape(r.shape), got[rr.shape[0] :].reshape(c.shape)
 
-    n = cols.shape[-1]
-    rows = rows.reshape(12, 2, 512)
-    r, c = both(rows[:, 1], cols, lambda v: swap(v, "core"))
-    rows, cols = rows[:, 0] + r, cols + c.swapaxes(0, 1)
-    for step in (2, 1):
-        r, c = both(rows, cols[1], lambda v: swap(v, "x", step))
-        rows, cols = rows + r, cols[0] + c
-    r, c = both(rows, cols[1], lambda v: plain_swap(v, "y", 2))
-    rows, cols = rows + r, cols[0] + c
-    rows = rows.reshape(12, 2, 256)
-    r, c = both(rows[:, 1], cols, lambda v: plain_swap(v, "y", 1))
-    rows, cols = rows[:, 0] + r, cols + c
-    for step in (2, 1):
-        rows = rows.reshape(12, 2, -1)
-        away = rows[:, 1]
-        width = away.shape[-1]
-        away = jnp.pad(away, ((0, 0), (0, 128 - width)))
+    if n == 0:
+        rows = rows.reshape(12, 2, 512)
+        r, c = both(rows[:, 1], cols, lambda v: swap(v, "core"))
+        return rows[:, 0] + r, cols + c.swapaxes(0, 1)
+    if n < 3:
+        step = 3 - n
+        rows = rows.reshape(12, 2, 2, -1)
+        away = rows[:, :, 1]
         r, c = both(away, cols, lambda v: swap(v, "z", step))
-        rows, cols = rows[:, 0] + r[:, :width], cols + c
-    return rows, cols
+        return (rows[:, :, 0] + r).reshape(12, -1), cols + c
+    if n == 3:
+        r, c = both(rows, cols[:, :, 1], lambda v: plain_swap(v, "y", 2))
+        return rows + r, cols[:, :, 0] + c
+    if n == 4:
+        rows = rows.reshape(12, 2, 64)
+        away = jnp.pad(rows[:, 1], ((0, 0), (0, 64)))
+        r, c = both(away, cols, lambda v: plain_swap(v, "y", 1))
+        return jnp.pad(rows[:, 0] + r[:, :64], ((0, 0), (0, 64))), cols + c
+    r, c = both(rows, cols[1], lambda v: swap(v, "x", 7 - n))
+    return rows + r, cols[0] + c
 
 
 def plus(a, b):
     return (a.astype(F32) + b.astype(F32)).astype(BF)
 
 
-def halved(lo, hi, order, n):
-    s = plus(lo, swap(hi, order[n // 2], n % 2 + 1))
-    return s[0], s[1]
-
-
-def scatter_both(sums, order):
-    s = jnp.stack(sums, axis=3)
-    for n in reversed(range(COMMON)):
-        lo, hi = s[0], s[1]
-        r = swap(hi, order[n // 2], n % 2 + 1)
-        if n:
-            s = plus(lo, r)
-        else:
-            return jnp.swapaxes(lo.astype(F32) + r.astype(F32), 0, 1)
+def halves(lo, recv):
+    hi = plus(lo[1], recv[1])
+    return plus(lo[0], recv[0]), hi
 
 
 def norm(h):
@@ -577,6 +572,25 @@
     own_rows = jnp.concatenate([ln_gain.reshape(64, 4), row_bias.reshape(64, 8)], axis=1)
     own_cols = jnp.concatenate([qv_bias.reshape(4, 2, 4), up_bias], axis=2).reshape(4, 24)
     small = (dot_tn(own_rows, put_row).astype(BF), dot_tn(own_cols, put_col).astype(BF))
+    def unpacked(small):
+        whole_rows = to_own(small[0].astype(F32))
+        gains, shifts = whole_rows[:4].reshape(2, 2, D), whole_rows[4:].reshape(2, 4, D)
+        whole_cols = small[1].astype(F32).reshape(4, 2, LAYERS, 12, 64)
+        vecs, qkv_shifts, up_shifts = [], [], []
+        for l in range(LAYERS):
+            vecs.append(
+                jnp.concatenate(
+                    [gains[l, 0:1], shifts[l, 0:1], gains[l, 1:2], shifts[l, 1:4]]
+                    + [jnp.zeros((2, D), F32)]
+                )
+            )
+            qv = whole_cols[:, :, l, :4].reshape(4, 2, 2, 128)
+            qkv_shifts.append(
+                jnp.concatenate([qv[:, :, 0], jnp.zeros((4, 2, 128), F32), qv[:, :, 1]], axis=2)
+            )
+            up_shifts.append(whole_cols[:, :, l, 4:].reshape(4, 2, 512))
+        return vecs, qkv_shifts, up_shifts
+
     h, dh = to_own(hidden_in), to_own(cotangent)
     bufs = joined(
         jnp.concatenate([w_qkv.reshape(64, LAYERS, 384), w_attn_out], axis=2).swapaxes(0, 1),
@@ -588,31 +602,17 @@
         bufs = doubled(bufs, recv)
     first, second = ([b[..., l, :, :] for b in bufs] for l in range(LAYERS))
 
-    for n in (3, 4):
-        recv, small = joined(exchange(first, n), small_step(n, *small))
-        first = doubled(first, recv)
-    first_hi, first_oth, small = joined(
-        exchange(first, 5), over_cores(first), small_step(6, *small_step(5, *small))
-    )
-    whole_rows = to_own(small[0].astype(F32))
-    gains, shifts = whole_rows[:4].reshape(2, 2, D), whole_rows[4:].reshape(2, 4, D)
-    whole_cols = small[1].astype(F32).reshape(4, 2, LAYERS, 12, 64)
-    vecs, qkv_shifts, up_shifts = [], [], []
-    for l in range(LAYERS):
-        vecs.append(
-            jnp.concatenate(
-                [gains[l, 0:1], shifts[l, 0:1], gains[l, 1:2], shifts[l, 1:4], jnp.zeros((2, D), F32)]
-            )
-        )
-        qv = whole_cols[:, :, l, :4].reshape(4, 2, 2, 128)
-        qkv_shifts.append(
-            jnp.concatenate([qv[:, :, 0], jnp.zeros((4, 2, 128), F32), qv[:, :, 1]], axis=2)
-        )
-        up_shifts.append(whole_cols[:, :, l, 4:].reshape(4, 2, 512))
-
-
-    mix_oth, recv = joined(swap(first_hi[0], "core"), exchange(second, 3))
+    recv, small = joined(exchange(first, 3), small_step(3, *small))
+    first = doubled(first, recv)
+    recv, small, h, dh = joined(exchange(first, 4), small_step(4, *small), h, dh)
+    first = doubled(first, recv)
+    first_hi, first_oth = joined(exchange(first, 5), over_cores_in_turn(first))
+
+    mix_oth, recv, small = joined(
+        swap(first_hi[0], "core"), exchange(second, 3), small_step(6, *small_step(5, *small))
+    )
     second = doubled(second, recv)
+    vecs, qkv_shifts, up_shifts = unpacked(small)
     mix0 = (first[0], first_hi[0], first_oth[0], mix_oth)
     (qkv0, ctx0, hm0), rest_oth, recv = joined(
         attn_fwd(core, slopes, h, vecs[0], qkv_shifts[0], mix0),
@@ -624,7 +624,7 @@
     (u0, h1), second_hi, second_oth = joined(
         feed_fwd(core, slopes, hm0, vecs[0], up_shifts[0], up0, down0),
         exchange(second, 5),
-        over_cores(second),
+        over_cores_in_turn(second),
     )
     h1, mix_oth, second_hi = joined(h1, swap(second_hi[0], "core"), second_hi)
     mix1 = (second[0], second_hi[0], second_oth[0], mix_oth)
@@ -633,7 +633,6 @@
     )
     up1, down1 = ((second[i], second_hi[i], second_oth[i], rest_oth[i - 1]) for i in (1, 2))
     u1, out = feed_fwd(core, slopes, hm1, vecs[1], up_shifts[1], up1, down1)
-    hidden_out = from_own(out)
 
     def feed_back(dh, hm, l, u, up, down):
         outs = feed_bwd(core, slopes, dh, hm, vecs[l], u, up, down)
@@ -643,65 +642,103 @@
         outs = attn_bwd(core, slopes, dhm, h, vecs[l], qkv, ctx, mix)
         return unmerged(outs[:4]), outs[4:]
 
-    def core_sum(grad, got):
-        return plus(grad[0], got[0]), plus(grad[1], got[1])
-
-    mix_order, up_order, down_order = ORDERS
+    def sent(part, hi, n):
+        return swap(hi, ORDERS[part][n // 2], n % 2 + 1)
+
+    def core_sums(grads, got):
+        return [plus(g, r) for g, r in zip(grads, got)]
+
     gup1, gdown1, (dhm1, gbu1, gvec21) = feed_back(dh, hm1, 1, u1, up1, down1)
     (gmix1, (dh, gqv1, gvec11)), up_got, down_got = joined(
         attn_back(dhm1, h1, 1, qkv1, ctx1, mix1), over_cores(gup1[2:]), over_cores(gdown1[2:])
     )
-    up_lo, up_hi = core_sum(gup1, up_got)
-    down_lo, down_hi = core_sum(gdown1, down_got)
-    (gup0, gdown0, (dhm0, gbu0, gvec20)), up1_s, down1_s, mix_got = joined(
-        feed_back(dh, hm0, 0, u0, up0, down0),
-        halved(up_lo, up_hi, up_order, 5),
-        halved(down_lo, down_hi, down_order, 5),
-        over_cores(gmix1[2:]),
-    )
-    mix_lo, mix_hi = core_sum(gmix1, mix_got)
-    (gmix0, (dh, gqv0, gvec10)), up1_s, down1_s, mix1_s, up_got, down_got = joined(
+    up1_lo, up1_hi = core_sums(gup1, up_got)
+    down1_lo, down1_hi = core_sums(gdown1, down_got)
+    up_got, down_got = sent(1, up1_hi, 5), sent(2, down1_hi, 5)
+    mix1_hi = plus(gmix1[1], swap(gmix1[3], "core"))
+    dh, mix1_hi, hm0, out = joined(dh, mix1_hi, hm0, out)
+    mix_got = sent(0, mix1_hi, 5)
+    mix1_lo = plus(gmix1[0], swap(gmix1[2], "core"))
+    (gup0, gdown0, (dhm0, gbu0, gvec20)), up_got, down_got, mix1_lo, hidden_out = joined(
+        feed_back(dh, hm0, 0, u0, up0, down0), up_got, down_got, mix1_lo, from_own(out)
+    )
+    up1_lo, up1_hi = halves(up1_lo, up_got)
+    down1_lo, down1_hi = halves(down1_lo, down_got)
+    up_got, down_got = sent(1, up1_hi, 4), sent(2, down1_hi, 4)
+    mix1_lo, mix1_hi = halves(mix1_lo, mix_got)
+    dhm0, mix1_hi = joined(dhm0, mix1_hi)
+    mix_got = sent(0, mix1_hi, 4)
+    (gmix0, (dh, gqv0, gvec10)), up_got, down_got, mix_got, up0_got, down0_got = joined(
         attn_back(dhm0, h, 0, qkv0, ctx0, mix0),
-        halved(*up1_s, up_order, 4),
-        halved(*down1_s, down_order, 4),
-        halved(mix_lo, mix_hi, mix_order, 5),
-        over_cores(gup0[2:]),
-        over_cores(gdown0[2:]),
-    )
-    lay1 = [halved(*mix1_s, mix_order, 4), up1_s, down1_s]
-    lay1 = [halved(*v, o, 3) for v, o in zip(lay1, ORDERS)]
-    lay0 = [
-        core_sum(gmix0, over_cores(gmix0[2:])),
-        core_sum(gup0, up_got),
-        core_sum(gdown0, down_got),
+        up_got,
+        down_got,
+        mix_got,
+        swap(gup0[3], "core"),
+        swap(gdown0[3], "core"),
+    )
+    lay1 = [
+        halves(lo, got)
+        for lo, got in ((mix1_lo, mix_got), (up1_lo, up_got), (down1_lo, down_got))
     ]
-    lay0 = [halved(*v, o, 5) for v, o in zip(lay0, ORDERS)]
-    rows_back = [
-        jnp.concatenate([v1[0:1], v2[0:1], v1[1:2], v2[1:2], v1[2:3], v2[2:3]])
-        for v1, v2 in ((gvec10, gvec20), (gvec11, gvec21))
+    up0_hi, down0_hi = plus(gup0[1], up0_got), plus(gdown0[1], down0_got)
+    rows = jnp.concatenate(
+        [
+            v
+            for v1, v2 in ((gvec10, gvec20), (gvec11, gvec21))
+            for v in (v1[0:1], v2[0:1], v1[1:2], v2[1:2], v1[2:3], v2[2:3])
+        ]
+    )
+    cols = jnp.concatenate(
+        [
+            v
+            for gqv, gbu in ((gqv0, gbu0), (gqv1, gbu1))
+            for v in (gqv[:, :, :128], gqv[:, :, 256:], gbu)
+        ],
+        axis=2,
+    ).reshape(2, 2, 2, LAYERS * 768)
+    mix0_got, got1, up0_hi, down0_hi, (rows, cols) = joined(
+        swap(gmix0[3], "core"),
+        [sent(i, lay1[i][1], 3) for i in range(3)],
+        up0_hi,
+        down0_hi,
+        sum_small_step(0, rows, cols),
+    )
+    up_got, down_got = sent(1, up0_hi, 5), sent(2, down0_hi, 5)
+    mix_got = sent(0, plus(gmix0[1], mix0_got), 5)
+    got, los, (rows, cols), grad_in, lay1 = joined(
+        [mix_got, up_got, down_got],
+        [plus(g[0], swap(g[2], "core")) for g in (gmix0, gup0, gdown0)],
+        sum_small_step(1, rows, cols),
+        from_own(dh),
+        [plus(s[0], g) for s, g in zip(lay1, got1)],
+    )
+    lay0 = [halves(lo, g) for lo, g in zip(los, got)]
+    got, (rows, cols) = joined(
+        [sent(i, lay0[i][1], 4) for i in range(3)], sum_small_step(2, rows, cols)
+    )
+    lay0 = [halves(s[0], g) for s, g in zip(lay0, got)]
+    got, (rows, cols) = joined(
+        [sent(i, lay0[i][1], 3) for i in range(3)], sum_small_step(3, rows, cols)
+    )
+    both = [
+        tuple(jnp.stack([plus(s[0][k], g[k]), s1[k]], axis=2) for k in (0, 1))
+        for s, g, s1 in zip(lay0, got, lay1)
     ]
-    cols_back = [
-        jnp.concatenate([gqv[:, :, :128], gqv[:, :, 256:], gbu], axis=2)
-        for gqv, gbu in ((gqv0, gbu0), (gqv1, gbu1))
-    ]
-    grad_in = from_own(dh)
-
-    rows_back, cols_back, up_s = joined(
-        jnp.concatenate(rows_back),
-        jnp.concatenate(cols_back, axis=2).reshape(2, 2, 2, LAYERS * 768),
-        lay0[1],
-    )
-    rows, cols = sum_small(rows_back, cols_back)
-    lay0 = [lay0[0], up_s, lay0[2]]
-    for n in (4, 3):
-        lay0 = [halved(*v, o, n) for v, o in zip(lay0, ORDERS)]
-    rows = rows.T.reshape(64, LAYERS, 6)
+    for n in (2, 1):
+        got, (rows, cols) = joined(
+            [sent(i, both[i][1], n) for i in range(3)], sum_small_step(6 - n, rows, cols)
+        )
+        both = [halves(s[0], g) for s, g in zip(both, got)]
+    got, (rows, cols) = joined(
+        [sent(i, both[i][1], 0) for i in range(3)], sum_small_step(6, rows, cols)
+    )
+    mixes, ups, downs = (
+        jnp.swapaxes(s[0].astype(F32) + g.astype(F32), 0, 1) for s, g in zip(both, got)
+    )
+    rows = rows[:, :64].T.reshape(64, LAYERS, 6)
     cols = lax.dot_general(
         put_col.astype(F32), cols.reshape(24, 64), (((1,), (1,)), ((), ())), precision=HIGH
     ).reshape(4, LAYERS, 12)
-    mixes, ups, downs = (
-        scatter_both([jnp.stack(lay0[i]), jnp.stack(lay1[i])], ORDERS[i]) for i in range(3)
-    )
     return (
         hidden_out,
         grad_in,

time: 564 us -> 526 us (0.933)
  waiting for transfers between devices: 185 us -> 136 us
  other arithmetic: 105 us -> 112 us
    ppermute x86, waiting for transfers between devices: 171 us -> 117 us  [swap(): return lax.ppermute(v, AXES, pairs(axis, step))]
    convert_element_type x24 -> x39, other arithmetic: 57.4 us -> 80.9 us  [plus(): return (a.astype(F32) + b.astype(F32)).astype(BF)]
    another operation x31 -> x24, other arithmetic: 44 us -> 26.6 us  [the longest x21 25.6 us: doubled(): jnp.stack([b, r])]
    squeeze x24 -> x4, local copies, waits for them, and re-layouts: 13.6 us -> 1.9 us  [the longest x1 0.61 us: unpacked(): shifts[l, 1:4]]
    another operation x6 -> x12, local copies, waits for them, and re-layouts: 0.34 us -> 7.36 us  [the longest x3 3.77 us: doubled(): jnp.stack([b, r])]
    unnamed x134 -> x168, local copies, waits for them, and re-layouts: 16.3 us -> 21.7 us
  transfers between devices with their start and end apart: 92 -> 92, of which waited for: 37 -> 36; matrix products, arithmetic and copies ran while one was open for 22% -> 25% of each run, Pallas kernels for 17% -> 18%
where the time goes in v3:
time: 526 us; the launch traced here: 517 us
  waiting for transfers between devices  136 us (26%)
  Pallas kernels  124 us (24%)
  other arithmetic  112 us (21%)
  starting transfers between devices  88.8 us (17%)
  local copies, waits for them, and re-layouts  40.4 us (8%)
  matrix products  13.4 us (3%)
    pallas_call x8, Pallas kernels, call(): pl.pallas_call(body, name=name, out_shape=outs, grid_spec=pltpu.PrefetchS...  124 us
    ppermute x86, waiting for transfers between devices, swap(): return lax.ppermute(v, AXES, pairs(axis, step))  117 us
    ppermute x86, starting transfers between devices, swap(): return lax.ppermute(v, AXES, pairs(axis, step))  83.2 us
    convert_element_type x39, other arithmetic, plus(): return (a.astype(F32) + b.astype(F32)).astype(BF)  80.9 us
    another operation x21, other arithmetic, doubled(): jnp.stack([b, r])  25.6 us
    unnamed x168, local copies, waits for them, and re-layouts  21.7 us
    ppermute x6, waiting for transfers between devices, plain_swap(): return lax.ppermute(v, AXES, plain_pairs(axis, flip))  18.8 us
  transfers between devices with their start and end apart: 92, of which 36 were waited for; matrix products, arithmetic and copies ran while one was open for 25% of the time, Pallas kernels for 18%

profile of v3, /device:TPU:0, one launch (start us, length us, event | category | flops | bytes accessed | tf_op | source)
XLA Modules:
  0.0 516.7 jit_solution(13573449111979894867)
XLA Ops:
  12.6 3.8 collective-permute-done.3
  25.2 4.0 collective-permute-done.7
  33.8 7.2 %collective-permute-done.11 = bf16[108,128]{1,0:T(8,128)(2,1)S(1)} collective-permute-done((bf16[108,128]{1,0:T(8,128)(2,1)S(1)}, bf16[108,128]{1,0:T(8,128)(2,1)S(1)}, u32[]{:S(2)}, u32[]{:S(2)}) %collective-permute-start.11) | collective-permute-done | bytes 27680 | tf_op jit(solution)/shard_map/ppermute | solution.py:57
  51.6 3.8 collective-permute-done.15
  73.7 6.4 %collective-permute-done.19 = bf16[2,24,64]{2,1,0:T(8,128)(2,1)S(1)} collective-permute-done((bf16[2,24,64]{2,1,0:T(8,128)(2,1)S(1)}, bf16[2,24,64]{2,1,0:T(8,128)(2,1)S(1)}, u32[]{:S(2)}, u32[]{:S(2)}) %collective-permute-start.19) | collective-permute-done | bytes 6176 | tf_op jit(solution)/shard_map/ppermute | solution.py:42
  84.9 4.3 collective-permute-start.20
  90.9 27.1 %collective-permute-done.22 = bf16[2,2,2,2,2,64,512]{6,5,4,3,2,1,0:T(8,128)(2,1)S(1)} collective-permute-done((bf16[2,2,2,2,2,64,512]{6,5,4,3,2,1,0:T(8,128)(2,1)S(1)}, bf16[2,2,2,2,2,64,512]{6,5,4,3,2,1,0:T(8,128)(2,1)S(1)}, u32[]{:S(2)}, u32[]{:S(2)}) %collective-permute-start.22) | collective-permute-done | bytes 2097184 | tf_op jit(solution)/shard_map/ppermute | solution.py:42
  129.5 6.4 %collective-permute-done.29 = bf16[2,2,2,64,512]{4,3,2,1,0:T(8,128)(2,1)} collective-permute-done((bf16[2,2,2,64,512]{4,3,2,1,0:T(8,128)(2,1)}, bf16[2,2,2,64,512]{4,3,2,1,0:T(8,128)(2,1)}, u32[]{:S(2)}, u32[]{:S(2)}) %collective-permute-start.29) | collective-permute-done | bytes 524320 | tf_op jit(solution)/shard_map/ppermute | solution.py:42
  147.9 9.9 %attn_fwd.2 = (bf16[4,2,160,384]{3,2,1,0:T(8,128)(2,1)S(1)}, bf16[4,2,160,128]{3,2,1,0:T(8,128)(2,1)S(1)}, f32[160,1024]{1,0:T(8,128)S(1)}) custom-call(s32[1]{0:T(128)} %bitcast.core_ref, f32[16]{0:T(128)S(1)} %reshape.1063.slope_ref, f32[160,1024]{1,0:T(8,128)S(1)} %fusion.14.h_ref, f32[8,1024]{1,0:T(8,128)S(1)} %concatenate.75.vec_ref, ...), custom_call_target="tpu_custom_call" | custom-call | tf_op jit(solution)/shard_map/attn_fwd/pallas_call | solution.py:273
  162.4 3.8 pad_maximum_fusion.4
  180.7 10.1 %feed_fwd.2 = (f32[4,2,160,512]{3,2,1,0:T(8,128)}, f32[160,1024]{1,0:T(8,128)S(1)}) custom-call(s32[1]{0:T(128)} %bitcast.core_ref, f32[16]{0:T(128)S(1)} %reshape.1063.slope_ref, f32[160,1024]{1,0:T(8,128)S(1)} %get-tuple-element.312.hm_ref, f32[8,1024]{1,0:T(8,128)S(1)} %concatenate.75.vec_ref, f32[4,2,512]{2,1,0:T(2,128)S(1)} %reshape_squeeze.31.bias_ref, ...), custom_call_target="tpu_custom_call" | custom-call | tf_op jit(solution)/shard_map/feed_fwd/pallas_call | solution.py:273
  191.6 11.1 %collective-permute-done.39 = bf16[2,2,2,2,2,64,512]{6,5,4,3,2,1,0:T(8,128)(2,1)} collective-permute-done((bf16[2,2,2,2,2,64,512]{6,5,4,3,2,1,0:T(8,128)(2,1)}, bf16[2,2,2,2,2,64,512]{6,5,4,3,2,1,0:T(8,128)(2,1)}, u32[]{:S(2)}, u32[]{:S(2)}) %collective-permute-start.39) | collective-permute-done | bytes 2097184 | tf_op jit(solution)/shard_map/ppermute | solution.py:42
  202.8 4.5 collective-permute-done.43
  209.1 9.9 %attn_fwd.3 = (bf16[4,2,160,384]{3,2,1,0:T(8,128)(2,1)S(1)}, bf16[4,2,160,128]{3,2,1,0:T(8,128)(2,1)S(1)}, f32[160,1024]{1,0:T(8,128)S(1)}) custom-call(s32[1]{0:T(128)} %bitcast.core_ref, f32[16]{0:T(128)S(1)} %reshape.1063.slope_ref, f32[160,1024]{1,0:T(8,128)S(1)} %copy-done.9, f32[8,1024]{1,0:T(8,128)S(1)} %concatenate.77.vec_ref, ...), custom_call_target="tpu_custom_call" | custom-call | tf_op jit(solution)/shard_map/attn_fwd/pallas_call | solution.py:273
  219.1 10.8 %feed_fwd.3 = (f32[4,2,160,512]{3,2,1,0:T(8,128)}, f32[160,1024]{1,0:T(8,128)S(1)}) custom-call(s32[1]{0:T(128)} %bitcast.core_ref, f32[16]{0:T(128)S(1)} %reshape.1063.slope_ref, f32[160,1024]{1,0:T(8,128)S(1)} %get-tuple-element.287.hm_ref, f32[8,1024]{1,0:T(8,128)S(1)} %concatenate.77.vec_ref, f32[4,2,512]{2,1,0:T(2,128)S(1)} %reshape_squeeze.33.bias_ref, ...), custom_call_target="tpu_custom_call" | custom-call | tf_op jit(solution)/shard_map/feed_fwd/pallas_call | solution.py:273
  229.9 19.5 %feed_bwd.2 = (bf16[2,4,4,64,512]{4,3,2,1,0:T(8,128)(2,1)S(1)}, bf16[2,4,4,64,512]{4,3,2,1,0:T(8,128)(2,1)}, bf16[2,4,4,64,512]{4,3,2,1,0:T(8,128)(2,1)}, bf16[2...) custom-call(s32[1]{0:T(128)} %bitcast.core_ref, ...), custom_call_target="tpu_custom_call" | custom-call | tf_op jit(solution)/shard_map/feed_bwd/pallas_call | solution.py:273
  250.8 21.8 %attn_bwd.2 = (bf16[8,4,64,512]{3,2,1,0:T(8,128)(2,1)S(1)}, bf16[8,4,64,512]{3,2,1,0:T(8,128)(2,1)}, bf16[8,4,64,512]{3,2,1,0:T(8,128)(2,1)}, bf16[8,4,64,512]{3...) custom-call(s32[1]{0:T(128)} %bitcast.core_ref, ...), custom_call_target="tpu_custom_call" | custom-call | tf_op jit(solution)/shard_map/attn_bwd/pallas_call | solution.py:273
  273.9 5.2 %fusion.3 = bf16[2,2,2,2,2,64,512]{6,5,4,3,2,1,0:T(8,128)(2,1)} fusion(bf16[2,2,2,2,2,64,512]{6,5,4,3,2,1,0:T(8,128)(2,1)} %bitcast.521, bf16[2,2,2,2,2,64,512]{6,5,4,3,2,1,0:T(8,128)(2,1)} %copy-done.49), kind=kLoop, calls=%fused_computation.7 | loop fusion | flops 4194304 | bytes 6291456 | tf_op jit(solution)/shard_map/convert_element_type | solution.py:132
  279.2 3.9 fusion.2
  289.8 19.6 %feed_bwd.3 = (bf16[2,4,4,64,512]{4,3,2,1,0:T(8,128)(2,1)S(1)}, bf16[2,4,4,64,512]{4,3,2,1,0:T(8,128)(2,1)}, bf16[2,4,4,64,512]{4,3,2,1,0:T(8,128)(2,1)}, bf16[2...) custom-call(s32[1]{0:T(128)} %bitcast.core_ref, ...), custom_call_target="tpu_custom_call" | custom-call | tf_op jit(solution)/shard_map/feed_bwd/pallas_call | solution.py:273
  317.4 3.8 add_convert_fusion.15
  323.4 3.8 add_convert_fusion.16
  329.2 21.8 %attn_bwd.3 = (bf16[8,4,64,512]{3,2,1,0:T(8,128)(2,1)S(1)}, bf16[8,4,64,512]{3,2,1,0:T(8,128)(2,1)}, bf16[8,4,64,512]{3,2,1,0:T(8,128)(2,1)}, bf16[8,4,64,512]{3...) custom-call(s32[1]{0:T(128)} %bitcast.core_ref, ...), custom_call_target="tpu_custom_call" | custom-call | tf_op jit(solution)/shard_map/attn_bwd/pallas_call | solution.py:273
  369.9 3.7 add_convert_fusion.4
  373.6 3.7 add_convert_fusion.5
  379.4 4.4 add_convert_fusion.3
  404.0 7.9 %collective-permute-done.71 = f32[120,128]{1,0:T(8,128)S(1)} collective-permute-done((f32[120,128]{1,0:T(8,128)S(1)}, f32[120,128]{1,0:T(8,128)S(1)}, u32[]{:S(2)}, u32[]{:S(2)}) %collective-permute-start.71) | collective-permute-done | bytes 61472 | tf_op jit(solution)/shard_map/ppermute | solution.py:42
  418.4 3.8 fusion.19
  437.3 5.2 %collective-permute-done.73 = bf16[2,2,2,2,64,512]{5,4,3,2,1,0:T(8,128)(2,1)} collective-permute-done((bf16[2,2,2,2,64,512]{5,4,3,2,1,0:T(8,128)(2,1)}, bf16[2,2,2,2,64,512]{5,4,3,2,1,0:T(8,128)(2,1)}, u32[]{:S(2)}, u32[]{:S(2)}) %collective-permute-start.73) | collective-permute-done | bytes 1048608 | tf_op jit(solution)/shard_map/ppermute | solution.py:42
  463.1 3.9 collective-permute-done.76
  478.1 4.1 collective-permute-done.81
  494.5 4.4 collective-permute-done.86
  (563 shorter events, 250.3 us)
Async XLA Ops:
  84.5 33.5 %collective-permute-start.24 = (bf16[2,2,2,2,2,64,512]{6,5,4,3,2,1,0:T(8,128)(2,1)S(1)}, bf16[2,2,2,2,2,64,512]{6,5,4,3,2,1,0:T(8,128)(2,1)S(1)}, u32[]{:S(2)}, u32[]{:S(2)}) collective-permute-start(bf16[2,2,2,2,2,64,512]{6,5,4,3,2,1,0:T(8,128)(2,1)S(1)} %pad_maximum_fusion.1), channel_id=1, source_target_pairs={{0,8},{1,9},{2,10},{3,11},{4,12},{5,13},{6,14},{7,15},{8,0},{9,1},... | collective-permute-start | bytes 6291464 | tf_op jit(solution)/shard_map/ppermute | solution.py:42
  84.6 33.5 %collective-permute-start.21 = (bf16[2,2,2,2,2,64,512]{6,5,4,3,2,1,0:T(8,128)(2,1)S(1)}, bf16[2,2,2,2,2,64,512]{6,5,4,3,2,1,0:T(8,128)(2,1)S(1)}, u32[]{:S(2)}, u32[]{:S(2)}) collective-permute-start(bf16[2,2,2,2,2,64,512]{6,5,4,3,2,1,0:T(8,128)(2,1)S(1)} %pad_maximum_fusion.1), channel_id=1, source_target_pairs={{0,6},{1,7},{2,4},{3,5},{4,2},{5,3},{6,0},{7,1},{8,10},{9,11},{10,... | collective-permute-start | bytes 6291464 | tf_op jit(solution)/shard_map/ppermute | solution.py:42
  84.9 33.1 %collective-permute-start.20 = (bf16[2,2,2,2,2,64,512]{6,5,4,3,2,1,0:T(8,128)(2,1)S(1)}, bf16[2,2,2,2,2,64,512]{6,5,4,3,2,1,0:T(8,128)(2,1)}, u32[]{:S(2)}, u32[]{:S(2)}) collective-permute-start(bf16[2,2,2,2,2,64,512]{6,5,4,3,2,1,0:T(8,128)(2,1)S(1)} %pad_maximum_fusion), channel_id=1, source_target_pairs={{0,48},{1,49},{2,50},{3,51},{4,52},{5,53},{6,54},{7,55},{8,24},{9,... | collective-permute-start | bytes 6291464 | tf_op jit(solution)/shard_map/ppermute | solution.py:42
  90.7 27.3 %collective-permute-start.22 = (bf16[2,2,2,2,2,64,512]{6,5,4,3,2,1,0:T(8,128)(2,1)S(1)}, bf16[2,2,2,2,2,64,512]{6,5,4,3,2,1,0:T(8,128)(2,1)S(1)}, u32[]{:S(2)}, u32[]{:S(2)}) collective-permute-start(bf16[2,2,2,2,2,64,512]{6,5,4,3,2,1,0:T(8,128)(2,1)S(1)} %pad_maximum_fusion.2), channel_id=1, source_target_pairs={{0,65},{1,64},{2,67},{3,66},{4,69},{5,68},{6,71},{7,70},{8,72},{9,... | collective-permute-start | bytes 6291464 | tf_op jit(solution)/shard_map/ppermute | solution.py:42
  90.8 28.6 %collective-permute-start.25 = (bf16[2,2,2,2,2,64,512]{6,5,4,3,2,1,0:T(8,128)(2,1)S(1)}, bf16[2,2,2,2,2,64,512]{6,5,4,3,2,1,0:T(8,128)(2,1)S(1)}, u32[]{:S(2)}, u32[]{:S(2)}) collective-permute-start(bf16[2,2,2,2,2,64,512]{6,5,4,3,2,1,0:T(8,128)(2,1)S(1)} %pad_maximum_fusion.2), channel_id=1, source_target_pairs={{0,8},{1,9},{2,10},{3,11},{4,12},{5,13},{6,14},{7,15},{8,0},{9,1},... | collective-permute-start | bytes 6291464 | tf_op jit(solution)/shard_map/ppermute | solution.py:42
  129.4 28.5 %collective-permute-start.32 = (bf16[2,2,2,2,2,64,512]{6,5,4,3,2,1,0:T(8,128)(2,1)}, bf16[2,2,2,2,2,64,512]{6,5,4,3,2,1,0:T(8,128)(2,1)}, u32[]{:S(2)}, u32[]{:S(2)}) collective-permute-start(bf16[2,2,2,2,2,64,512]{6,5,4,3,2,1,0:T(8,128)(2,1)} %copy-done.6), channel_id=1, source_target_pairs={{0,8},{1,9},{2,10},{3,11},{4,12},{5,13},{6,14},{7,15},{8,0},{9,1},... | collective-permute-start | bytes 6291464 | tf_op jit(solution)/shard_map/ppermute | solution.py:42
  136.0 21.9 %collective-permute-start.33 = (bf16[2,2,2,2,2,64,512]{6,5,4,3,2,1,0:T(8,128)(2,1)}, bf16[2,2,2,2,2,64,512]{6,5,4,3,2,1,0:T(8,128)(2,1)}, u32[]{:S(2)}, u32[]{:S(2)}) collective-permute-start(bf16[2,2,2,2,2,64,512]{6,5,4,3,2,1,0:T(8,128)(2,1)} %copy-done.25), channel_id=1, source_target_pairs={{0,8},{1,9},{2,10},{3,11},{4,12},{5,13},{6,14},{7,15},{8,0},{9,1},... | collective-permute-start | bytes 6291464 | tf_op jit(solution)/shard_map/ppermute | solution.py:42
  166.2 36.5 %collective-permute-start.41 = (bf16[2,2,2,2,2,64,512]{6,5,4,3,2,1,0:T(8,128)(2,1)}, bf16[2,2,2,2,2,64,512]{6,5,4,3,2,1,0:T(8,128)(2,1)}, u32[]{:S(2)}, u32[]{:S(2)}) collective-permute-start(bf16[2,2,2,2,2,64,512]{6,5,4,3,2,1,0:T(8,128)(2,1)} %pad_maximum_fusion.4), channel_id=1, source_target_pairs={{0,8},{1,9},{2,10},{3,11},{4,12},{5,13},{6,14},{7,15},{8,0},{9,1},... | collective-permute-start | bytes 6291464 | tf_op jit(solution)/shard_map/ppermute | solution.py:42
  166.3 36.4 %collective-permute-start.38 = (bf16[2,2,2,2,2,64,512]{6,5,4,3,2,1,0:T(8,128)(2,1)}, bf16[2,2,2,2,2,64,512]{6,5,4,3,2,1,0:T(8,128)(2,1)}, u32[]{:S(2)}, u32[]{:S(2)}) collective-permute-start(bf16[2,2,2,2,2,64,512]{6,5,4,3,2,1,0:T(8,128)(2,1)} %pad_maximum_fusion.4), channel_id=1, source_target_pairs={{0,6},{1,7},{2,4},{3,5},{4,2},{5,3},{6,0},{7,1},{8,10},{9,11},{10,... | collective-permute-start | bytes 6291464 | tf_op jit(solution)/shard_map/ppermute | solution.py:42
  169.6 33.2 %collective-permute-start.37 = (bf16[2,2,2,2,2,64,512]{6,5,4,3,2,1,0:T(8,128)(2,1)S(1)}, bf16[2,2,2,2,2,64,512]{6,5,4,3,2,1,0:T(8,128)(2,1)}, u32[]{:S(2)}, u32[]{:S(2)}) collective-permute-start(bf16[2,2,2,2,2,64,512]{6,5,4,3,2,1,0:T(8,128)(2,1)S(1)} %pad_maximum_fusion.3), channel_id=1, source_target_pairs={{0,48},{1,49},{2,50},{3,51},{4,52},{5,53},{6,54},{7,55},{8,24},{9,... | collective-permute-start | bytes 6291464 | tf_op jit(solution)/shard_map/ppermute | solution.py:42
  175.1 27.6 %collective-permute-start.39 = (bf16[2,2,2,2,2,64,512]{6,5,4,3,2,1,0:T(8,128)(2,1)}, bf16[2,2,2,2,2,64,512]{6,5,4,3,2,1,0:T(8,128)(2,1)}, u32[]{:S(2)}, u32[]{:S(2)}) collective-permute-start(bf16[2,2,2,2,2,64,512]{6,5,4,3,2,1,0:T(8,128)(2,1)} %pad_maximum_fusion.5), channel_id=1, source_target_pairs={{0,65},{1,64},{2,67},{3,66},{4,69},{5,68},{6,71},{7,70},{8,72},{9,... | collective-permute-start | bytes 6291464 | tf_op jit(solution)/shard_map/ppermute | solution.py:42
  176.0 26.8 %collective-permute-start.42 = (bf16[2,2,2,2,2,64,512]{6,5,4,3,2,1,0:T(8,128)(2,1)}, bf16[2,2,2,2,2,64,512]{6,5,4,3,2,1,0:T(8,128)(2,1)}, u32[]{:S(2)}, u32[]{:S(2)}) collective-permute-start(bf16[2,2,2,2,2,64,512]{6,5,4,3,2,1,0:T(8,128)(2,1)} %pad_maximum_fusion.5), channel_id=1, source_target_pairs={{0,8},{1,9},{2,10},{3,11},{4,12},{5,13},{6,14},{7,15},{8,0},{9,1},... | collective-permute-start | bytes 6291464 | tf_op jit(solution)/shard_map/ppermute | solution.py:42
  249.4 23.1 %collective-permute-start.46 = (bf16[2,2,2,2,2,64,512]{6,5,4,3,2,1,0:T(8,128)(2,1)}, bf16[2,2,2,2,2,64,512]{6,5,4,3,2,1,0:T(8,128)(2,1)S(1)}, u32[]{:S(2)}, u32[]{:S(2)}) collective-permute-start(bf16[2,2,2,2,2,64,512]{6,5,4,3,2,1,0:T(8,128)(2,1)} %bitcast.575), channel_id=1, source_target_pairs={{0,8},{1,9},{2,10},{3,11},{4,12},{5,13},{6,14},{7,15},{8,0},{9,1},... | collective-permute-start | bytes 6291464 | tf_op jit(solution)/shard_map/ppermute | solution.py:42
  249.9 22.7 %collective-permute-start.47 = (bf16[2,2,2,2,2,64,512]{6,5,4,3,2,1,0:T(8,128)(2,1)}, bf16[2,2,2,2,2,64,512]{6,5,4,3,2,1,0:T(8,128)(2,1)S(1)}, u32[]{:S(2)}, u32[]{:S(2)}) collective-permute-start(bf16[2,2,2,2,2,64,512]{6,5,4,3,2,1,0:T(8,128)(2,1)} %bitcast.574), channel_id=1, source_target_pairs={{0,8},{1,9},{2,10},{3,11},{4,12},{5,13},{6,14},{7,15},{8,0},{9,1},... | collective-permute-start | bytes 6291464 | tf_op jit(solution)/shard_map/ppermute | solution.py:42
  250.3 22.3 %collective-permute-start.48 = (bf16[2,2,2,2,2,64,512]{6,5,4,3,2,1,0:T(8,128)(2,1)}, bf16[2,2,2,2,2,64,512]{6,5,4,3,2,1,0:T(8,128)(2,1)S(1)}, u32[]{:S(2)}, u32[]{:S(2)}) collective-permute-start(bf16[2,2,2,2,2,64,512]{6,5,4,3,2,1,0:T(8,128)(2,1)} %bitcast.573), channel_id=1, source_target_pairs={{0,8},{1,9},{2,10},{3,11},{4,12},{5,13},{6,14},{7,15},{8,0},{9,1},... | collective-permute-start | bytes 6291464 | tf_op jit(solution)/shard_map/ppermute | solution.py:42
  250.4 22.2 %collective-permute-start.49 = (bf16[2,2,2,2,2,64,512]{6,5,4,3,2,1,0:T(8,128)(2,1)}, bf16[2,2,2,2,2,64,512]{6,5,4,3,2,1,0:T(8,128)(2,1)}, u32[]{:S(2)}, u32[]{:S(2)}) collective-permute-start(bf16[2,2,2,2,2,64,512]{6,5,4,3,2,1,0:T(8,128)(2,1)} %bitcast.572), channel_id=1, source_target_pairs={{0,8},{1,9},{2,10},{3,11},{4,12},{5,13},{6,14},{7,15},{8,0},{9,1},... | collective-permute-start | bytes 6291464 | tf_op jit(solution)/shard_map/ppermute | solution.py:42
  272.8 16.2 %collective-permute-start.53 = (bf16[2,2,2,2,2,64,512]{6,5,4,3,2,1,0:T(8,128)(2,1)}, bf16[2,2,2,2,2,64,512]{6,5,4,3,2,1,0:T(8,128)(2,1)S(1)}, u32[]{:S(2)}, u32[]{:S(2)}) collective-permute-start(bf16[2,2,2,2,2,64,512]{6,5,4,3,2,1,0:T(8,128)(2,1)} %bitcast.571), channel_id=1, source_target_pairs={{0,8},{1,9},{2,10},{3,11},{4,12},{5,13},{6,14},{7,15},{8,0},{9,1},... | collective-permute-start | bytes 6291464 | tf_op jit(solution)/shard_map/ppermute | solution.py:42
  279.1 32.9 %collective-permute-start.51 = (bf16[2,2,2,2,2,64,512]{6,5,4,3,2,1,0:T(8,128)(2,1)}, bf16[2,2,2,2,2,64,512]{6,5,4,3,2,1,0:T(8,128)(2,1)}, u32[]{:S(2)}, u32[]{:S(2)}) collective-permute-start(bf16[2,2,2,2,2,64,512]{6,5,4,3,2,1,0:T(8,128)(2,1)} %fusion.3), channel_id=1, source_target_pairs={{0,6},{1,7},{2,4},{3,5},{4,2},{5,3},{6,0},{7,1},{8,10},{9,11},{10,... | collective-permute-start | bytes 6291464 | tf_op jit(solution)/shard_map/ppermute | solution.py:42
  283.1 28.9 %collective-permute-start.52 = (bf16[2,2,2,2,2,64,512]{6,5,4,3,2,1,0:T(8,128)(2,1)}, bf16[2,2,2,2,2,64,512]{6,5,4,3,2,1,0:T(8,128)(2,1)S(1)}, u32[]{:S(2)}, u32[]{:S(2)}) collective-permute-start(bf16[2,2,2,2,2,64,512]{6,5,4,3,2,1,0:T(8,128)(2,1)} %fusion.2), channel_id=1, source_target_pairs={{0,65},{1,64},{2,67},{3,66},{4,69},{5,68},{6,71},{7,70},{8,72},{9,... | collective-permute-start | bytes 6291464 | tf_op jit(solution)/shard_map/ppermute | solution.py:42
  286.3 37.0 %collective-permute-start.54 = (bf16[2,2,2,2,2,64,512]{6,5,4,3,2,1,0:T(8,128)(2,1)}, bf16[2,2,2,2,2,64,512]{6,5,4,3,2,1,0:T(8,128)(2,1)}, u32[]{:S(2)}, u32[]{:S(2)}) collective-permute-start(bf16[2,2,2,2,2,64,512]{6,5,4,3,2,1,0:T(8,128)(2,1)} %add_convert_fusion.7), channel_id=1, source_target_pairs={{0,48},{1,49},{2,50},{3,51},{4,52},{5,53},{6,54},{7,55},{8,24},{9,... | collective-permute-start | bytes 6291464 | tf_op jit(solution)/shard_map/ppermute | solution.py:42
  316.8 39.5 %collective-permute-start.58 = (bf16[2,2,2,2,2,64,512]{6,5,4,3,2,1,0:T(8,128)(2,1)}, bf16[2,2,2,2,2,64,512]{6,5,4,3,2,1,0:T(8,128)(2,1)}, u32[]{:S(2)}, u32[]{:S(2)}) collective-permute-start(bf16[2,2,2,2,2,64,512]{6,5,4,3,2,1,0:T(8,128)(2,1)} %bitcast.142), channel_id=1, source_target_pairs={{0,8},{1,9},{2,10},{3,11},{4,12},{5,13},{6,14},{7,15},{8,0},{9,1},... | collective-permute-start | bytes 6291464 | tf_op jit(solution)/shard_map/ppermute | solution.py:42
  316.9 39.4 %collective-permute-start.59 = (bf16[2,2,2,2,2,64,512]{6,5,4,3,2,1,0:T(8,128)(2,1)}, bf16[2,2,2,2,2,64,512]{6,5,4,3,2,1,0:T(8,128)(2,1)}, u32[]{:S(2)}, u32[]{:S(2)}) collective-permute-start(bf16[2,2,2,2,2,64,512]{6,5,4,3,2,1,0:T(8,128)(2,1)} %bitcast.146), channel_id=1, source_target_pairs={{0,8},{1,9},{2,10},{3,11},{4,12},{5,13},{6,14},{7,15},{8,0},{9,1},... | collective-permute-start | bytes 6291464 | tf_op jit(solution)/shard_map/ppermute | solution.py:42
  323.3 33.0 %collective-permute-start.56 = (bf16[2,2,2,2,64,512]{5,4,3,2,1,0:T(8,128)(2,1)}, bf16[2,2,2,2,64,512]{5,4,3,2,1,0:T(8,128)(2,1)S(1)}, u32[]{:S(2)}, u32[]{:S(2)}) collective-permute-start(bf16[2,2,2,2,64,512]{5,4,3,2,1,0:T(8,128)(2,1)} %get-tuple-element.465), channel_id=1, source_target_pairs={{0,64},{1,65},{2,66},{3,67},{4,68},{5,69},{6,70},{7,71},{8,73},{9,... | collective-permute-start | bytes 3145736 | tf_op jit(solution)/shard_map/ppermute | solution.py:42
  327.2 29.1 %collective-permute-start.55 = (bf16[2,2,2,2,64,512]{5,4,3,2,1,0:T(8,128)(2,1)}, bf16[2,2,2,2,64,512]{5,4,3,2,1,0:T(8,128)(2,1)}, u32[]{:S(2)}, u32[]{:S(2)}) collective-permute-start(bf16[2,2,2,2,64,512]{5,4,3,2,1,0:T(8,128)(2,1)} %get-tuple-element.467), channel_id=1, source_target_pairs={{0,2},{1,3},{2,0},{3,1},{4,6},{5,7},{6,4},{7,5},{8,14},{9,15},{10,... | collective-permute-start | bytes 3145736 | tf_op jit(solution)/shard_map/ppermute | solution.py:42
  327.2 29.1 %collective-permute-start.57 = (bf16[2,2,2,2,64,512]{5,4,3,2,1,0:T(8,128)(2,1)}, bf16[2,2,2,2,64,512]{5,4,3,2,1,0:T(8,128)(2,1)S(1)}, u32[]{:S(2)}, u32[]{:S(2)}) collective-permute-start(bf16[2,2,2,2,64,512]{5,4,3,2,1,0:T(8,128)(2,1)} %get-tuple-element.352), channel_id=1, source_target_pairs={{0,16},{1,17},{2,18},{3,19},{4,20},{5,21},{6,22},{7,23},{8,56},{9,... | collective-permute-start | bytes 3145736 | tf_op jit(solution)/shard_map/ppermute | solution.py:42
  357.9 19.4 %collective-permute-start.64 = (f32[144,128]{1,0:T(8,128)S(1)}, f32[144,128]{1,0:T(8,128)S(1)}, u32[]{:S(2)}, u32[]{:S(2)}) collective-permute-start(f32[144,128]{1,0:T(8,128)S(1)} %pad_maximum_fusion.27), channel_id=1, source_target_pairs={{0,8},{1,9},{2,10},{3,11},{4,12},{5,13},{6,14},{7,15},{8,0},{9,1},... | collective-permute-start | bytes 221192 | tf_op jit(solution)/shard_map/ppermute | solution.py:42
  361.6 17.9 %collective-permute-start.60 = (bf16[2,2,2,2,2,64,512]{6,5,4,3,2,1,0:T(8,128)(2,1)}, bf16[2,2,2,2,2,64,512]{6,5,4,3,2,1,0:T(8,128)(2,1)}, u32[]{:S(2)}, u32[]{:S(2)}) collective-permute-start(bf16[2,2,2,2,2,64,512]{6,5,4,3,2,1,0:T(8,128)(2,1)} %bitcast.568), channel_id=1, source_target_pairs={{0,8},{1,9},{2,10},{3,11},{4,12},{5,13},{6,14},{7,15},{8,0},{9,1},... | collective-permute-start | bytes 6291464 | tf_op jit(solution)/shard_map/ppermute | solution.py:42
  377.3 20.8 %collective-permute-start.68 = (bf16[2,2,2,2,2,64,512]{6,5,4,3,2,1,0:T(8,128)(2,1)}, bf16[2,2,2,2,2,64,512]{6,5,4,3,2,1,0:T(8,128)(2,1)}, u32[]{:S(2)}, u32[]{:S(2)}) collective-permute-start(bf16[2,2,2,2,2,64,512]{6,5,4,3,2,1,0:T(8,128)(2,1)} %bitcast.152), channel_id=1, source_target_pairs={{0,8},{1,9},{2,10},{3,11},{4,12},{5,13},{6,14},{7,15},{8,0},{9,1},... | collective-permute-start | bytes 6291464 | tf_op jit(solution)/shard_map/ppermute | solution.py:42
  383.8 28.2 %collective-permute-start.65 = (bf16[2,2,2,2,2,64,512]{6,5,4,3,2,1,0:T(8,128)(2,1)}, bf16[2,2,2,2,2,64,512]{6,5,4,3,2,1,0:T(8,128)(2,1)}, u32[]{:S(2)}, u32[]{:S(2)}) collective-permute-start(bf16[2,2,2,2,2,64,512]{6,5,4,3,2,1,0:T(8,128)(2,1)} %add_convert_fusion.3), channel_id=1, source_target_pairs={{0,48},{1,49},{2,50},{3,51},{4,52},{5,53},{6,54},{7,55},{8,24},{9,... | collective-permute-start | bytes 6291464 | tf_op jit(solution)/shard_map/ppermute | solution.py:42
  385.2 27.6 %collective-permute-start.66 = (bf16[2,2,2,2,2,64,512]{6,5,4,3,2,1,0:T(8,128)(2,1)}, bf16[2,2,2,2,2,64,512]{6,5,4,3,2,1,0:T(8,128)(2,1)}, u32[]{:S(2)}, u32[]{:S(2)}) collective-permute-start(bf16[2,2,2,2,2,64,512]{6,5,4,3,2,1,0:T(8,128)(2,1)} %add_convert_fusion.5), channel_id=1, source_target_pairs={{0,6},{1,7},{2,4},{3,5},{4,2},{5,3},{6,0},{7,1},{8,10},{9,11},{10,... | collective-permute-start | bytes 6291464 | tf_op jit(solution)/shard_map/ppermute | solution.py:42
  387.9 27.8 %collective-permute-start.67 = (bf16[2,2,2,2,2,64,512]{6,5,4,3,2,1,0:T(8,128)(2,1)}, bf16[2,2,2,2,2,64,512]{6,5,4,3,2,1,0:T(8,128)(2,1)}, u32[]{:S(2)}, u32[]{:S(2)}) collective-permute-start(bf16[2,2,2,2,2,64,512]{6,5,4,3,2,1,0:T(8,128)(2,1)} %add_convert_fusion.4), channel_id=1, source_target_pairs={{0,65},{1,64},{2,67},{3,66},{4,69},{5,68},{6,71},{7,70},{8,72},{9,... | collective-permute-start | bytes 6291464 | tf_op jit(solution)/shard_map/ppermute | solution.py:42
  392.4 19.6 %collective-permute-start.71 = (f32[120,128]{1,0:T(8,128)S(1)}, f32[120,128]{1,0:T(8,128)S(1)}, u32[]{:S(2)}, u32[]{:S(2)}) collective-permute-start(f32[120,128]{1,0:T(8,128)S(1)} %pad_maximum_fusion.28), channel_id=1, source_target_pairs={{0,48},{1,49},{2,50},{3,51},{4,52},{5,53},{6,54},{7,55},{8,24},{9,... | collective-permute-start | bytes 184328 | tf_op jit(solution)/shard_map/ppermute | solution.py:42
  (136 other events, 1455.6 us)

commit v4 on v3

--- a/solution.py
+++ b/solution.py
@@ -16,6 +16,7 @@
 TENSOR = ("x", "yhi")
 ORDERS = ("xyz", "yzx", "zxy")
 LAYERS = 2
+COMMON = 3
 TOK = 160
 D = 1024
 HEADS = 16
@@ -42,24 +43,6 @@
     return lax.ppermute(v, AXES, pairs(axis, step))
 
 
-def plain_pairs(axis, flip):
-    out = []
-    for ylo, z, core, x, yhi in itertools.product(*map(range, SIZES)):
-        c = {"x": x, "y": 2 * yhi + ylo, "z": z, "core": core}
-        c[axis] ^= flip
-        src = np.ravel_multi_index((ylo, z, core, x, yhi), SIZES)
-        dst = np.ravel_multi_index((c["y"] & 1, c["z"], c["core"], c["x"], c["y"] >> 1), SIZES)
-        out.append((int(src), int(dst)))
-    return out
-
-
-def plain_swap(v, axis, flip):
-    return lax.ppermute(v, AXES, plain_pairs(axis, flip))
-
-
-COMMON = 3
-
-
 def joined(*values):
     return lax.optimization_barrier(values)
 
@@ -82,50 +65,8 @@
     return [one, two, swap(last, "core")]
 
 
-def small_step(n, rows, cols):
-    def both(r, c, fn):
-        flat = jnp.concatenate([r.reshape(96, 128), c.reshape(-1, 128)])
-        got = fn(flat)
-        return got[:96].reshape(12, 1024), got[96:].reshape(c.shape)
-
-    if n < 3:
-        axis, flip = (("z", 1), ("z", 2), ("y", 1))[n]
-        r, c = both(rows, cols, lambda v: plain_swap(v, axis, flip))
-        return rows + r, cols + c
-    if n == 3:
-        return rows, jnp.stack([cols, plain_swap(cols, "y", 2)])
-    if n < 6:
-        return rows, jnp.stack([cols, swap(cols, "x", n - 3)])
-    r, c = both(rows, cols, lambda v: swap(v, "core"))
-    return rows + r, cols + c.swapaxes(0, 1)
-
-
-def sum_small_step(n, rows, cols):
-    def both(r, c, fn):
-        rr, cc = r.reshape(-1, 128), c.reshape(-1, 128)
-        got = fn(jnp.concatenate([rr, cc]))
-        return got[: rr.shape[0]].reshape(r.shape), got[rr.shape[0] :].reshape(c.shape)
-
-    if n == 0:
-        rows = rows.reshape(12, 2, 512)
-        r, c = both(rows[:, 1], cols, lambda v: swap(v, "core"))
-        return rows[:, 0] + r, cols + c.swapaxes(0, 1)
-    if n < 3:
-        step = 3 - n
-        rows = rows.reshape(12, 2, 2, -1)
-        away = rows[:, :, 1]
-        r, c = both(away, cols, lambda v: swap(v, "z", step))
-        return (rows[:, :, 0] + r).reshape(12, -1), cols + c
-    if n == 3:
-        r, c = both(rows, cols[:, :, 1], lambda v: plain_swap(v, "y", 2))
-        return rows + r, cols[:, :, 0] + c
-    if n == 4:
-        rows = rows.reshape(12, 2, 64)
-        away = jnp.pad(rows[:, 1], ((0, 0), (0, 64)))
-        r, c = both(away, cols, lambda v: plain_swap(v, "y", 1))
-        return jnp.pad(rows[:, 0] + r[:, :64], ((0, 0), (0, 64))), cols + c
-    r, c = both(rows, cols[1], lambda v: swap(v, "x", 7 - n))
-    return rows + r, cols[0] + c
+def to_each(v):
+    return lax.all_to_all(v, AXES, 0, 0, tiled=True)
 
 
 def plus(a, b):
@@ -173,7 +114,7 @@
 
 def each_block(part, step, quad):
     a, b = step // 2, step % 2
-    for half in (0, 1):
+    for half in range(len(quad) // 2):
         lo, hi = quad[2 * half], quad[2 * half + 1]
         for (z2, z1), (y2, y1) in itertools.product(BITS, BITS):
             row = half * 8 + (y1 ^ y2) * 4 + z2 * 2 + z1
@@ -281,6 +222,7 @@
             out_specs=out_specs,
             scratch_shapes=scratch,
         ),
+        cost_estimate=pl.CostEstimate(flops=1 << 20, transcendentals=0, bytes_accessed=1 << 18),
         compiler_params=pltpu.CompilerParams(
             dimension_semantics=("arbitrary",), vmem_limit_bytes=48 << 20
         ),
@@ -399,22 +341,28 @@
     return jnp.sum(x, axis=0, keepdims=True)
 
 
+def keep_halves(own_ref, oth_ref, i, x):
+    own_ref[i] = x[:, :512]
+    oth_ref[i] = x[:, 512:]
+
+
 def feed_bwd_body(core_ref, slope_ref, dh_ref, hm_ref, vec_ref, u_ref, *rest):
     up, down = rest[:4], rest[4:8]
-    gup, gdown, (dhm_ref, gbu_ref, gvec_ref) = rest[8:12], rest[12:16], rest[16:19]
-    wu_ref, wd_ref, gu_ref, gd_ref, mt_ref, dyt_ref, dm_ref = rest[19:]
+    dhm_ref, gbu_ref, gvec_ref, ad_ref, own_ref, oth_ref = rest[8:14]
+    wu_ref, wd_ref, dm_ref = rest[14:]
     s, core = pl.program_id(0), core_ref[0]
+    dy = dh_ref[...].astype(BF)
 
     @pl.when(s == 0)
     def _():
         n, _ = norm(hm_ref[...])
-        mt_ref[...] = turned((n * vec_ref[2:3, :] + vec_ref[3:4, :]).astype(BF))
-        dyt_ref[...] = turned(dh_ref[...].astype(BF))
+        m = (n * vec_ref[2:3, :] + vec_ref[3:4, :]).astype(BF)
+        keep_halves(own_ref, oth_ref, 0, m)
+        keep_halves(own_ref, oth_ref, 1, dy)
         dm_ref[...] = jnp.zeros((TOK, D), F32)
 
     assemble(1, s, core, up, wu_ref)
     assemble(2, s, core, down, wd_ref)
-    dy = dh_ref[...].astype(BF)
     total = jnp.zeros((TOK, D), F32)
     for g in (0, 1):
         u = u_ref[0, g]
@@ -423,12 +371,10 @@
         du = dot(dy, wd_ref[g]) * slope
         gbu_ref[0, g : g + 1, :] = col_sum(du)
         dub = du.astype(BF)
-        gd_ref[g] = dot(dyt_ref[...], act.astype(BF)).astype(BF)
-        gu_ref[g] = dot(mt_ref[...], dub).astype(BF)
+        ad_ref[0, g, 0] = dub
+        ad_ref[0, g, 1] = act.astype(BF)
         total = total + dot_nt(dub, wu_ref[g])
     dm_ref[...] += total
-    disassemble(1, s, core, gup, gu_ref)
-    disassemble(2, s, core, gdown, gd_ref)
 
     @pl.when(s == 3)
     def _():
@@ -442,7 +388,7 @@
 
 
 def feed_bwd(core, slopes, dh, hm, vec, u, up, down):
-    wide = pltpu.VMEM((2, D, 512), BF)
+    half = (2, TOK, 512)
     return call(
         feed_bwd_body,
         "feed_bwd",
@@ -452,32 +398,33 @@
         [whole((TOK, D)), whole((TOK, D)), whole((8, D)), per_step((4, 2, TOK, 512))]
         + quad_specs(1)
         + quad_specs(2),
-        quad_shapes(1) + quad_shapes(2) + [sds((TOK, D)), sds((4, 2, 512)), sds((8, D))],
-        quad_specs(1) + quad_specs(2) + [whole((TOK, D)), per_step((4, 2, 512)), whole((8, D))],
-        [wide] * 4
-        + [pltpu.VMEM((D, TOK), BF), pltpu.VMEM((D, TOK), BF), pltpu.VMEM((TOK, D), F32)],
+        [sds((TOK, D)), sds((4, 2, 512)), sds((8, D)), sds((4, 2, 2, TOK, 512), BF)]
+        + [sds(half, BF)] * 2,
+        [whole((TOK, D)), per_step((4, 2, 512)), whole((8, D)), per_step((4, 2, 2, TOK, 512))]
+        + [whole(half)] * 2,
+        [pltpu.VMEM((2, D, 512), BF)] * 2 + [pltpu.VMEM((TOK, D), F32)],
     )
 
 
 def attn_bwd_body(core_ref, slope_ref, dhm_ref, h_ref, vec_ref, qkv_ref, ctx_ref, *rest):
-    quad, gquad, (dh_ref, gqv_ref, gvec_ref) = rest[:4], rest[4:8], rest[8:11]
-    w_ref, gw_ref, at_ref, dzt_ref, da_ref = rest[11:]
+    quad, (dh_ref, gqv_ref, gvec_ref, dc_ref, own_ref, oth_ref) = rest[:4], rest[4:10]
+    w_ref, da_ref = rest[10:]
     s, core = pl.program_id(0), core_ref[0]
+    dz = dhm_ref[...].astype(BF)
 
     @pl.when(s == 0)
     def _():
         n, _ = norm(h_ref[...])
-        at_ref[...] = turned((n * vec_ref[0:1, :] + vec_ref[1:2, :]).astype(BF))
-        dzt_ref[...] = turned(dhm_ref[...].astype(BF))
+        a = (n * vec_ref[0:1, :] + vec_ref[1:2, :]).astype(BF)
+        keep_halves(own_ref, oth_ref, 0, a)
+        keep_halves(own_ref, oth_ref, 1, dz)
         da_ref[...] = jnp.zeros((TOK, D), F32)
 
     assemble(0, s, core, quad, w_ref)
-    dz = dhm_ref[...].astype(BF)
     total = jnp.zeros((TOK, D), F32)
     for g in (0, 1):
         qkv = qkv_ref[0, g]
         dctx = dot(dz, w_ref[g, :, 384:512]).astype(BF)
-        gw_ref[g, :, 384:512] = dot(dzt_ref[...], ctx_ref[0, g]).astype(BF)
         grads = [[], [], []]
         for hd in (0, 1):
             q, k, v = (qkv[:, j * 128 + hd * 64 : j * 128 + hd * 64 + 64] for j in range(3))
@@ -492,10 +439,10 @@
         dqkv = jnp.concatenate([g_ for three in grads for g_ in three], axis=1)
         gqv_ref[0, g : g + 1, :] = col_sum(dqkv)
         dqkv = dqkv.astype(BF)
-        gw_ref[g, :, 0:384] = dot(at_ref[...], dqkv).astype(BF)
+        dc_ref[0, g, :, 0:384] = dqkv
+        dc_ref[0, g, :, 384:512] = ctx_ref[0, g]
         total = total + dot_nt(dqkv, w_ref[g, :, 0:384])
     da_ref[...] += total
-    disassemble(0, s, core, gquad, gw_ref)
 
     @pl.when(s == 3)
     def _():
@@ -509,7 +456,7 @@
 
 
 def attn_bwd(core, slopes, dhm, h, vec, qkv, ctx, quad):
-    wide = pltpu.VMEM((2, D, 512), BF)
+    half = (2, TOK, 512)
     return call(
         attn_bwd_body,
         "attn_bwd",
@@ -524,11 +471,67 @@
             per_step((4, 2, TOK, 128)),
         ]
         + quad_specs(0),
-        quad_shapes(0) + [sds((TOK, D)), sds((4, 2, 384)), sds((8, D))],
-        quad_specs(0) + [whole((TOK, D)), per_step((4, 2, 384)), whole((8, D))],
-        [wide] * 2
-        + [pltpu.VMEM((D, TOK), BF), pltpu.VMEM((D, TOK), BF), pltpu.VMEM((TOK, D), F32)],
-    )
+        [sds((TOK, D)), sds((4, 2, 384)), sds((8, D)), sds((4, 2, TOK, 512), BF)]
+        + [sds(half, BF)] * 2,
+        [whole((TOK, D)), per_step((4, 2, 384)), whole((8, D)), per_step((4, 2, TOK, 512))]
+        + [whole(half)] * 2,
+        [pltpu.VMEM((2, D, 512), BF), pltpu.VMEM((TOK, D), F32)],
+    )
+
+
+def both_tokens(mine, theirs):
+    return turned(jnp.concatenate([mine, theirs], axis=0))
+
+
+def feed_grad_body(core_ref, slope_ref, ad_ref, ad2_ref, own_ref, own2_ref, *rest):
+    gup, gdown, (mt_ref, dyt_ref, gu_ref, gd_ref) = rest[:2], rest[2:4], rest[4:]
+    s, core = pl.program_id(0), core_ref[0]
+
+    @pl.when(s == 0)
+    def _():
+        mt_ref[...] = both_tokens(own_ref[0], own2_ref[0])
+        dyt_ref[...] = both_tokens(own_ref[1], own2_ref[1])
+
+    for g in (0, 1):
+        du = jnp.concatenate([ad_ref[0, g, 0], ad2_ref[0, g, 0]], axis=0)
+        act = jnp.concatenate([ad_ref[0, g, 1], ad2_ref[0, g, 1]], axis=0)
+        gu_ref[g] = dot(mt_ref[...], du).astype(BF)
+        gd_ref[g] = dot(dyt_ref[...], act).astype(BF)
+    disassemble(1, s, core, gup, gu_ref)
+    disassemble(2, s, core, gdown, gd_ref)
+
+
+def attn_grad_body(core_ref, slope_ref, dc_ref, dc2_ref, own_ref, own2_ref, *rest):
+    gmix, (at_ref, dzt_ref, gw_ref) = rest[:2], rest[2:]
+    s, core = pl.program_id(0), core_ref[0]
+
+    @pl.when(s == 0)
+    def _():
+        at_ref[...] = both_tokens(own_ref[0], own2_ref[0])
+        dzt_ref[...] = both_tokens(own_ref[1], own2_ref[1])
+
+    for g in (0, 1):
+        dc = jnp.concatenate([dc_ref[0, g], dc2_ref[0, g]], axis=0)
+        gw_ref[g, :, 0:384] = dot(at_ref[...], dc[:, 0:384]).astype(BF)
+        gw_ref[g, :, 384:512] = dot(dzt_ref[...], dc[:, 384:512]).astype(BF)
+    disassemble(0, s, core, gmix, gw_ref)
+
+
+def weight_grads(body, name, parts, core, slopes, cols, cols2, rows, rows2):
+    zeros = (0,) * (cols.ndim - 1)
+    crossed = pl.BlockSpec((1, *cols.shape[1:]), lambda s, *_: ((s % 2) * 2 + s // 2, *zeros))
+    outs = call(
+        body,
+        name,
+        core,
+        slopes,
+        (cols, cols2, rows, rows2),
+        [per_step(cols.shape), crossed, whole(rows.shape), whole(rows.shape)],
+        [v for part in parts for v in quad_shapes(part)[:2]],
+        [v for part in parts for v in quad_specs(part)[:2]],
+        [pltpu.VMEM((512, 2 * TOK), BF)] * 2 + [pltpu.VMEM((2, 512, 512), BF)] * len(parts),
+    )
+    return [unmerged(outs[2 * i : 2 * i + 2]) for i in range(len(parts))]
 
 
 def orders():
@@ -567,15 +570,23 @@
     slopes = jnp.exp2(-8.0 * (heads.astype(F32) + 1.0) / HEADS).reshape(-1)
 
     p = (at["ylo"] * 4 + at["z"]) * 2 + at["core"]
-    put_row = (jnp.arange(D)[None, :] == p * 64 + jnp.arange(64)[:, None]).astype(BF)
-    put_col = (jnp.arange(64)[None, :] == p * 4 + jnp.arange(4)[:, None]).astype(BF)
+    col_hot = one_hot(cols, 8)
     own_rows = jnp.concatenate([ln_gain.reshape(64, 4), row_bias.reshape(64, 8)], axis=1)
     own_cols = jnp.concatenate([qv_bias.reshape(4, 2, 4), up_bias], axis=2).reshape(4, 24)
-    small = (dot_tn(own_rows, put_row).astype(BF), dot_tn(own_cols, put_col).astype(BF))
+    small = jnp.concatenate([own_rows.T.reshape(-1), own_cols.T.reshape(-1)])
+    small = jnp.pad(small, (0, 160)).reshape(8, 128)
+    at_row = jnp.arange(1536)
+    moved = (at_row % 96) // 4 * 64 + at_row // 96 * 4 + at_row % 4
+    move = (moved[:, None] == at_row[None, :]).astype(BF)
+
     def unpacked(small):
-        whole_rows = to_own(small[0].astype(F32))
+        small = small.reshape(16, 8, 8, 128)
+        whole_rows = small[:, 0, :6].reshape(16, 12, 64).swapaxes(0, 1).reshape(12, D)
+        whole_rows = to_own(whole_rows.astype(F32))
         gains, shifts = whole_rows[:4].reshape(2, 2, D), whole_rows[4:].reshape(2, 4, D)
-        whole_cols = small[1].astype(F32).reshape(4, 2, LAYERS, 12, 64)
+        whole_cols = dot(small[:, :, 6, :96].swapaxes(0, 1).reshape(8, 1536), move)
+        whole_cols = jnp.dot(col_hot, whole_cols, precision=HIGH)
+        whole_cols = whole_cols.reshape(4, 2, LAYERS, 12, 64)
         vecs, qkv_shifts, up_shifts = [], [], []
         for l in range(LAYERS):
             vecs.append(
@@ -598,19 +609,21 @@
         w_down.swapaxes(0, 1),
     )
     for n in range(COMMON):
-        recv, small = joined(exchange(bufs, n), small_step(n, *small))
+        (recv,) = joined(exchange(bufs, n))
         bufs = doubled(bufs, recv)
     first, second = ([b[..., l, :, :] for b in bufs] for l in range(LAYERS))
 
-    recv, small = joined(exchange(first, 3), small_step(3, *small))
+    (recv,) = joined(exchange(first, 3))
     first = doubled(first, recv)
-    recv, small, h, dh = joined(exchange(first, 4), small_step(4, *small), h, dh)
+    recv, h, dh = joined(exchange(first, 4), h, dh)
     first = doubled(first, recv)
-    first_hi, first_oth = joined(exchange(first, 5), over_cores_in_turn(first))
-
-    mix_oth, recv, small = joined(
-        swap(first_hi[0], "core"), exchange(second, 3), small_step(6, *small_step(5, *small))
-    )
+    first_hi, first_oth, small = joined(
+        exchange(first, 5),
+        over_cores_in_turn(first),
+        to_each(jnp.broadcast_to(small[None], (128, 8, 128))),
+    )
+
+    mix_oth, recv = joined(swap(first_hi[0], "core"), exchange(second, 3))
     second = doubled(second, recv)
     vecs, qkv_shifts, up_shifts = unpacked(small)
     mix0 = (first[0], first_hi[0], first_oth[0], mix_oth)
@@ -634,53 +647,44 @@
     up1, down1 = ((second[i], second_hi[i], second_oth[i], rest_oth[i - 1]) for i in (1, 2))
     u1, out = feed_fwd(core, slopes, hm1, vecs[1], up_shifts[1], up1, down1)
 
-    def feed_back(dh, hm, l, u, up, down):
-        outs = feed_bwd(core, slopes, dh, hm, vecs[l], u, up, down)
-        return unmerged(outs[:4]), unmerged(outs[4:8]), outs[8:]
-
-    def attn_back(dhm, h, l, qkv, ctx, mix):
-        outs = attn_bwd(core, slopes, dhm, h, vecs[l], qkv, ctx, mix)
-        return unmerged(outs[:4]), outs[4:]
-
     def sent(part, hi, n):
         return swap(hi, ORDERS[part][n // 2], n % 2 + 1)
 
-    def core_sums(grads, got):
-        return [plus(g, r) for g, r in zip(grads, got)]
-
-    gup1, gdown1, (dhm1, gbu1, gvec21) = feed_back(dh, hm1, 1, u1, up1, down1)
-    (gmix1, (dh, gqv1, gvec11)), up_got, down_got = joined(
-        attn_back(dhm1, h1, 1, qkv1, ctx1, mix1), over_cores(gup1[2:]), over_cores(gdown1[2:])
-    )
-    up1_lo, up1_hi = core_sums(gup1, up_got)
-    down1_lo, down1_hi = core_sums(gdown1, down_got)
-    up_got, down_got = sent(1, up1_hi, 5), sent(2, down1_hi, 5)
-    mix1_hi = plus(gmix1[1], swap(gmix1[3], "core"))
-    dh, mix1_hi, hm0, out = joined(dh, mix1_hi, hm0, out)
-    mix_got = sent(0, mix1_hi, 5)
-    mix1_lo = plus(gmix1[0], swap(gmix1[2], "core"))
-    (gup0, gdown0, (dhm0, gbu0, gvec20)), up_got, down_got, mix1_lo, hidden_out = joined(
-        feed_back(dh, hm0, 0, u0, up0, down0), up_got, down_got, mix1_lo, from_own(out)
-    )
-    up1_lo, up1_hi = halves(up1_lo, up_got)
-    down1_lo, down1_hi = halves(down1_lo, down_got)
-    up_got, down_got = sent(1, up1_hi, 4), sent(2, down1_hi, 4)
-    mix1_lo, mix1_hi = halves(mix1_lo, mix_got)
-    dhm0, mix1_hi = joined(dhm0, mix1_hi)
-    mix_got = sent(0, mix1_hi, 4)
-    (gmix0, (dh, gqv0, gvec10)), up_got, down_got, mix_got, up0_got, down0_got = joined(
-        attn_back(dhm0, h, 0, qkv0, ctx0, mix0),
-        up_got,
-        down_got,
-        mix_got,
-        swap(gup0[3], "core"),
-        swap(gdown0[3], "core"),
-    )
-    lay1 = [
-        halves(lo, got)
-        for lo, got in ((mix1_lo, mix_got), (up1_lo, up_got), (down1_lo, down_got))
-    ]
-    up0_hi, down0_hi = plus(gup0[1], up0_got), plus(gdown0[1], down0_got)
+    feed_grads = partial(weight_grads, feed_grad_body, "feed_grad", (1, 2), core, slopes)
+    attn_grads = partial(weight_grads, attn_grad_body, "attn_grad", (0,), core, slopes)
+
+    dhm1, gbu1, gvec21, ad1, md1, md1_oth = feed_bwd(core, slopes, dh, hm1, vecs[1], u1, up1, down1)
+    (dh, gqv1, gvec11, dc1, az1, az1_oth), ad1_got, md1_got = joined(
+        attn_bwd(core, slopes, dhm1, h1, vecs[1], qkv1, ctx1, mix1),
+        swap(ad1, "core"),
+        swap(md1_oth, "core"),
+    )
+    (gup1, gdown1), dc1_got, az1_got = joined(
+        feed_grads(ad1, ad1_got, md1, md1_got), swap(dc1, "core"), swap(az1_oth, "core")
+    )
+    up_got, down_got = sent(1, gup1[1], 5), sent(2, gdown1[1], 5)
+    (gmix1,) = attn_grads(dc1, dc1_got, az1, az1_got)
+    dh, gmix1 = joined(dh, gmix1)
+    mix_got = sent(0, gmix1[1], 5)
+    dhm0, gbu0, gvec20, ad0, md0, md0_oth = feed_bwd(core, slopes, dh, hm0, vecs[0], u0, up0, down0)
+    (dh, gqv0, gvec10, dc0, az0, az0_oth), ad0_got, md0_got, got = joined(
+        attn_bwd(core, slopes, dhm0, h, vecs[0], qkv0, ctx0, mix0),
+        swap(ad0, "core"),
+        swap(md0_oth, "core"),
+        [mix_got, up_got, down_got],
+    )
+    lay1 = [halves(g[0], r) for g, r in zip((gmix1, gup1, gdown1), got)]
+    ad0, his = joined(ad0, [v[1] for v in lay1])
+    (gup0, gdown0), dc0_got, az0_got, got = joined(
+        feed_grads(ad0, ad0_got, md0, md0_got),
+        swap(dc0, "core"),
+        swap(az0_oth, "core"),
+        [sent(i, his[i], 4) for i in range(3)],
+    )
+    up_got, down_got = sent(1, gup0[1], 5), sent(2, gdown0[1], 5)
+    (gmix0,) = attn_grads(dc0, dc0_got, az0, az0_got)
+    mix_got = sent(0, gmix0[1], 5)
+    lay1 = [halves(v[0], r) for v, r in zip(lay1, got)]
     rows = jnp.concatenate(
         [
             v
@@ -695,50 +699,41 @@
             for v in (gqv[:, :, :128], gqv[:, :, 256:], gbu)
         ],
         axis=2,
-    ).reshape(2, 2, 2, LAYERS * 768)
-    mix0_got, got1, up0_hi, down0_hi, (rows, cols) = joined(
-        swap(gmix0[3], "core"),
+    ).reshape(8, 1536)
+    rows = dot(rows.astype(BF), lane_hot.astype(BF)).astype(BF)
+    rows = rows.reshape(12, 16, 64).swapaxes(0, 1).reshape(16, 1, 768)
+    cols = dot_nt(dot_tn(col_hot.astype(BF), cols.astype(BF)).astype(BF), move).astype(BF)
+    cols = cols.reshape(8, 16, 96).swapaxes(0, 1)
+    small = jnp.concatenate([jnp.broadcast_to(rows, (16, 8, 768)), cols], axis=2)
+    small = jnp.pad(small, ((0, 0), (0, 0), (0, 160))).reshape(128, 8, 128)
+    got, got1, small, grad_in, hidden_out = joined(
+        [mix_got, up_got, down_got],
         [sent(i, lay1[i][1], 3) for i in range(3)],
-        up0_hi,
-        down0_hi,
-        sum_small_step(0, rows, cols),
-    )
-    up_got, down_got = sent(1, up0_hi, 5), sent(2, down0_hi, 5)
-    mix_got = sent(0, plus(gmix0[1], mix0_got), 5)
-    got, los, (rows, cols), grad_in, lay1 = joined(
-        [mix_got, up_got, down_got],
-        [plus(g[0], swap(g[2], "core")) for g in (gmix0, gup0, gdown0)],
-        sum_small_step(1, rows, cols),
+        to_each(small),
         from_own(dh),
+        from_own(out),
+    )
+    small = jnp.sum(small.astype(F32), axis=0).reshape(-1)
+    rows = small[:768].reshape(12, 64).T.reshape(64, LAYERS, 6)
+    cols = small[768:864].reshape(24, 4).T.reshape(4, LAYERS, 12)
+    lay0 = [halves(g[0], r) for g, r in zip((gmix0, gup0, gdown0), got)]
+    got, lay1 = joined(
+        [sent(i, lay0[i][1], 4) for i in range(3)],
         [plus(s[0], g) for s, g in zip(lay1, got1)],
     )
-    lay0 = [halves(lo, g) for lo, g in zip(los, got)]
-    got, (rows, cols) = joined(
-        [sent(i, lay0[i][1], 4) for i in range(3)], sum_small_step(2, rows, cols)
-    )
     lay0 = [halves(s[0], g) for s, g in zip(lay0, got)]
-    got, (rows, cols) = joined(
-        [sent(i, lay0[i][1], 3) for i in range(3)], sum_small_step(3, rows, cols)
-    )
+    (got,) = joined([sent(i, lay0[i][1], 3) for i in range(3)])
     both = [
         tuple(jnp.stack([plus(s[0][k], g[k]), s1[k]], axis=2) for k in (0, 1))
         for s, g, s1 in zip(lay0, got, lay1)
     ]
     for n in (2, 1):
-        got, (rows, cols) = joined(
-            [sent(i, both[i][1], n) for i in range(3)], sum_small_step(6 - n, rows, cols)
-        )
+        (got,) = joined([sent(i, both[i][1], n) for i in range(3)])
         both = [halves(s[0], g) for s, g in zip(both, got)]
-    got, (rows, cols) = joined(
-        [sent(i, both[i][1], 0) for i in range(3)], sum_small_step(6, rows, cols)
-    )
+    (got,) = joined([sent(i, both[i][1], 0) for i in range(3)])
     mixes, ups, downs = (
         jnp.swapaxes(s[0].astype(F32) + g.astype(F32), 0, 1) for s, g in zip(both, got)
     )
-    rows = rows[:, :64].T.reshape(64, LAYERS, 6)
-    cols = lax.dot_general(
-        put_col.astype(F32), cols.reshape(24, 64), (((1,), (1,)), ((), ())), precision=HIGH
-    ).reshape(4, LAYERS, 12)
     return (
         hidden_out,
         grad_in,

time: 526 us -> 496 us (0.943)
  other arithmetic: 112 us -> 63.6 us
  blocking collectives: 0 us -> 28 us
  waiting for transfers between devices: 136 us -> 119 us
  local copies, waits for them, and re-layouts: 40.4 us -> 31.7 us
  Pallas kernels: 124 us -> 132 us
    convert_element_type x39 -> x27, other arithmetic: 80.9 us -> 34.1 us  [plus(): return (a.astype(F32) + b.astype(F32)).astype(BF)]
    all_to_all x0 -> x1, blocking collectives: none -> 28 us  [to_each(): return lax.all_to_all(v, AXES, 0, 0, tiled=True)]
    ppermute x6 -> x0, waiting for transfers between devices: 18.8 us -> none  [plain_swap(): return lax.ppermute(v, AXES, plain_pairs(axis, flip))]
    pallas_call x8 -> x12, Pallas kernels: 124 us -> 132 us  [call(): pl.pallas_call(body, name=name, out_shape=outs, grid_spec=pltpu.PrefetchS...]
    all_to_all x0 -> x1, starting transfers between devices: none -> 5.82 us  [to_each(): return lax.all_to_all(v, AXES, 0, 0, tiled=True)]
    ppermute x6 -> x0, starting transfers between devices: 5.63 us -> none  [plain_swap(): return lax.ppermute(v, AXES, plain_pairs(axis, flip))]
    unnamed x168 -> x112, local copies, waits for them, and re-layouts: 21.7 us -> 17.5 us
    ppermute x86 -> x74, starting transfers between devices: 83.2 us -> 86 us  [swap(): return lax.ppermute(v, AXES, pairs(axis, step))]
  transfers between devices with their start and end apart: 92 -> 75, of which waited for: 36 -> 39; matrix products, arithmetic and copies ran while one was open for 25% -> 15% of each run, Pallas kernels for 18% -> 17%
where the time goes in v4:
time: 496 us; the launch traced here: 486 us
  Pallas kernels  132 us (27%)
  waiting for transfers between devices  119 us (24%)
  starting transfers between devices  91.8 us (19%)
  other arithmetic  63.6 us (13%)
  local copies, waits for them, and re-layouts  31.7 us (6%)
  blocking collectives  28 us (6%)
  matrix products  17.6 us (4%)
    pallas_call x12, Pallas kernels, call(): pl.pallas_call(body, name=name, out_shape=outs, grid_spec=pltpu.PrefetchS...  132 us
    ppermute x74, waiting for transfers between devices, swap(): return lax.ppermute(v, AXES, pairs(axis, step))  119 us
    ppermute x74, starting transfers between devices, swap(): return lax.ppermute(v, AXES, pairs(axis, step))  86 us
    convert_element_type x27, other arithmetic, plus(): return (a.astype(F32) + b.astype(F32)).astype(BF)  34.1 us
    all_to_all x1, blocking collectives, to_each(): return lax.all_to_all(v, AXES, 0, 0, tiled=True)  28 us
    another operation x21, other arithmetic, doubled(): jnp.stack([b, r])  26.1 us
    unnamed x112, local copies, waits for them, and re-layouts  17.5 us
  transfers between devices with their start and end apart: 75, of which 39 were waited for; matrix products, arithmetic and copies ran while one was open for 15% of the time, Pallas kernels for 17%

profile of v4, /device:TPU:0, one launch (start us, length us, event | category | flops | bytes accessed | tf_op | source)
XLA Modules:
  0.0 485.9 jit_solution(9720993230226396665)
XLA Ops:
  12.7 4.1 collective-permute-start.5
  28.6 8.5 %collective-permute-done.8 = bf16[2,2,2,64,512]{4,3,1,0,2:T(8,128)(2,1)S(1)} collective-permute-done((bf16[2,2,2,64,512]{4,3,1,0,2:T(8,128)(2,1)S(1)}, bf16[2,2,2,64,512]{4,3,1,0,2:T(8,128)(2,1)S(1)}, u32[]{:S(2)}, u32[]{:S(2)}) %collective-permute-start.8) | collective-permute-done | bytes 524320 | tf_op jit(solution)/shard_map/ppermute | solution.py:43
  45.8 3.7 collective-permute-done.11
  49.6 4.3 collective-permute-done.10
  70.4 4.0 collective-permute-done.14
  78.1 3.7 pad_maximum_fusion.1
  81.8 5.1 %collective-permute-start.15 = (bf16[2,2,2,2,2,64,512]{6,5,4,3,2,1,0:T(8,128)(2,1)S(1)}, bf16[2,2,2,2,2,64,512]{6,5,4,3,2,1,0:T(8,128)(2,1)}, u32[]{:S(2)}, u32[]{:S(2)}) collective-permute-start(bf16[2,2,2,2,2,64,512]{6,5,4,3,2,1,0:T(8,128)(2,1)S(1)} %pad_maximum_fusion), channel_id=1, source_target_pairs={{0,48},{1,49},{2,50},{3,51},{4,52},{5,53},{6,54},{7,55},{8,24},{9,... | collective-permute-start | bytes 6291464 | tf_op jit(solution)/shard_map/ppermute | solution.py:43
  93.3 28.0 %all_to_all.10 = bf16[128,8,128]{2,1,0:T(8,128)(2,1)} all-to-all(bf16[128,8,128]{2,1,0:T(8,128)(2,1)S(1)} %broadcast_in_dim.9), channel_id=1, replica_groups=mesh['ylo'=2,'z'=4,'core'=2,'x'=4,'yhi'=2] {'ylo','z','core','x','yhi'}, dimensions={0} | all-to-all | bytes 524288 | tf_op jit(solution)/shard_map/all_to_all | solution.py:69
  146.1 9.9 %attn_fwd.2 = (bf16[4,2,160,384]{3,2,1,0:T(8,128)(2,1)S(1)}, bf16[4,2,160,128]{3,2,1,0:T(8,128)(2,1)S(1)}, f32[160,1024]{1,0:T(8,128)S(1)}) custom-call(s32[1]{0:T(128)} %bitcast.core_ref, f32[16]{0:T(128)S(1)} %reshape.953.slope_ref, f32[160,1024]{1,0:T(8,128)S(1)} %fusion.19.h_ref, f32[8,1024]{1,0:T(8,128)S(1)} %concatenate.47.vec_ref, ...), custom_call_target="tpu_custom_call" | custom-call | flops 1048576 | bytes 262144 | tf_op jit(solution)/shard_map/attn_fwd/pallas_call | solution.py:214
  156.1 4.2 collective-permute-done.29
  162.4 3.7 pad_maximum_fusion.4
  176.2 10.7 %feed_fwd.2 = (f32[4,2,160,512]{3,2,1,0:T(8,128)}, f32[160,1024]{1,0:T(8,128)S(1)}) custom-call(s32[1]{0:T(128)} %bitcast.core_ref, f32[16]{0:T(128)S(1)} %reshape.953.slope_ref, f32[160,1024]{1,0:T(8,128)S(1)} %copy-done.5, f32[8,1024]{1,0:T(8,128)S(1)} %concatenate.47.vec_ref, f32[4,2,512]{2,1,0:T(2,128)S(1)} %reshape_squeeze.17.bias_ref, ...), custom_call_target="tpu_custom_call" | custom-call | flops 1048576 | bytes 262144 | tf_op jit(solution)/shard_map/feed_fwd/pallas_call | solution.py:214
  186.9 12.6 %collective-permute-done.32 = bf16[2,2,2,2,2,64,512]{6,5,4,3,2,1,0:T(8,128)(2,1)} collective-permute-done((bf16[2,2,2,2,2,64,512]{6,5,4,3,2,1,0:T(8,128)(2,1)}, bf16[2,2,2,2,2,64,512]{6,5,4,3,2,1,0:T(8,128)(2,1)}, u32[]{:S(2)}, u32[]{:S(2)}) %collective-permute-start.32) | collective-permute-done | bytes 2097184 | tf_op jit(solution)/shard_map/ppermute | solution.py:43
  199.6 4.4 collective-permute-done.36
  206.2 9.9 %attn_fwd.3 = (bf16[4,2,160,384]{3,2,1,0:T(8,128)(2,1)S(1)}, bf16[4,2,160,128]{3,2,1,0:T(8,128)(2,1)S(1)}, f32[160,1024]{1,0:T(8,128)S(1)}) custom-call(s32[1]{0:T(128)} %bitcast.core_ref, f32[16]{0:T(128)S(1)} %reshape.953.slope_ref, f32[160,1024]{1,0:T(8,128)S(1)} %get-tuple-element.235.h_ref, f32[8,1024]{1,0:T(8,128)S(1)} %concatenate.49.vec_ref, ...), custom_call_target="tpu_custom_call" | custom-call | flops 1048576 | bytes 262144 | tf_op jit(solution)/shard_map/attn_fwd/pallas_call | solution.py:214
  216.1 10.8 %feed_fwd.3 = (f32[4,2,160,512]{3,2,1,0:T(8,128)}, f32[160,1024]{1,0:T(8,128)S(1)}) custom-call(s32[1]{0:T(128)} %bitcast.core_ref, f32[16]{0:T(128)S(1)} %reshape.953.slope_ref, f32[160,1024]{1,0:T(8,128)S(1)} %get-tuple-element.244.hm_ref, f32[8,1024]{1,0:T(8,128)S(1)} %concatenate.49.vec_ref, f32[4,2,512]{2,1,0:T(2,128)S(1)} %reshape_squeeze.19.bias_ref, ...), custom_call_target="tpu_custom_call" | custom-call | flops 1048576 | bytes 262144 | tf_op jit(solution)/shard_map/feed_fwd/pallas_call | solution.py:214
  226.9 13.3 %feed_bwd.2 = (f32[160,1024]{1,0:T(8,128)S(1)}, f32[4,2,512]{2,1,0:T(2,128)S(1)}, f32[8,1024]{1,0:T(8,128)S(1)}, bf16[4,2,2,160,512]{4,3,2,1,0:T(8,128)(2,1)}, b...) custom-call(s32[1]{0:T(128)} %bitcast.core_ref, f32[16]{0:T(128)S(1)} %reshape.953.slope_ref, ...), custom_call_target="tpu_custom_call" | custom-call | flops 1048576 | bytes 262144 | tf_op jit(solution)/shard_map/feed_bwd/pallas_call | solution.py:214
  241.1 16.3 %attn_bwd.2 = (f32[160,1024]{1,0:T(8,128)S(1)}, f32[4,2,384]{2,1,0:T(2,128)S(1)}, f32[8,1024]{1,0:T(8,128)S(1)}, bf16[4,2,160,512]{3,2,1,0:T(8,128)(2,1)S(1)}, b...) custom-call(s32[1]{0:T(128)} %bitcast.core_ref, f32[16]{0:T(128)S(1)} %reshape.953.slope_ref, ...), custom_call_target="tpu_custom_call" | custom-call | flops 1048576 | bytes 262144 | tf_op jit(solution)/shard_map/attn_bwd/pallas_call | solution.py:214
  259.0 9.0 %feed_grad.2 = (bf16[2,4,4,64,512]{4,3,2,1,0:T(8,128)(2,1)S(1)}, bf16[2,4,4,64,512]{4,3,2,1,0:T(8,128)(2,1)S(1)}, bf16[2,4,4,64,512]{4,3,2,1,0:T(8,128)(2,1)}, bf16[2,4,4,64,512]{4,3,2,1,0:T(8,128)(2,1)}) custom-call(s32[1]{0:T(128)} %bitcast.core_ref, f32[16]{0:T(128)S(1)} %reshape.953.slope_ref, bf16[4,2,2,160,512]{4,3,2,1,0:T(8,128)(2,1)} %get-tuple-element.259.ad_ref, ...), custom_call_target="tpu_custom_call" | custom-call | flops 1048576 | bytes 262144 | tf_op jit(solution)/shard_map/feed_grad/pallas_call | solution.py:214
  269.3 5.6 %attn_grad.2 = (bf16[8,4,64,512]{3,2,1,0:T(8,128)(2,1)S(1)}, bf16[8,4,64,512]{3,2,1,0:T(8,128)(2,1)}) custom-call(s32[1]{0:T(128)} %bitcast.core_ref, f32[16]{0:T(128)S(1)} %reshape.953.slope_ref, bf16[4,2,160,512]{3,2,1,0:T(8,128)(2,1)S(1)} %get-tuple-element.262.dc_ref, bf16[4,2,160,512]{3,2,1,0:T(8,128)(2,1)S(1)} %collective-permute-done.41.dc2_ref, ...), custom_call_target="tpu_custom_call" | custom-call | flops 1048576 | bytes 262144 | tf_op jit(solution)/shard_map/attn_grad/pallas_call | solution.py:214
  274.9 13.3 %feed_bwd.3 = (f32[160,1024]{1,0:T(8,128)S(1)}, f32[4,2,512]{2,1,0:T(2,128)S(1)}, f32[8,1024]{1,0:T(8,128)S(1)}, bf16[4,2,2,160,512]{4,3,2,1,0:T(8,128)(2,1)}, b...) custom-call(s32[1]{0:T(128)} %bitcast.core_ref, f32[16]{0:T(128)S(1)} %reshape.953.slope_ref, ...), custom_call_target="tpu_custom_call" | custom-call | flops 1048576 | bytes 262144 | tf_op jit(solution)/shard_map/feed_bwd/pallas_call | solution.py:214
  297.3 17.1 %attn_bwd.3 = (f32[160,1024]{1,0:T(8,128)S(1)}, f32[4,2,384]{2,1,0:T(2,128)S(1)}, f32[8,1024]{1,0:T(8,128)S(1)}, bf16[4,2,160,512]{3,2,1,0:T(8,128)(2,1)}, bf16[...) custom-call(s32[1]{0:T(128)} %bitcast.core_ref, f32[16]{0:T(128)S(1)} %reshape.953.slope_ref, ...), custom_call_target="tpu_custom_call" | custom-call | flops 1048576 | bytes 262144 | tf_op jit(solution)/shard_map/attn_bwd/pallas_call | solution.py:214
  320.4 3.6 add_convert_fusion.6
  324.0 3.8 add_convert_fusion.5
  338.5 9.4 %feed_grad.3 = (bf16[2,4,4,64,512]{4,3,2,1,0:T(8,128)(2,1)S(1)}, bf16[2,4,4,64,512]{4,3,2,1,0:T(8,128)(2,1)}, bf16[2,4,4,64,512]{4,3,2,1,0:T(8,128)(2,1)}, bf16[2,4,4,64,512]{4,3,2,1,0:T(8,128)(2,1)}) custom-call(s32[1]{0:T(128)} %bitcast.core_ref, f32[16]{0:T(128)S(1)} %reshape.953.slope_ref, bf16[4,2,2,160,512]{4,3,2,1,0:T(8,128)(2,1)} %get-tuple-element.299.ad_ref, ...), custom_call_target="tpu_custom_call" | custom-call | flops 1048576 | bytes 262144 | tf_op jit(solution)/shard_map/feed_grad/pallas_call | solution.py:214
  347.9 6.8 %attn_grad.3 = (bf16[8,4,64,512]{3,2,1,0:T(8,128)(2,1)S(1)}, bf16[8,4,64,512]{3,2,1,0:T(8,128)(2,1)}) custom-call(s32[1]{0:T(128)} %bitcast.core_ref, f32[16]{0:T(128)S(1)} %reshape.953.slope_ref, bf16[4,2,160,512]{3,2,1,0:T(8,128)(2,1)} %get-tuple-element.292.dc_ref, bf16[4,2,160,512]{3,2,1,0:T(8,128)(2,1)S(1)} %collective-permute-done.48.dc2_ref, ...), custom_call_target="tpu_custom_call" | custom-call | flops 1048576 | bytes 262144 | tf_op jit(solution)/shard_map/attn_grad/pallas_call | solution.py:214
  364.4 5.8 %all-to-all-start.1 = ((bf16[128,8,128]{2,1,0:T(8,128)(2,1)}), bf16[128,8,128]{2,1,0:T(8,128)(2,1)S(1)}, u32[]{:S(2)}, u32[]{:S(2)}) async-start(bf16[128,8,128]{2,1,0:T(8,128)(2,1)} %bitcast.465), calls=%async_computation.1 | async-start | bytes 524288 | tf_op jit(solution)/shard_map/all_to_all | solution.py:69
  381.4 12.0 %collective-permute-done.58 = bf16[2,2,2,64,512]{4,3,2,1,0:T(8,128)(2,1)S(1)} collective-permute-done((bf16[2,2,2,64,512]{4,3,2,1,0:T(8,128)(2,1)S(1)}, bf16[2,2,2,64,512]{4,3,2,1,0:T(8,128)(2,1)S(1)}, u32[]{:S(2)}, u32[]{:S(2)}) %collective-permute-start.58) | collective-permute-done | bytes 524320 | tf_op jit(solution)/shard_map/ppermute | solution.py:43
  399.4 4.7 collective-permute-done.56
  434.7 3.9 collective-permute-done.64
  447.2 5.3 %collective-permute-start.65 = (bf16[2,2,2,64,512]{4,3,2,1,0:T(8,128)(2,1)S(1)}, bf16[2,2,2,64,512]{4,3,2,1,0:T(8,128)(2,1)S(1)}, u32[]{:S(2)}, u32[]{:S(2)}) collective-permute-start(bf16[2,2,2,64,512]{4,3,2,1,0:T(8,128)(2,1)S(1)} %pad_maximum_fusion.18), channel_id=1, source_target_pairs={{0,64},{1,65},{2,66},{3,67},{4,68},{5,69},{6,70},{7,71},{8,73},{9,... | collective-permute-start | bytes 1572872 | tf_op jit(solution)/shard_map/ppermute | solution.py:43
  454.1 5.0 %collective-permute-done.66 = bf16[2,2,2,64,512]{4,3,2,1,0:T(8,128)(2,1)} collective-permute-done((bf16[2,2,2,64,512]{4,3,2,1,0:T(8,128)(2,1)}, bf16[2,2,2,64,512]{4,3,2,1,0:T(8,128)(2,1)}, u32[]{:S(2)}, u32[]{:S(2)}) %collective-permute-start.66) | collective-permute-done | bytes 524320 | tf_op jit(solution)/shard_map/ppermute | solution.py:43
  (399 shorter events, 221.0 us)
Async XLA Ops:
  60.2 16.1 %collective-permute-start.12 = (bf16[2,2,2,2,64,512]{5,4,3,2,1,0:T(8,128)(2,1)}, bf16[2,2,2,2,64,512]{5,4,3,2,1,0:T(8,128)(2,1)}, u32[]{:S(2)}, u32[]{:S(2)}) collective-permute-start(bf16[2,2,2,2,64,512]{5,4,3,2,1,0:T(8,128)(2,1)} %pad_maximum_fusion.9), channel_id=1, source_target_pairs={{0,16},{1,17},{2,18},{3,19},{4,20},{5,21},{6,22},{7,23},{8,56},{9,... | collective-permute-start | bytes 3145736 | tf_op jit(solution)/shard_map/ppermute | solution.py:43
  81.8 39.6 %collective-permute-start.19 = (bf16[2,2,2,2,2,64,512]{6,5,4,3,2,1,0:T(8,128)(2,1)}, bf16[2,2,2,2,2,64,512]{6,5,4,3,2,1,0:T(8,128)(2,1)}, u32[]{:S(2)}, u32[]{:S(2)}) collective-permute-start(bf16[2,2,2,2,2,64,512]{6,5,4,3,2,1,0:T(8,128)(2,1)} %pad_maximum_fusion.1), channel_id=1, source_target_pairs={{0,8},{1,9},{2,10},{3,11},{4,12},{5,13},{6,14},{7,15},{8,0},{9,1},... | collective-permute-start | bytes 6291464 | tf_op jit(solution)/shard_map/ppermute | solution.py:43
  81.8 39.6 %collective-permute-start.16 = (bf16[2,2,2,2,2,64,512]{6,5,4,3,2,1,0:T(8,128)(2,1)}, bf16[2,2,2,2,2,64,512]{6,5,4,3,2,1,0:T(8,128)(2,1)}, u32[]{:S(2)}, u32[]{:S(2)}) collective-permute-start(bf16[2,2,2,2,2,64,512]{6,5,4,3,2,1,0:T(8,128)(2,1)} %pad_maximum_fusion.1), channel_id=1, source_target_pairs={{0,6},{1,7},{2,4},{3,5},{4,2},{5,3},{6,0},{7,1},{8,10},{9,11},{10,... | collective-permute-start | bytes 6291464 | tf_op jit(solution)/shard_map/ppermute | solution.py:43
  81.8 39.6 %collective-permute-start.15 = (bf16[2,2,2,2,2,64,512]{6,5,4,3,2,1,0:T(8,128)(2,1)S(1)}, bf16[2,2,2,2,2,64,512]{6,5,4,3,2,1,0:T(8,128)(2,1)}, u32[]{:S(2)}, u32[]{:S(2)}) collective-permute-start(bf16[2,2,2,2,2,64,512]{6,5,4,3,2,1,0:T(8,128)(2,1)S(1)} %pad_maximum_fusion), channel_id=1, source_target_pairs={{0,48},{1,49},{2,50},{3,51},{4,52},{5,53},{6,54},{7,55},{8,24},{9,... | collective-permute-start | bytes 6291464 | tf_op jit(solution)/shard_map/ppermute | solution.py:43
  89.7 31.7 %collective-permute-start.17 = (bf16[2,2,2,2,2,64,512]{6,5,4,3,2,1,0:T(8,128)(2,1)}, bf16[2,2,2,2,2,64,512]{6,5,4,3,2,1,0:T(8,128)(2,1)}, u32[]{:S(2)}, u32[]{:S(2)}) collective-permute-start(bf16[2,2,2,2,2,64,512]{6,5,4,3,2,1,0:T(8,128)(2,1)} %pad_maximum_fusion.2), channel_id=1, source_target_pairs={{0,65},{1,64},{2,67},{3,66},{4,69},{5,68},{6,71},{7,70},{8,72},{9,... | collective-permute-start | bytes 6291464 | tf_op jit(solution)/shard_map/ppermute | solution.py:43
  92.7 28.7 %collective-permute-start.20 = (bf16[2,2,2,2,2,64,512]{6,5,4,3,2,1,0:T(8,128)(2,1)}, bf16[2,2,2,2,2,64,512]{6,5,4,3,2,1,0:T(8,128)(2,1)}, u32[]{:S(2)}, u32[]{:S(2)}) collective-permute-start(bf16[2,2,2,2,2,64,512]{6,5,4,3,2,1,0:T(8,128)(2,1)} %pad_maximum_fusion.2), channel_id=1, source_target_pairs={{0,8},{1,9},{2,10},{3,11},{4,12},{5,13},{6,14},{7,15},{8,0},{9,1},... | collective-permute-start | bytes 6291464 | tf_op jit(solution)/shard_map/ppermute | solution.py:43
  121.4 17.3 %collective-permute-start.21 = (bf16[2,2,2,2,2,64,512]{6,5,4,3,2,1,0:T(8,128)(2,1)}, bf16[2,2,2,2,2,64,512]{6,5,4,3,2,1,0:T(8,128)(2,1)}, u32[]{:S(2)}, u32[]{:S(2)}) collective-permute-start(bf16[2,2,2,2,2,64,512]{6,5,4,3,2,1,0:T(8,128)(2,1)} %collective-permute-done.15), channel_id=1, source_target_pairs={{0,8},{1,9},{2,10},{3,11},{4,12},{5,13},{6,14},{7,15},{8,0},{9,1},... | collective-permute-start | bytes 6291464 | tf_op jit(solution)/shard_map/ppermute | solution.py:43
  130.9 25.2 %collective-permute-start.25 = (bf16[2,2,2,2,2,64,512]{6,5,4,3,2,1,0:T(8,128)(2,1)}, bf16[2,2,2,2,2,64,512]{6,5,4,3,2,1,0:T(8,128)(2,1)}, u32[]{:S(2)}, u32[]{:S(2)}) collective-permute-start(bf16[2,2,2,2,2,64,512]{6,5,4,3,2,1,0:T(8,128)(2,1)} %collective-permute-done.16), channel_id=1, source_target_pairs={{0,8},{1,9},{2,10},{3,11},{4,12},{5,13},{6,14},{7,15},{8,0},{9,1},... | collective-permute-start | bytes 6291464 | tf_op jit(solution)/shard_map/ppermute | solution.py:43
  133.7 22.4 %collective-permute-start.26 = (bf16[2,2,2,2,2,64,512]{6,5,4,3,2,1,0:T(8,128)(2,1)}, bf16[2,2,2,2,2,64,512]{6,5,4,3,2,1,0:T(8,128)(2,1)}, u32[]{:S(2)}, u32[]{:S(2)}) collective-permute-start(bf16[2,2,2,2,2,64,512]{6,5,4,3,2,1,0:T(8,128)(2,1)} %collective-permute-done.17), channel_id=1, source_target_pairs={{0,8},{1,9},{2,10},{3,11},{4,12},{5,13},{6,14},{7,15},{8,0},{9,1},... | collective-permute-start | bytes 6291464 | tf_op jit(solution)/shard_map/ppermute | solution.py:43
  166.1 33.4 %collective-permute-start.34 = (bf16[2,2,2,2,2,64,512]{6,5,4,3,2,1,0:T(8,128)(2,1)}, bf16[2,2,2,2,2,64,512]{6,5,4,3,2,1,0:T(8,128)(2,1)}, u32[]{:S(2)}, u32[]{:S(2)}) collective-permute-start(bf16[2,2,2,2,2,64,512]{6,5,4,3,2,1,0:T(8,128)(2,1)} %pad_maximum_fusion.4), channel_id=1, source_target_pairs={{0,8},{1,9},{2,10},{3,11},{4,12},{5,13},{6,14},{7,15},{8,0},{9,1},... | collective-permute-start | bytes 6291464 | tf_op jit(solution)/shard_map/ppermute | solution.py:43
  166.1 33.4 %collective-permute-start.31 = (bf16[2,2,2,2,2,64,512]{6,5,4,3,2,1,0:T(8,128)(2,1)}, bf16[2,2,2,2,2,64,512]{6,5,4,3,2,1,0:T(8,128)(2,1)}, u32[]{:S(2)}, u32[]{:S(2)}) collective-permute-start(bf16[2,2,2,2,2,64,512]{6,5,4,3,2,1,0:T(8,128)(2,1)} %pad_maximum_fusion.4), channel_id=1, source_target_pairs={{0,6},{1,7},{2,4},{3,5},{4,2},{5,3},{6,0},{7,1},{8,10},{9,11},{10,... | collective-permute-start | bytes 6291464 | tf_op jit(solution)/shard_map/ppermute | solution.py:43
  167.1 32.4 %collective-permute-start.30 = (bf16[2,2,2,2,2,64,512]{6,5,4,3,2,1,0:T(8,128)(2,1)S(1)}, bf16[2,2,2,2,2,64,512]{6,5,4,3,2,1,0:T(8,128)(2,1)}, u32[]{:S(2)}, u32[]{:S(2)}) collective-permute-start(bf16[2,2,2,2,2,64,512]{6,5,4,3,2,1,0:T(8,128)(2,1)S(1)} %pad_maximum_fusion.3), channel_id=1, source_target_pairs={{0,48},{1,49},{2,50},{3,51},{4,52},{5,53},{6,54},{7,55},{8,24},{9,... | collective-permute-start | bytes 6291464 | tf_op jit(solution)/shard_map/ppermute | solution.py:43
  172.0 27.6 %collective-permute-start.32 = (bf16[2,2,2,2,2,64,512]{6,5,4,3,2,1,0:T(8,128)(2,1)}, bf16[2,2,2,2,2,64,512]{6,5,4,3,2,1,0:T(8,128)(2,1)}, u32[]{:S(2)}, u32[]{:S(2)}) collective-permute-start(bf16[2,2,2,2,2,64,512]{6,5,4,3,2,1,0:T(8,128)(2,1)} %pad_maximum_fusion.5), channel_id=1, source_target_pairs={{0,65},{1,64},{2,67},{3,66},{4,69},{5,68},{6,71},{7,70},{8,72},{9,... | collective-permute-start | bytes 6291464 | tf_op jit(solution)/shard_map/ppermute | solution.py:43
  173.7 25.9 %collective-permute-start.35 = (bf16[2,2,2,2,2,64,512]{6,5,4,3,2,1,0:T(8,128)(2,1)}, bf16[2,2,2,2,2,64,512]{6,5,4,3,2,1,0:T(8,128)(2,1)}, u32[]{:S(2)}, u32[]{:S(2)}) collective-permute-start(bf16[2,2,2,2,2,64,512]{6,5,4,3,2,1,0:T(8,128)(2,1)} %pad_maximum_fusion.5), channel_id=1, source_target_pairs={{0,8},{1,9},{2,10},{3,11},{4,12},{5,13},{6,14},{7,15},{8,0},{9,1},... | collective-permute-start | bytes 6291464 | tf_op jit(solution)/shard_map/ppermute | solution.py:43
  240.2 17.2 %collective-permute-start.39 = (bf16[4,2,2,160,512]{4,3,2,1,0:T(8,128)(2,1)}, bf16[4,2,2,160,512]{4,3,2,1,0:T(8,128)(2,1)S(1)}, u32[]{:S(2)}, u32[]{:S(2)}) collective-permute-start(bf16[4,2,2,160,512]{4,3,2,1,0:T(8,128)(2,1)} %get-tuple-element.259.ad_ref), channel_id=1, source_target_pairs={{0,8},{1,9},{2,10},{3,11},{4,12},{5,13},{6,14},{7,15},{8,0},{9,1},... | collective-permute-start | bytes 7864328 | tf_op jit(solution)/shard_map/ppermute | solution.py:43
  240.3 17.1 %collective-permute-start.40 = (bf16[2,160,512]{2,1,0:T(8,128)(2,1)S(1)}, bf16[2,160,512]{2,1,0:T(8,128)(2,1)S(1)}, u32[]{:S(2)}, u32[]{:S(2)}) collective-permute-start(bf16[2,160,512]{2,1,0:T(8,128)(2,1)S(1)} %get-tuple-element.260), channel_id=1, source_target_pairs={{0,8},{1,9},{2,10},{3,11},{4,12},{5,13},{6,14},{7,15},{8,0},{9,1},... | collective-permute-start | bytes 983048 | tf_op jit(solution)/shard_map/ppermute | solution.py:43
  289.0 31.4 %collective-permute-start.43 = (bf16[4,2,2,160,512]{4,3,2,1,0:T(8,128)(2,1)}, bf16[4,2,2,160,512]{4,3,2,1,0:T(8,128)(2,1)}, u32[]{:S(2)}, u32[]{:S(2)}) collective-permute-start(bf16[4,2,2,160,512]{4,3,2,1,0:T(8,128)(2,1)} %get-tuple-element.299.ad_ref), channel_id=1, source_target_pairs={{0,8},{1,9},{2,10},{3,11},{4,12},{5,13},{6,14},{7,15},{8,0},{9,1},... | collective-permute-start | bytes 7864328 | tf_op jit(solution)/shard_map/ppermute | solution.py:43
  289.1 27.6 %collective-permute-start.45 = (bf16[2,2,2,2,2,64,512]{6,5,4,3,2,1,0:T(8,128)(2,1)}, bf16[2,2,2,2,2,64,512]{6,5,4,3,2,1,0:T(8,128)(2,1)}, u32[]{:S(2)}, u32[]{:S(2)}) collective-permute-start(bf16[2,2,2,2,2,64,512]{6,5,4,3,2,1,0:T(8,128)(2,1)} %bitcast.503), channel_id=1, source_target_pairs={{0,48},{1,49},{2,50},{3,51},{4,52},{5,53},{6,54},{7,55},{8,24},{9,... | collective-permute-start | bytes 6291464 | tf_op jit(solution)/shard_map/ppermute | solution.py:43
  290.6 27.4 %collective-permute-start.46 = (bf16[2,2,2,2,2,64,512]{6,5,4,3,2,1,0:T(8,128)(2,1)S(1)}, bf16[2,2,2,2,2,64,512]{6,5,4,3,2,1,0:T(8,128)(2,1)}, u32[]{:S(2)}, u32[]{:S(2)}) collective-permute-start(bf16[2,2,2,2,2,64,512]{6,5,4,3,2,1,0:T(8,128)(2,1)S(1)} %bitcast.450), channel_id=1, source_target_pairs={{0,6},{1,7},{2,4},{3,5},{4,2},{5,3},{6,0},{7,1},{8,10},{9,11},{10,... | collective-permute-start | bytes 6291464 | tf_op jit(solution)/shard_map/ppermute | solution.py:43
  292.8 27.6 %collective-permute-start.47 = (bf16[2,2,2,2,2,64,512]{6,5,4,3,2,1,0:T(8,128)(2,1)}, bf16[2,2,2,2,2,64,512]{6,5,4,3,2,1,0:T(8,128)(2,1)}, u32[]{:S(2)}, u32[]{:S(2)}) collective-permute-start(bf16[2,2,2,2,2,64,512]{6,5,4,3,2,1,0:T(8,128)(2,1)} %bitcast.502), channel_id=1, source_target_pairs={{0,65},{1,64},{2,67},{3,66},{4,69},{5,68},{6,71},{7,70},{8,72},{9,... | collective-permute-start | bytes 6291464 | tf_op jit(solution)/shard_map/ppermute | solution.py:43
  297.0 17.4 %collective-permute-start.44 = (bf16[2,160,512]{2,1,0:T(8,128)(2,1)S(1)}, bf16[2,160,512]{2,1,0:T(8,128)(2,1)S(1)}, u32[]{:S(2)}, u32[]{:S(2)}) collective-permute-start(bf16[2,160,512]{2,1,0:T(8,128)(2,1)S(1)} %get-tuple-element.288), channel_id=1, source_target_pairs={{0,8},{1,9},{2,10},{3,11},{4,12},{5,13},{6,14},{7,15},{8,0},{9,1},... | collective-permute-start | bytes 983048 | tf_op jit(solution)/shard_map/ppermute | solution.py:43
  331.4 16.4 %collective-permute-start.49 = (bf16[2,160,512]{2,1,0:T(8,128)(2,1)}, bf16[2,160,512]{2,1,0:T(8,128)(2,1)}, u32[]{:S(2)}, u32[]{:S(2)}) collective-permute-start(bf16[2,160,512]{2,1,0:T(8,128)(2,1)} %get-tuple-element.307), channel_id=1, source_target_pairs={{0,8},{1,9},{2,10},{3,11},{4,12},{5,13},{6,14},{7,15},{8,0},{9,1},... | collective-permute-start | bytes 983048 | tf_op jit(solution)/shard_map/ppermute | solution.py:43
  331.5 16.3 %collective-permute-start.50 = (bf16[2,2,2,2,64,512]{5,4,3,2,1,0:T(8,128)(2,1)}, bf16[2,2,2,2,64,512]{5,4,3,2,1,0:T(8,128)(2,1)}, u32[]{:S(2)}, u32[]{:S(2)}) collective-permute-start(bf16[2,2,2,2,64,512]{5,4,3,2,1,0:T(8,128)(2,1)} %get-tuple-element.308), channel_id=1, source_target_pairs={{0,16},{1,17},{2,18},{3,19},{4,20},{5,21},{6,22},{7,23},{8,56},{9,... | collective-permute-start | bytes 3145736 | tf_op jit(solution)/shard_map/ppermute | solution.py:43
  331.6 16.3 %collective-permute-start.51 = (bf16[2,2,2,2,64,512]{5,4,3,2,1,0:T(8,128)(2,1)}, bf16[2,2,2,2,64,512]{5,4,3,2,1,0:T(8,128)(2,1)}, u32[]{:S(2)}, u32[]{:S(2)}) collective-permute-start(bf16[2,2,2,2,64,512]{5,4,3,2,1,0:T(8,128)(2,1)} %get-tuple-element.309), channel_id=1, source_target_pairs={{0,2},{1,3},{2,0},{3,1},{4,6},{5,7},{6,4},{7,5},{8,14},{9,15},{10,... | collective-permute-start | bytes 3145736 | tf_op jit(solution)/shard_map/ppermute | solution.py:43
  332.3 15.6 %collective-permute-start.52 = (bf16[2,2,2,2,64,512]{5,4,3,2,1,0:T(8,128)(2,1)}, bf16[2,2,2,2,64,512]{5,4,3,2,1,0:T(8,128)(2,1)}, u32[]{:S(2)}, u32[]{:S(2)}) collective-permute-start(bf16[2,2,2,2,64,512]{5,4,3,2,1,0:T(8,128)(2,1)} %get-tuple-element.310), channel_id=1, source_target_pairs={{0,64},{1,65},{2,66},{3,67},{4,68},{5,69},{6,70},{7,71},{8,73},{9,... | collective-permute-start | bytes 3145736 | tf_op jit(solution)/shard_map/ppermute | solution.py:43
  332.3 15.6 %collective-permute-start.48 = (bf16[4,2,160,512]{3,2,1,0:T(8,128)(2,1)}, bf16[4,2,160,512]{3,2,1,0:T(8,128)(2,1)S(1)}, u32[]{:S(2)}, u32[]{:S(2)}) collective-permute-start(bf16[4,2,160,512]{3,2,1,0:T(8,128)(2,1)} %get-tuple-element.292.dc_ref), channel_id=1, source_target_pairs={{0,8},{1,9},{2,10},{3,11},{4,12},{5,13},{6,14},{7,15},{8,0},{9,1},... | collective-permute-start | bytes 3932168 | tf_op jit(solution)/shard_map/ppermute | solution.py:43
  356.1 48.1 %collective-permute-start.53 = (bf16[2,2,2,2,2,64,512]{6,5,4,3,2,1,0:T(8,128)(2,1)}, bf16[2,2,2,2,2,64,512]{6,5,4,3,2,1,0:T(8,128)(2,1)}, u32[]{:S(2)}, u32[]{:S(2)}) collective-permute-start(bf16[2,2,2,2,2,64,512]{6,5,4,3,2,1,0:T(8,128)(2,1)} %bitcast.504), channel_id=1, source_target_pairs={{0,48},{1,49},{2,50},{3,51},{4,52},{5,53},{6,54},{7,55},{8,24},{9,... | collective-permute-start | bytes 6291464 | tf_op jit(solution)/shard_map/ppermute | solution.py:43
  357.5 46.6 %collective-permute-start.54 = (bf16[2,2,2,2,2,64,512]{6,5,4,3,2,1,0:T(8,128)(2,1)}, bf16[2,2,2,2,2,64,512]{6,5,4,3,2,1,0:T(8,128)(2,1)}, u32[]{:S(2)}, u32[]{:S(2)}) collective-permute-start(bf16[2,2,2,2,2,64,512]{6,5,4,3,2,1,0:T(8,128)(2,1)} %bitcast.140), channel_id=1, source_target_pairs={{0,6},{1,7},{2,4},{3,5},{4,2},{5,3},{6,0},{7,1},{8,10},{9,11},{10,... | collective-permute-start | bytes 6291464 | tf_op jit(solution)/shard_map/ppermute | solution.py:43
  359.6 44.5 %collective-permute-start.55 = (bf16[2,2,2,2,2,64,512]{6,5,4,3,2,1,0:T(8,128)(2,1)}, bf16[2,2,2,2,2,64,512]{6,5,4,3,2,1,0:T(8,128)(2,1)}, u32[]{:S(2)}, u32[]{:S(2)}) collective-permute-start(bf16[2,2,2,2,2,64,512]{6,5,4,3,2,1,0:T(8,128)(2,1)} %bitcast.142), channel_id=1, source_target_pairs={{0,65},{1,64},{2,67},{3,66},{4,69},{5,68},{6,71},{7,70},{8,72},{9,... | collective-permute-start | bytes 6291464 | tf_op jit(solution)/shard_map/ppermute | solution.py:43
  364.4 35.0 %all-to-all-start.1 = ((bf16[128,8,128]{2,1,0:T(8,128)(2,1)}), bf16[128,8,128]{2,1,0:T(8,128)(2,1)S(1)}, u32[]{:S(2)}, u32[]{:S(2)}) async-start(bf16[128,8,128]{2,1,0:T(8,128)(2,1)} %bitcast.465), calls=%async_computation.1 | async-start | bytes 524288 | tf_op jit(solution)/shard_map/all_to_all | solution.py:69
  371.6 21.8 %collective-permute-start.58 = (bf16[2,2,2,64,512]{4,3,2,1,0:T(8,128)(2,1)S(1)}, bf16[2,2,2,64,512]{4,3,2,1,0:T(8,128)(2,1)S(1)}, u32[]{:S(2)}, u32[]{:S(2)}) collective-permute-start(bf16[2,2,2,64,512]{4,3,2,1,0:T(8,128)(2,1)S(1)} %fusion.43), channel_id=1, source_target_pairs={{0,6},{1,7},{2,4},{3,5},{4,2},{5,3},{6,0},{7,1},{8,10},{9,11},{10,... | collective-permute-start | bytes 1572872 | tf_op jit(solution)/shard_map/ppermute | solution.py:43
  376.0 23.4 %collective-permute-start.57 = (bf16[2,2,2,64,512]{4,3,2,1,0:T(8,128)(2,1)}, bf16[2,2,2,64,512]{4,3,2,1,0:T(8,128)(2,1)}, u32[]{:S(2)}, u32[]{:S(2)}) collective-permute-start(bf16[2,2,2,64,512]{4,3,2,1,0:T(8,128)(2,1)} %fusion.42), channel_id=1, source_target_pairs={{0,48},{1,49},{2,50},{3,51},{4,52},{5,53},{6,54},{7,55},{8,24},{9,... | collective-permute-start | bytes 1572872 | tf_op jit(solution)/shard_map/ppermute | solution.py:43
  (93 other events, 1026.0 us)
